TPU v7x, 32 devices: a whole 2x2x4 slice. The times are simulated.
32 devices in a mesh: dp: 8 (over z, y), mp: 4 (over x, core).
Axes of the slice: x: 2, y: 2, z: 4, core: 2. Of those that a mesh axis runs over, the one named last changes fastest.
Arguments:
- inputs: float32 [7168, 2304], P(('dp', 'mp')), may hold values from -16 to 16
- out_grad: float32 [7168, 2304], P(('dp', 'mp')), may hold values from -6 to 6
- segment_ids: int32 [8, 896], P('dp'), may hold values from 0 to 13, never falling along the last dimension, each value on 1 to 448 neighbouring positions
- pad_mask: int32 [8, 896], P('dp'), may hold values 0 or 1
- bit_sel: int32 [3], replicated, may hold values from 0 to 2
- w_qo: float32 [2, 2304, 2048], P(None, 'dp', 'mp'), may hold values from -1 to 1
- w_kv: float32 [2, 2304, 1024], P(None, 'dp', 'mp'), may hold values from -1 to 1
- w_mlp: float32 [3, 2304, 9216], P(None, 'dp', 'mp'), may hold values from -1 to 1
- norm_gains: float32 [9216], P(('dp', 'mp')), may hold values from -0.32 to 0.32
- m_qo: float32 [2, 2304, 2048], P(None, 'dp', 'mp'), may hold values from -0.3125 to 0.3125
- m_kv: float32 [2, 2304, 1024], P(None, 'dp', 'mp'), may hold values from -0.3125 to 0.3125
- m_mlp: float32 [3, 2304, 9216], P(None, 'dp', 'mp'), may hold values from -0.3125 to 0.3125
- m_gains: float32 [9216], P(('dp', 'mp')), may hold values from -0.3125 to 0.3125
- v_qo: float32 [2, 2304, 2048], P(None, 'dp', 'mp'), may hold values from 0.0066 to 0.105
- v_kv: float32 [2, 2304, 1024], P(None, 'dp', 'mp'), may hold values from 0.0066 to 0.105
- v_mlp: float32 [3, 2304, 9216], P(None, 'dp', 'mp'), may hold values from 0.0066 to 0.105
- v_gains: float32 [9216], P(('dp', 'mp')), may hold values from 0.0066 to 0.105
Outputs:
- outputs: float32 [7168, 2304], P(('dp', 'mp'))
- grad_in: float32 [7168, 2304], P(('dp', 'mp'))
- grad_norm: float32 [1], replicated
- new_w_qo: float32 [2, 2304, 2048], P(None, 'dp', 'mp')
- new_w_kv: float32 [2, 2304, 1024], P(None, 'dp', 'mp')
- new_w_mlp: float32 [3, 2304, 9216], P(None, 'dp', 'mp')
- new_gains: float32 [9216], P(('dp', 'mp'))
- new_m_qo: float32 [2, 2304, 2048], P(None, 'dp', 'mp')
- new_m_kv: float32 [2, 2304, 1024], P(None, 'dp', 'mp')
- new_m_mlp: float32 [3, 2304, 9216], P(None, 'dp', 'mp')
- new_m_gains: float32 [9216], P(('dp', 'mp'))
- new_v_qo: float32 [2, 2304, 2048], P(None, 'dp', 'mp')
- new_v_kv: float32 [2, 2304, 1024], P(None, 'dp', 'mp')
- new_v_mlp: float32 [3, 2304, 9216], P(None, 'dp', 'mp')
- new_v_gains: float32 [9216], P(('dp', 'mp'))
Inputs may be any that keep to these rules, and one draw needn't show every extreme that they name: `segment_ids`: ids never fall along a sequence; a document holds 1 to 448 slots, one exactly that many in each sequence.
All inputs are finite; a program needn't handle non-finite values. No bound on the sum of `pad_mask` on one device may be relied on, other than what follows from the above.
Results may differ from a plain program's by a relative error of at most 0.02.
Values may be sent and summed in bfloat16 or wider, within the bound.
A program may use at most 320 MiB of HBM per device.

v0:
```python
import math

import jax
import jax.numpy as jnp
from jax import lax
from jax.sharding import PartitionSpec as P

D = 2304
HEAD_WIDTH = 256
FF = 9216
NORMS = 4
QW = 2048
PARAMS = 77865984


EPSILON = 1e-06
SOFT_CAP = 50.0
ROPE_BASE = 10000.0
MASKED_SCORE = -1e30
FIRST_DECAY = 0.9
SECOND_DECAY = 0.95
LEARN_RATE = 0.04
WEIGHT_DECAY = 0.1
ADAM_EPSILON = 1e-08
CLIP_SCALE = 0.5


def quantize(master, fan_list, selector):
    shifts = jnp.where(selector == 0, 0, jnp.where(selector == 1, 4, 6)).astype(jnp.int32)
    spacing = jnp.left_shift(jnp.int32(1), shifts)
    step_sizes = jnp.array(
        [1.0 / (32.0 * math.sqrt(fan_in)) for fan_in in fan_list], jnp.float32
    ).reshape(-1, 1, 1)
    codes = jnp.clip(jnp.floor(master / step_sizes + 0.5), -128.0, 127.0).astype(jnp.int32)
    sliced = jnp.floor_divide(codes + spacing // 2, spacing)
    sliced = jnp.clip(sliced, -(128 // spacing), 128 // spacing - 1)
    return ((sliced * spacing).astype(jnp.float32) * step_sizes).astype(jnp.bfloat16)


def rms_norm(values, norm_gain):
    return (
        values
        * lax.rsqrt(jnp.mean(values * values, axis=-1, keepdims=True) + EPSILON)
        * (1.0 + norm_gain)
    )


def doc_positions(segments):
    slot_index = jnp.arange(segments.shape[0], dtype=jnp.int32)
    previous = jnp.concatenate([segments[:1] - 1, segments[:-1]])
    starts = segments != previous
    doc_begin = lax.cummax(jnp.where(starts, slot_index, 0), axis=0)
    return slot_index - doc_begin


def allowed_pairs(segments, padding):
    slot_index = jnp.arange(segments.shape[0], dtype=jnp.int32)
    same_doc = segments[:, None] == segments[None, :]
    causal = slot_index[None, :] <= slot_index[:, None]
    live_key = (padding[None, :] == 1) | (slot_index[None, :] == slot_index[:, None])
    return same_doc & causal & live_key


def apply_rotation(values, token_positions):
    half_dim = HEAD_WIDTH // 2
    frequency = ROPE_BASE ** (-jnp.arange(half_dim, dtype=jnp.float32) * 2.0 / HEAD_WIDTH)
    angles = token_positions.astype(jnp.float32)[:, None] * frequency[None, :]
    angles = jnp.concatenate([angles, angles], -1)
    cosine = jnp.cos(angles)[:, None, :]
    sine = jnp.sin(angles)[:, None, :]
    first_half = values[..., :half_dim]
    second = values[..., half_dim:]
    turned = jnp.concatenate([-second, first_half], -1)
    return values * cosine + turned * sine


def contract_rows(left, right):
    return lax.dot_general(
        left, right, (((0,), (0,)), ((), ())), preferred_element_type=jnp.float32
    )


def contract_cols(left, right):
    return lax.dot_general(
        left, right, (((1,), (1,)), ((), ())), preferred_element_type=jnp.float32
    )


def adam_update(master, first_moment, second_moment, gradient, factor):
    clipped = gradient * factor
    new_first = FIRST_DECAY * first_moment + (1.0 - FIRST_DECAY) * clipped
    new_second = SECOND_DECAY * second_moment + (1.0 - SECOND_DECAY) * clipped * clipped
    new_master = master - LEARN_RATE * (
        new_first / (jnp.sqrt(new_second) + ADAM_EPSILON) + WEIGHT_DECAY * master
    )
    return (new_master, new_first, new_second)


def local(
    inputs,
    out_grad,
    segment_ids,
    pad_mask,
    bit_sel,
    w_qo,
    w_kv,
    w_mlp,
    norm_gains,
    m_qo,
    m_kv,
    m_mlp,
    m_gains,
    v_qo,
    v_kv,
    v_mlp,
    v_gains,
):
    row_count = inputs.shape[0]
    seq_len = segment_ids.shape[1]
    low_qo = quantize(w_qo, (D, QW), bit_sel[0])
    low_kv = quantize(w_kv, (D, D), bit_sel[1])
    low_mlp = quantize(w_mlp, (D, D, FF), bit_sel[2])
    full_qo, full_kv, full_mlp = (
        lax.all_gather(low_qo, "dp", axis=1, tiled=True),
        lax.all_gather(low_kv, "dp", axis=1, tiled=True),
        lax.all_gather(low_mlp, "dp", axis=1, tiled=True),
    )
    gain_rows = lax.all_gather(norm_gains, ("dp", "mp"), axis=0, tiled=True).reshape(NORMS, D)
    segments = segment_ids[0]
    padding = pad_mask[0]
    token_positions = doc_positions(segments)
    allowed = allowed_pairs(segments, padding)
    local_heads = full_qo.shape[2] // HEAD_WIDTH
    kv_heads = full_kv.shape[2] // HEAD_WIDTH
    group_size = local_heads // kv_heads
    scale = HEAD_WIDTH ** (-0.5)
    normalized_rows = rms_norm(inputs, gain_rows[0]).astype(jnp.bfloat16)
    seq_normed = lax.all_gather(normalized_rows, "mp", axis=0, tiled=True)
    query_linear = jnp.dot(seq_normed, full_qo[0], preferred_element_type=jnp.float32)
    key_linear = jnp.dot(seq_normed, full_kv[0], preferred_element_type=jnp.float32)
    value_lin = jnp.dot(seq_normed, full_kv[1], preferred_element_type=jnp.float32)

    def rope_query(values):
        turned = apply_rotation(values.reshape(seq_len, local_heads, HEAD_WIDTH), token_positions)
        return turned.reshape(seq_len, kv_heads, group_size, HEAD_WIDTH)

    def rope_key(values):
        return apply_rotation(values.reshape(seq_len, kv_heads, HEAD_WIDTH), token_positions)

    query_bf = rope_query(query_linear).astype(jnp.bfloat16)
    key_bf = rope_key(key_linear).astype(jnp.bfloat16)
    value_bf = value_lin.astype(jnp.bfloat16).reshape(seq_len, kv_heads, HEAD_WIDTH)

    def masked_scores():
        raw_scores = (
            jnp.einsum("qkgd,pkd->kgqp", query_bf, key_bf, preferred_element_type=jnp.float32)
            * scale
        )
        capped = jnp.where(
            allowed[None, None], SOFT_CAP * jnp.tanh(raw_scores / SOFT_CAP), MASKED_SCORE
        )
        return (raw_scores, capped)

    raw_scores, capped = masked_scores()
    row_top = jnp.max(capped, axis=-1, keepdims=True)
    log_total = row_top + jnp.log(jnp.sum(jnp.exp(capped - row_top), axis=-1, keepdims=True))
    probs_bf = jnp.exp(capped - log_total).astype(jnp.bfloat16)
    mixed_bf = (
        jnp.einsum("kgqp,pkd->qkgd", probs_bf, value_bf, preferred_element_type=jnp.float32)
        .reshape(seq_len, -1)
        .astype(jnp.bfloat16)
    )
    row_block = mixed_bf
    attended = lax.psum_scatter(
        contract_cols(row_block, full_qo[1]), "mp", scatter_dimension=0, tiled=True
    )
    hidden_in = inputs + rms_norm(attended, gain_rows[1])
    ffn_normed = rms_norm(hidden_in, gain_rows[2]).astype(jnp.bfloat16)
    seq_ffn = lax.all_gather(ffn_normed, "mp", axis=0, tiled=True)
    gate_up = jnp.einsum("td,kdf->ktf", seq_ffn, full_mlp[:2], preferred_element_type=jnp.float32)
    activated_bf = (jax.nn.gelu(gate_up[0], approximate=True) * gate_up[1]).astype(jnp.bfloat16)
    row_block = activated_bf
    branch = lax.psum_scatter(
        contract_cols(row_block, full_mlp[2]), "mp", scatter_dimension=0, tiled=True
    )
    outputs = hidden_in + rms_norm(branch, gain_rows[3])
    row_live = lax.dynamic_slice_in_dim(
        padding, lax.axis_index("mp") * row_count, row_count
    ).astype(jnp.float32)
    cotangent = out_grad * row_live[:, None]
    _, branch_pull = jax.vjp(rms_norm, branch, gain_rows[3])
    grad_branch, grad_gain_three = branch_pull(cotangent)
    seq_grad_branch = lax.all_gather(grad_branch.astype(jnp.bfloat16), "mp", axis=0, tiled=True)
    back_qo, back_kv, back_mlp = (
        lax.all_gather(low_qo, "dp", axis=1, tiled=True),
        lax.all_gather(low_kv, "dp", axis=1, tiled=True),
        lax.all_gather(low_mlp, "dp", axis=1, tiled=True),
    )
    grad_act = jnp.dot(seq_grad_branch, back_mlp[2], preferred_element_type=jnp.float32)
    grad_down = contract_rows(seq_grad_branch, activated_bf)
    _, act_pull = jax.vjp(
        lambda gate_in, up_in: jax.nn.gelu(gate_in, approximate=True) * up_in,
        gate_up[0],
        gate_up[1],
    )
    grad_gate, grad_up = act_pull(grad_act)
    grad_gate_up = jnp.stack([grad_gate, grad_up]).astype(jnp.bfloat16)
    grad_gate_up_w = jnp.einsum(
        "ktf,td->kdf", grad_gate_up, seq_ffn, preferred_element_type=jnp.float32
    )
    row_block = grad_gate_up
    grad_ffn_normed = lax.psum_scatter(
        jnp.einsum("ktf,kdf->td", row_block, back_mlp[:2], preferred_element_type=jnp.float32),
        "mp",
        scatter_dimension=0,
        tiled=True,
    )
    _, ffn_pull = jax.vjp(rms_norm, hidden_in, gain_rows[2])
    grad_hidden_part, grad_gain_two = ffn_pull(grad_ffn_normed)
    grad_hidden = cotangent + grad_hidden_part
    _, attn_pull = jax.vjp(rms_norm, attended, gain_rows[1])
    grad_attended, grad_gain_one = attn_pull(grad_hidden)
    seq_grad_attended = lax.all_gather(grad_attended.astype(jnp.bfloat16), "mp", axis=0, tiled=True)
    grad_mixed = jnp.dot(seq_grad_attended, back_qo[1], preferred_element_type=jnp.float32)
    grad_mixed = grad_mixed.astype(jnp.bfloat16).reshape(seq_len, kv_heads, group_size, HEAD_WIDTH)
    grad_out_w = contract_rows(seq_grad_attended, mixed_bf)
    raw_scores, capped = masked_scores()
    probs = jnp.exp(capped - log_total)
    probs_bf = probs.astype(jnp.bfloat16)
    grad_value = jnp.einsum(
        "kgqp,qkgd->pkd", probs_bf, grad_mixed, preferred_element_type=jnp.float32
    )
    grad_probs = jnp.einsum(
        "qkgd,pkd->kgqp", grad_mixed, value_bf, preferred_element_type=jnp.float32
    )
    inner_sum = jnp.sum(probs * grad_probs, axis=-1, keepdims=True)
    grad_capped = probs * (grad_probs - inner_sum)
    grad_raw = (grad_capped * (1.0 - jnp.square(jnp.tanh(raw_scores / SOFT_CAP)))).astype(
        jnp.bfloat16
    )
    grad_query = (
        jnp.einsum("kgqp,pkd->qkgd", grad_raw, key_bf, preferred_element_type=jnp.float32) * scale
    )
    grad_key = (
        jnp.einsum("kgqp,qkgd->pkd", grad_raw, query_bf, preferred_element_type=jnp.float32) * scale
    )
    _, query_pull = jax.vjp(rope_query, query_linear)
    grad_query_lin = query_pull(grad_query)[0].astype(jnp.bfloat16)
    _, key_pull = jax.vjp(rope_key, key_linear)
    grad_key_lin = key_pull(grad_key)[0].astype(jnp.bfloat16)
    grad_value_lin = grad_value.reshape(seq_len, -1).astype(jnp.bfloat16)
    grad_query_w = contract_rows(seq_normed, grad_query_lin)
    grad_key_w = contract_rows(seq_normed, grad_key_lin)
    grad_value_w = contract_rows(seq_normed, grad_value_lin)
    grad_normed = lax.psum_scatter(
        contract_cols(grad_query_lin, back_qo[0])
        + contract_cols(grad_key_lin, back_kv[0])
        + contract_cols(grad_value_lin, back_kv[1]),
        "mp",
        scatter_dimension=0,
        tiled=True,
    )
    _, input_pull = jax.vjp(rms_norm, inputs, gain_rows[0])
    grad_input_part, grad_gain_zero = input_pull(grad_normed)
    grad_in = grad_hidden + grad_input_part
    sum_qo, sum_kv, sum_mlp = (
        lax.psum_scatter(
            jnp.stack([grad_query_w, grad_out_w]).astype(jnp.bfloat16),
            "dp",
            scatter_dimension=1,
            tiled=True,
        ).astype(jnp.float32),
        lax.psum_scatter(
            jnp.stack([grad_key_w, grad_value_w]).astype(jnp.bfloat16),
            "dp",
            scatter_dimension=1,
            tiled=True,
        ).astype(jnp.float32),
        lax.psum_scatter(
            jnp.concatenate([grad_gate_up_w, grad_down[None]], 0).astype(jnp.bfloat16),
            "dp",
            scatter_dimension=1,
            tiled=True,
        ).astype(jnp.float32),
    )
    gain_terms = jnp.stack([grad_gain_zero, grad_gain_one, grad_gain_two, grad_gain_three]).reshape(
        -1
    )
    sum_gains = lax.psum_scatter(gain_terms, ("dp", "mp"), scatter_dimension=0, tiled=True)
    local_squares = (
        jnp.sum(sum_qo * sum_qo)
        + jnp.sum(sum_kv * sum_kv)
        + jnp.sum(sum_mlp * sum_mlp)
        + jnp.sum(sum_gains * sum_gains)
    )
    grad_norm = jnp.sqrt(lax.psum(local_squares, ("dp", "mp")))
    factor = jnp.minimum(1.0, CLIP_SCALE * math.sqrt(PARAMS) / grad_norm)
    new_w_qo, new_m_qo, new_v_qo = adam_update(w_qo, m_qo, v_qo, sum_qo, factor)
    new_w_kv, new_m_kv, new_v_kv = adam_update(w_kv, m_kv, v_kv, sum_kv, factor)
    new_w_mlp, new_m_mlp, new_v_mlp = adam_update(w_mlp, m_mlp, v_mlp, sum_mlp, factor)
    new_gains, new_m_gains, new_v_gains = adam_update(
        norm_gains, m_gains, v_gains, sum_gains, factor
    )
    return (
        outputs,
        grad_in,
        grad_norm.reshape(1),
        new_w_qo,
        new_w_kv,
        new_w_mlp,
        new_gains,
        new_m_qo,
        new_m_kv,
        new_m_mlp,
        new_m_gains,
        new_v_qo,
        new_v_kv,
        new_v_mlp,
        new_v_gains,
    )


def solution(mesh):
    placed = (
        P(("dp", "mp"), None),
        P(("dp", "mp"), None),
        P("dp", None),
        P("dp", None),
        P(),
        P(None, "dp", "mp"),
        P(None, "dp", "mp"),
        P(None, "dp", "mp"),
        P(("dp", "mp")),
        P(None, "dp", "mp"),
        P(None, "dp", "mp"),
        P(None, "dp", "mp"),
        P(("dp", "mp")),
        P(None, "dp", "mp"),
        P(None, "dp", "mp"),
        P(None, "dp", "mp"),
        P(("dp", "mp")),
    )
    return jax.shard_map(
        local,
        mesh=mesh,
        in_specs=placed,
        out_specs=(
            P(("dp", "mp"), None),
            P(("dp", "mp"), None),
            P(),
            P(None, "dp", "mp"),
            P(None, "dp", "mp"),
            P(None, "dp", "mp"),
            P(("dp", "mp")),
            P(None, "dp", "mp"),
            P(None, "dp", "mp"),
            P(None, "dp", "mp"),
            P(("dp", "mp")),
            P(None, "dp", "mp"),
            P(None, "dp", "mp"),
            P(None, "dp", "mp"),
            P(("dp", "mp")),
        ),
        check_vma=False,
    )
```

profile of v0, /device:TPU:0, one launch (start us, length us, event | category | flops | bytes accessed | tf_op | source)
XLA Modules:
  0.0 2190.1 jit_solution(6801145849870063751)
XLA Ops:
  10.1 7.8 fusion.135
  18.9 43.8 %all-reduce.4 = f32[9216]{0:T(1024)S(1)} all-reduce(f32[9216]{0:T(1024)S(1)} %dynamic-update-slice), channel_id=1, replica_groups=mesh['dp'=8,'mp'=4] {'dp','mp'}, use_global_device_ids=true, to_apply=%add.4 | all-reduce | flops 9216 | bytes 73728
  68.6 24.3 %fusion.107 = bf16[2,288,512]{2,1,0:T(8,128)(2,1)} fusion(f32[2,288,512]{2,1,0:T(8,128)S(1)} %copy-done.17, f32[2]{0:T(128)S(1)} %copy-done.56, s32[]{:T(128)} %bitcast.12, s32[]{:T(128)S(6)} %sign.48, s32[]{:T(128)S(6)} %select_n.87, f32[2]{0:T(128)S(1)} %copy-done.57, s32[]{:T(128)S(6)} %neg.34, s32[]{:T(128)S(6)} %sub.122), kind=kLoop, calls=%fused_computation.167 | loop fusion | flops 5898240 | bytes 1769508 | tf_op jit(solution)/shard_map/convert_element_type | solution.py:37
  97.9 10.5 all-gather.8.cloned.1.call-done
  112.6 4.6 fusion.117
  119.3 71.8 %all-gather.12.cloned.1.call-done = bf16[2,2304,512]{2,1,0:T(8,128)(2,1)} async-done(((bf16[2,288,512]{2,1,0:T(8,128)(2,1)}), bf16[2,2304,512]{2,1,0:T(8,128)(2,1)}) %all-gather.12.cloned.1.call-update) | async-done | bytes 4718608 | tf_op jit(solution)/shard_map/all_gather | solution.py:124
  198.6 5.5 fusion.52
  212.5 5.6 fusion.75
  218.1 69.1 %reduce-scatter.8.cloned.1.call-done = f32[224,2304]{1,0:T(8,128)} async-done(((f32[896,2304]{1,0:T(8,128)}), f32[224,2304]{1,0:T(8,128)}) %reduce-scatter.8.cloned.1.call-update) | async-done | bytes 2064400 | tf_op jit(solution)/shard_map/reduce_scatter | solution.py:174
  295.2 84.8 %fusion.33 = bf16[3,288,2304]{2,1,0:T(8,128)(2,1)} fusion(f32[3,288,2304]{2,1,0:T(8,128)} %param.27, f32[3]{0:T(128)S(1)} %copy-done.54, s32[]{:T(128)} %bitcast.23, s32[]{:T(128)S(6)} %sign.50, s32[]{:T(128)S(6)} %select_n.93, f32[3]{0:T(128)S(1)} %copy-done.55, s32[]{:T(128)S(6)} %neg.36, s32[]{:T(128)S(6)} %sub.130), kind=kLoop, calls=%fused_computation.52 | loop fusion | flops 39813120 | bytes 11943980 | tf_op jit(solution)/shard_map/convert_element_type | solution.py:37
  380.0 605.9 %all-gather.14.cloned.1.call-done = bf16[3,2304,2304]{2,1,0:T(8,128)(2,1)} async-done(((bf16[3,288,2304]{2,1,0:T(8,128)(2,1)}), bf16[3,2304,2304]{2,1,0:T(8,128)(2,1)}) %all-gather.14.cloned.1.call-update) | async-done | bytes 31850512 | tf_op jit(solution)/shard_map/all_gather | solution.py:126
  985.9 28.8 %convolution_bitcast_fusion = f32[2,896,2304]{1,2,0:T(8,128)} fusion(bf16[3,2304,2304]{2,1,0:T(8,128)(2,1)} %all-gather.14.cloned.1.call-done, bf16[896,2304]{1,0:T(8,128)(2,1)} %all-gather.16.cloned.1.call-done), kind=kOutput, calls=%fused_computation.18 | convolution fusion | flops 19025362944 | bytes 52494336 | tf_op jit(solution)/shard_map/td,kdf->ktf/dot_general | solution.py:180
  1014.7 22.6 %fusion.6 = f32[896,2304]{1,0:T(8,128)} fusion(bf16[3,2304,2304]{2,1,0:T(8,128)(2,1)} %all-gather.14.cloned.1.call-done, f32[2,896,2304]{1,2,0:T(8,128)} %convolution_bitcast_fusion), kind=kOutput, calls=%fused_computation.17 | convolution fusion | flops 9533325312 | bytes 35389440 | tf_op jit(solution)/shard_map/dot_general | solution.py:84
  1037.4 70.9 %reduce-scatter.10.cloned.1.call-done = f32[224,2304]{1,0:T(8,128)} async-done(((f32[896,2304]{1,0:T(8,128)}), f32[224,2304]{1,0:T(8,128)}) %reduce-scatter.10.cloned.1.call-update) | async-done | bytes 2064400 | tf_op jit(solution)/shard_map/reduce_scatter | solution.py:183
  1116.5 34.2 %all-gather.18.cloned.1.call-done = bf16[896,2304]{1,0:T(8,128)(2,1)} async-done(((bf16[224,2304]{1,0:T(8,128)(2,1)}), bf16[896,2304]{1,0:T(8,128)(2,1)}) %all-gather.18.cloned.1.call-update) | async-done | bytes 4128784 | tf_op jit(solution)/shard_map/all_gather | solution.py:193
  1150.7 26.8 %fusion.58 = (bf16[1,896,2304]{1,2,0:T(8,128)(2,1)}, bf16[1,896,2304]{1,2,0:T(8,128)(2,1)}) fusion(f32[2,896,2304]{1,2,0:T(8,128)} %convolution_bitcast_fusion, bf16[896,2304]{1,0:T(8,128)(2,1)} %all-gather.18.cloned.1.call-done, bf16[3,2304,2304]{2,1,0:T(8,128)(2,1)} %all-gather.14.cloned.1.call-done), kind=kOutput, calls=%fused_computation.87 | convolution fusion | flops 9562226688 | bytes 39518208 | tf_op jit(solution)/shard_map/dot_general | solution.py:199
  1177.5 27.3 %fusion.43 = f32[896,2304]{1,0:T(8,128)} fusion(bf16[3,2304,2304]{2,1,0:T(8,128)(2,1)} %all-gather.14.cloned.1.call-done, bf16[1,896,2304]{1,2,0:T(8,128)(2,1)} %get-tuple-element.39, bf16[1,896,2304]{1,2,0:T(8,128)(2,1)} %get-tuple-element.38), kind=kOutput, calls=%fused_computation.73 | convolution fusion | flops 19029491712 | bytes 37748736 | tf_op jit(solution)/shard_map/ktf,kdf->td/dot_general | solution.py:213
  1204.9 71.0 %reduce-scatter.12.cloned.1.call-done = f32[224,2304]{1,0:T(8,128)} async-done(((f32[896,2304]{1,0:T(8,128)}), f32[224,2304]{1,0:T(8,128)}) %reduce-scatter.12.cloned.1.call-update) | async-done | bytes 2064400 | tf_op jit(solution)/shard_map/reduce_scatter | solution.py:212
  1284.4 34.2 %all-gather.20.cloned.1.call-done = bf16[896,2304]{1,0:T(8,128)(2,1)} async-done(((bf16[224,2304]{1,0:T(8,128)(2,1)}), bf16[896,2304]{1,0:T(8,128)(2,1)}) %all-gather.20.cloned.1.call-update) | async-done | bytes 4128784 | tf_op jit(solution)/shard_map/all_gather | solution.py:223
  1318.6 5.6 fusion.86
  1324.2 5.2 fusion.41
  1329.5 5.4 fusion.99
  1375.5 20.8 fusion.3
  1396.3 29.2 %fusion.2 = bf16[2,2304,2304]{2,1,0:T(8,128)(2,1)} fusion(bf16[1,896,2304]{1,2,0:T(8,128)(2,1)} %get-tuple-element.39, bf16[1,896,2304]{1,2,0:T(8,128)(2,1)} %get-tuple-element.38, bf16[896,2304]{1,0:T(8,128)(2,1)S(1)} %copy-done.61), kind=kOutput, calls=%fused_computation.4 | convolution fusion | flops 19052494848 | bytes 33619968 | tf_op jit(solution)/shard_map/ktf,td->kdf/dot_general | solution.py:208
  1425.5 22.0 %pad_maximum_fusion = bf16[3,2304,2304]{2,1,0:T(8,128)(2,1)} fusion(bf16[1,2304,2304]{2,1,0:T(8,128)(2,1)} %fusion.3, bf16[2,2304,2304]{2,1,0:T(8,128)(2,1)} %fusion.2), kind=kLoop, calls=%fused_computation | loop fusion | flops 15925248 | bytes 63700992 | tf_op jit(solution)/shard_map/concatenate | solution.py:280
  1450.1 67.5 %reduce-scatter.16.cloned.1.call-done = bf16[2,288,512]{2,1,0:T(8,128)(2,1)} async-done(((bf16[2,2304,512]{2,1,0:T(8,128)(2,1)}), bf16[2,288,512]{2,1,0:T(8,128)(2,1)}) %reduce-scatter.16.cloned.1.call-update) | async-done | bytes 589840 | tf_op jit(solution)/shard_map/reduce_scatter | solution.py:267
  1520.8 70.1 %reduce-scatter.14.cloned.1.call-done = f32[224,2304]{1,0:T(8,128)} async-done(((f32[896,2304]{1,0:T(8,128)}), f32[224,2304]{1,0:T(8,128)}) %reduce-scatter.14.cloned.1.call-update) | async-done | bytes 2064400 | tf_op jit(solution)/shard_map/reduce_scatter | solution.py:255
  1593.0 44.4 %all-reduce.5 = f32[9216]{0:T(1024)S(1)} all-reduce(f32[9216]{0:T(1024)S(1)} %reshape.540), channel_id=9, replica_groups=mesh['dp'=8,'mp'=4] {'dp','mp'}, use_global_device_ids=true, to_apply=%region_27.28.clone | all-reduce | flops 9216 | bytes 73728
  1638.1 469.9 %reduce-scatter.20.cloned.1.call-done = bf16[3,288,2304]{2,1,0:T(8,128)(2,1)} async-done(((bf16[3,2304,2304]{2,1,0:T(8,128)(2,1)}), bf16[3,288,2304]{2,1,0:T(8,128)(2,1)}) %reduce-scatter.20.cloned.1.call-update) | async-done | bytes 3981328 | tf_op jit(solution)/shard_map/reduce_scatter | solution.py:279
  2108.1 4.8 fusion.27
  2118.2 39.5 %psum.7 = f32[]{:T(128)} all-reduce(f32[]{:T(128)S(6)} %add.301), channel_id=1, replica_groups=mesh['dp'=8,'mp'=4] {'dp','mp'}, use_global_device_ids=true, to_apply=%region_29.30 | all-reduce | flops 1 | bytes 8 | tf_op jit(solution)/shard_map/psum | solution.py:296
  2166.6 15.6 multiply_subtract_fusion
  (253 shorter events, 116.1 us)
Async XLA Ops:
  7.2 61.3 %copy-start.56 = (f32[2]{0:T(128)S(1)}, f32[2]{0:T(128)}, u32[]{:S(2)}) copy-start(f32[2]{0:T(128)} %constant.220) | copy-start | bytes 28
  7.2 61.3 %copy-start.57 = (f32[2]{0:T(128)S(1)}, f32[2]{0:T(128)}, u32[]{:S(2)}) copy-start(f32[2]{0:T(128)} %constant.206.clone) | copy-start | bytes 28
  7.2 58.4 %copy-start = (f32[224,2304]{1,0:T(8,128)S(1)}, f32[224,2304]{1,0:T(8,128)}, u32[]{:S(2)}) copy-start(f32[224,2304]{1,0:T(8,128)} %param.20) | copy-start | bytes 6193156
  7.2 61.3 %copy-start.17 = (f32[2,288,512]{2,1,0:T(8,128)S(1)}, f32[2,288,512]{2,1,0:T(8,128)}, u32[]{:S(2)}) copy-start(f32[2,288,512]{2,1,0:T(8,128)} %param.25) | copy-start | bytes 3538948
  7.2 90.7 %all-gather.10.cloned.1.call-start = ((), (), s32[]{:S(2)}) async-start(), calls=%async_computation.8 | async-start | bytes 2654208 | tf_op jit(solution)/shard_map/all_gather | solution.py:125
  17.9 90.5 %all-gather.8.cloned.1.call-start = ((), (), s32[]{:S(2)}) async-start(), calls=%async_computation.7 | async-start | bytes 5160960 | tf_op jit(solution)/shard_map/all_gather | solution.py:138
  65.0 224.0 %copy-start.34 = (f32[2304]{0:T(1024)}, f32[2304]{0:T(1024)S(1)}, u32[]{:S(2)}) copy-start(f32[2304]{0:T(1024)S(1)} %get-tuple-element.55) | copy-start | bytes 27652
  66.9 124.2 %all-gather.12.cloned.1.call-start = ((), (), s32[]{:S(2)}) async-start(), calls=%async_computation.9 | async-start | bytes 5308416 | tf_op jit(solution)/shard_map/all_gather | solution.py:124
  92.9 194.4 %reduce-scatter.8.cloned.1.call-start = ((), (), s32[]{:S(2)}) async-start(), calls=%async_computation.10 | async-start | bytes 10321920 | tf_op jit(solution)/shard_map/reduce_scatter | solution.py:174
  117.2 87.1 %copy-start.11 = (f32[896,256]{0,1:T(8,128)}, f32[896,256]{0,1:T(8,128)S(1)}, u32[]{:S(2)}) copy-start(f32[896,256]{0,1:T(8,128)S(1)} %get-tuple-element.52) | copy-start | bytes 2752516
  218.1 162.0 %all-gather.16.cloned.1.call-start = ((), (), s32[]{:S(2)}) async-start(), calls=%async_computation.12 | async-start | bytes 5160960 | tf_op jit(solution)/shard_map/all_gather | solution.py:179
  291.2 88.7 %copy-start.48 = (f32[224]{0:T(256)}, f32[224]{0:T(256)S(1)}, u32[]{:S(2)}) copy-start(f32[224]{0:T(256)S(1)} %get-tuple-element.36) | copy-start | bytes 2692
  293.7 692.2 %all-gather.14.cloned.1.call-start = ((), (), s32[]{:S(2)}) async-start(), calls=%async_computation.11 | async-start | bytes 35831808 | tf_op jit(solution)/shard_map/all_gather | solution.py:126
  380.0 728.4 %reduce-scatter.10.cloned.1.call-start = ((), (), s32[]{:S(2)}) async-start(), calls=%async_computation.13 | async-start | bytes 10321920 | tf_op jit(solution)/shard_map/reduce_scatter | solution.py:183
  1037.3 76.5 %copy-start.3 = (f32[224,2304]{1,0:T(8,128)S(1)}, f32[224,2304]{1,0:T(8,128)}, u32[]{:S(2)}) copy-start(f32[224,2304]{1,0:T(8,128)} %copy-done.2) | copy-start | bytes 6193156
  1037.3 113.4 %all-gather.18.cloned.1.call-start = ((), (), s32[]{:S(2)}) async-start(), calls=%async_computation.14 | async-start | bytes 5160960 | tf_op jit(solution)/shard_map/all_gather | solution.py:193
  1116.5 159.4 %reduce-scatter.12.cloned.1.call-start = ((), (), s32[]{:S(2)}) async-start(), calls=%async_computation.15 | async-start | bytes 10321920 | tf_op jit(solution)/shard_map/reduce_scatter | solution.py:212
  1204.8 73.3 %copy-start.49 = (f32[224]{0:T(256)S(1)}, f32[224]{0:T(256)}, u32[]{:S(2)}) copy-start(f32[224]{0:T(256)} %copy-done.48) | copy-start | bytes 2692
  1204.9 73.3 %copy-start.35 = (f32[2304]{0:T(1024)S(1)}, f32[2304]{0:T(1024)}, u32[]{:S(2)}) copy-start(f32[2304]{0:T(1024)} %copy-done.34) | copy-start | bytes 27652
  1204.9 73.3 %copy-start.42 = (f32[224]{0:T(256)S(1)}, f32[224]{0:T(256)}, u32[]{:S(2)}) copy-start(f32[224]{0:T(256)} %copy-done.41) | copy-start | bytes 2692
  1204.9 113.7 %all-gather.20.cloned.1.call-start = ((), (), s32[]{:S(2)}) async-start(), calls=%async_computation.16 | async-start | bytes 5160960 | tf_op jit(solution)/shard_map/all_gather | solution.py:223
  1284.4 163.9 %reduce-scatter.18.cloned.1.call-start = ((), (), s32[]{:S(2)}) async-start(), calls=%async_computation.19 | async-start | bytes 2654208 | tf_op jit(solution)/shard_map/reduce_scatter | solution.py:273
  1350.0 167.5 %reduce-scatter.16.cloned.1.call-start = ((), (), s32[]{:S(2)}) async-start(), calls=%async_computation.18 | async-start | bytes 5308416 | tf_op jit(solution)/shard_map/reduce_scatter | solution.py:267
  1363.7 227.1 %reduce-scatter.14.cloned.1.call-start = ((), (), s32[]{:S(2)}) async-start(), calls=%async_computation.17 | async-start | bytes 10321920 | tf_op jit(solution)/shard_map/reduce_scatter | solution.py:255
  1375.4 732.6 %reduce-scatter.20.cloned.1.call-start = ((), (), s32[]{:S(2)}) async-start(), calls=%async_computation.20 | async-start | bytes 35831808 | tf_op jit(solution)/shard_map/reduce_scatter | solution.py:279
  1447.6 143.3 %copy-start.1 = (f32[224,2304]{1,0:T(8,128)S(1)}, f32[224,2304]{1,0:T(8,128)}, u32[]{:S(2)}) copy-start(f32[224,2304]{1,0:T(8,128)} %param.20) | copy-start | bytes 6193156
  1447.6 143.3 %copy-start.33 = (f32[2304]{0:T(1024)S(1)}, f32[2304]{0:T(1024)}, u32[]{:S(2)}) copy-start(f32[2304]{0:T(1024)} %copy-done.32) | copy-start | bytes 27652
  1447.6 143.3 %copy-start.40 = (f32[224]{0:T(256)S(1)}, f32[224]{0:T(256)}, u32[]{:S(2)}) copy-start(f32[224]{0:T(256)} %copy-done.39) | copy-start | bytes 2692
  1447.6 190.5 %copy-start.45 = (f32[224]{0:T(256)S(1)}, f32[224]{0:T(256)}, u32[]{:S(2)}) copy-start(f32[224]{0:T(256)} %copy-done.44) | copy-start | bytes 2692
  2114.2 44.3 %copy-start.50 = (f32[288]{0:T(512)S(1)}, f32[288]{0:T(512)}, u32[]{:S(2)}) copy-start(f32[288]{0:T(512)} %param.28) | copy-start | bytes 3460
  2118.2 45.6 %copy-start.23 = (f32[2,288,256]{2,1,0:T(8,128)S(1)}, f32[2,288,256]{2,1,0:T(8,128)}, u32[]{:S(2)}) copy-start(f32[2,288,256]{2,1,0:T(8,128)} %param.26) | copy-start | bytes 1769476
  2118.2 45.6 %copy-start.27 = (bf16[2,288,256]{2,1,0:T(8,128)(2,1)S(1)}, bf16[2,288,256]{2,1,0:T(8,128)(2,1)}, u32[]{:S(2)}) copy-start(bf16[2,288,256]{2,1,0:T(8,128)(2,1)} %reduce-scatter.18.cloned.1.call-done) | copy-start | bytes 884740
  (53 other events, 490.5 us)
Sparse Core Ops, SparseCore 0:
  18.0 55.5 all-gather.9
  75.7 32.6 all-gather.7
  111.2 79.8 all-gather.11
  218.2 69.0 reduce-scatter.7
  293.9 34.1 all-gather.15
  380.1 605.7 all-gather.13
  1037.4 70.8 reduce-scatter.9
  1116.6 34.0 all-gather.17
  1205.0 70.8 reduce-scatter.11
  1284.5 34.1 all-gather.19
  1350.1 68.9 reduce-scatter.17
  1423.2 94.2 reduce-scatter.15
  1520.2 70.6 reduce-scatter.13
  1594.6 513.4 reduce-scatter.19
where the time goes:
time: 2200 us; the launch traced here: 2190 us
  waiting for transfers between devices  1580 us (72%)
  other arithmetic  223 us (10%)
  matrix products  218 us (10%)
  blocking collectives  128 us (6%)
  between operations  24.4 us (1%)
    all_gather x1, waiting for transfers between devices, local(): lax.all_gather(low_mlp, 'dp', axis=1, tiled=True)  606 us
    reduce_scatter x1, waiting for transfers between devices, local(): lax.psum_scatter(jnp.concatenate([grad_gate_up_w, grad_down[None]], 0).as...  470 us
    convert_element_type x3, other arithmetic, quantize(): ((sliced * spacing).astype(jnp.float32) * step_sizes).astype(jnp.bfloat16)  117 us
    unnamed x2, blocking collectives  88.2 us
    all_gather x1, waiting for transfers between devices, local(): lax.all_gather(low_qo, 'dp', axis=1, tiled=True)  71.8 us
    reduce_scatter x1, waiting for transfers between devices, local(): lax.psum_scatter(jnp.einsum('ktf,kdf->td', row_block, back_mlp[:2], prefe...  71 us
    reduce_scatter x1, waiting for transfers between devices, local(): lax.psum_scatter(contract_cols(row_block, full_mlp[2]), 'mp', scatter_dim...  70.9 us
    reduce_scatter x1, waiting for transfers between devices, local(): lax.psum_scatter(contract_cols(grad_query_lin, back_qo[0]) + contract_col...  70.1 us
  transfers between devices with their start and end apart: 14, of which 11 were waited for; matrix products, arithmetic and copies ran while one was open for 10% of the time, Pallas kernels for 0%

commit v1 on v0

v1 whole, which is shorter than its diff:
```python
import functools
import math

import jax
import jax.numpy as jnp
from jax import lax
from jax.experimental import pallas as pl
from jax.experimental.pallas import tpu as pltpu
from jax.sharding import PartitionSpec as P

D = 2304
HEAD_WIDTH = 256
FF = 9216
NORMS = 4
QW = 2048
PARAMS = 77865984

EPSILON = 1e-06
SOFT_CAP = 50.0
ROPE_BASE = 10000.0
MASKED_SCORE = -1e30
FIRST_DECAY = 0.9
SECOND_DECAY = 0.95
LEARN_RATE = 0.04
WEIGHT_DECAY = 0.1
ADAM_EPSILON = 1e-08
CLIP_SCALE = 0.5

BF = jnp.bfloat16
F32 = jnp.float32


def quantize(master, fan_in, selector):
    return quantize_by(master, jnp.float32(1.0 / (32.0 * math.sqrt(fan_in))), selector)


def quantize_by(master, step, selector):
    spacing = jnp.where(selector == 0, 1.0, jnp.where(selector == 1, 16.0, 64.0)).astype(F32)
    half = jnp.floor(spacing * 0.5)
    inverse = 1.0 / spacing
    codes = jnp.clip(jnp.floor(master / step + 0.5), -128.0, 127.0)
    top = 128.0 * inverse
    sliced = jnp.clip(jnp.floor((codes + half) * inverse), -top, top - 1.0)
    return ((sliced * spacing) * step).astype(BF)


def inv_root(values):
    return lax.rsqrt(jnp.mean(values * values, axis=-1, keepdims=True) + EPSILON)


def rms_norm(values, norm_gain):
    return values * inv_root(values) * (1.0 + norm_gain)


def rms_back(values, norm_gain, grad):
    root = inv_root(values)
    scaled = grad * (1.0 + norm_gain)
    dot = jnp.mean(values * scaled, axis=-1, keepdims=True)
    grad_values = root * scaled - values * (root * root * root * dot)
    grad_gain = jnp.sum(values * root * grad, axis=0)
    return grad_values, grad_gain


def doc_positions(segments):
    slot_index = jnp.arange(segments.shape[0], dtype=jnp.int32)
    previous = jnp.concatenate([segments[:1] - 1, segments[:-1]])
    starts = segments != previous
    doc_begin = lax.cummax(jnp.where(starts, slot_index, 0), axis=0)
    return slot_index - doc_begin


def rotate(values, cosine, sine):
    half_dim = HEAD_WIDTH // 2
    turned = jnp.concatenate([-values[..., half_dim:], values[..., :half_dim]], -1)
    return values * cosine + turned * sine


def rotate_back(grads, cosine, sine):
    half_dim = HEAD_WIDTH // 2
    scaled = grads * sine
    turned = jnp.concatenate([scaled[..., half_dim:], -scaled[..., :half_dim]], -1)
    return grads * cosine + turned


def mm(left, right):
    return lax.dot_general(left, right, (((1,), (0,)), ((), ())), preferred_element_type=F32)


def mm_rows(left, right):
    return lax.dot_general(left, right, (((0,), (0,)), ((), ())), preferred_element_type=F32)


def mm_cols(left, right):
    return lax.dot_general(left, right, (((1,), (1,)), ((), ())), preferred_element_type=F32)


def adam_update(master, first_moment, second_moment, gradient, factor):
    clipped = gradient * factor
    new_first = FIRST_DECAY * first_moment + (1.0 - FIRST_DECAY) * clipped
    new_second = SECOND_DECAY * second_moment + (1.0 - SECOND_DECAY) * clipped * clipped
    new_master = master - LEARN_RATE * (
        new_first / (jnp.sqrt(new_second) + ADAM_EPSILON) + WEIGHT_DECAY * master
    )
    return (new_master, new_first, new_second)


MESH = pl.DeviceIdType.MESH
ANY = pl.BlockSpec(memory_space=pl.ANY)
VMEM = pl.BlockSpec(memory_space=pltpu.VMEM)
ROWS = 32


class Net:
    def __init__(self, n_dp, n_mp, send_sems, recv_sems, local_sems=None):
        self.n_dp, self.n_mp = n_dp, n_mp
        self.send_sems, self.recv_sems, self.local_sems = send_sems, recv_sems, local_sems
        self.used, self.used_local, self.open = 0, 0, []
        self.i, self.m = lax.axis_index("dp"), lax.axis_index("mp")
        self.y, self.j = self.i % 2, self.i // 2
        self.zl = self.j % 2
        self.c, self.x = self.m % 2, self.m // 2
        self.core_n = (self.i, self.m + 1 - 2 * self.c)
        self.x_n = (self.i, (self.m + 2) % 4)
        self.y_n = (self.i + 1 - 2 * self.y, self.m)
        self.z_n = (self.i + 2 - 4 * self.zl, self.m)

    def z_at(self, d):
        nj = self.n_dp // 2
        return (((self.j + d) % nj) * 2 + self.y, self.m)

    def place(self):
        return (1 - self.y) * self.j + self.y * (self.n_dp - 1 - self.j)

    def ring(self, at):
        n, nj = self.n_dp, self.n_dp // 2
        at = at % n
        late = at // nj
        return (1 - late) * 2 * at + late * (2 * (n - 1 - at) + 1)

    def meet(self, devices):
        barrier = pltpu.get_barrier_semaphore()
        for device in devices:
            pl.semaphore_signal(barrier, inc=1, device_id=device, device_id_type=MESH)
        pl.semaphore_wait(barrier, len(devices))

    def send(self, src, dst, device):
        at = self.used
        self.used += 1
        copy = pltpu.make_async_remote_copy(
            src_ref=src, dst_ref=dst, send_sem=self.send_sems.at[at], recv_sem=self.recv_sems.at[at],
            device_id=device, device_id_type=MESH,
        )
        copy.start()
        self.open.append(copy.wait_send)
        return copy

    def move(self, src, dst):
        at = self.used_local
        self.used_local += 1
        copy = pltpu.make_async_copy(src, dst, self.local_sems.at[at])
        copy.start()
        return copy

    def keep(self, src, dst):
        self.open.append(self.move(src, dst).wait)

    def close(self):
        for wait in self.open:
            wait()


def upper(count):
    return count // 16 * 8


def dma(n):
    return pltpu.SemaphoreType.DMA((n,))


def call(kernel, outs, out_specs, in_specs, scratch, cid, mb, flops=0):
    return pl.pallas_call(
        kernel,
        out_shape=outs,
        in_specs=in_specs,
        out_specs=out_specs,
        scratch_shapes=scratch,
        compiler_params=pltpu.CompilerParams(
            collective_id=cid, has_side_effects=True, vmem_limit_bytes=mb << 20
        ),
    )


def by_rows(total, body, carry=0):
    return lax.fori_loop(
        0, total // ROWS, lambda t, state: body(pl.ds(pl.multiple_of(t * ROWS, ROWS), ROWS), state), carry
    )


def everyone(n_dp, n_mp, i, m):
    flat = i * n_mp + m
    total = n_dp * n_mp
    return [(((flat + t) % total) // n_mp, (flat + t) % n_mp) for t in range(1, total)]


def spread_kernel(n_dp, n_mp, own, full, ss, rs, ls):
    net = Net(n_dp, n_mp, ss, rs, ls)
    others = everyone(n_dp, n_mp, net.i, net.m)
    net.meet(others)
    flat = net.i * n_mp + net.m
    copies = [net.send(own, full.at[flat], device) for device in others]
    net.keep(own, full.at[flat])
    for copy in copies:
        copy.wait_recv()
    net.close()


def spread(n_dp, n_mp, own):
    total = n_dp * n_mp
    return call(
        functools.partial(spread_kernel, n_dp, n_mp),
        jax.ShapeDtypeStruct((total,) + own.shape, own.dtype), VMEM, [VMEM],
        [dma(total), dma(total), dma(1)], 1, 16,
    )(own)


def gather_seq_steps(net, own, seq):
    far = net.send(own, seq.at[1], net.x_n)
    near = net.send(own, seq.at[2], net.core_n)
    net.keep(own, seq.at[0])

    def finish():
        far.wait_recv()
        both = net.send(seq.at[1], seq.at[3], net.core_n)
        near.wait_recv()
        both.wait_recv()

    return finish


def head_kernel(n_dp, n_mp, q, kv, o, tok, wq, wkv, wo, seq, ss, rs, ls):
    net = Net(n_dp, n_mp, ss, rs, ls)
    p = net.place()
    right = (net.ring(p + 1), net.m)
    left = (net.ring(p + n_dp - 1), net.m)
    net.meet([right, left, net.x_n, net.core_n])
    wrows = o.shape[0]
    hr = upper(wrows)
    top, low = pl.ds(0, hr), pl.ds(hr, wrows - hr)
    a = net.send(q, wq.at[net.i], right)
    b = net.send(kv, wkv.at[net.i], left)
    finish = gather_seq_steps(net, tok, seq)
    net.keep(q, wq.at[net.i])
    net.keep(kv, wkv.at[net.i])
    net.keep(o, wo.at[net.i])
    for hop in range(1, n_dp):
        from_right, from_left = net.ring(p + n_dp - hop), net.ring(p + hop)
        a.wait_recv()
        if hop < n_dp - 1:
            a = net.send(wq.at[from_right], wq.at[from_right], right)
        else:
            oa = net.send(o.at[top], wo.at[net.i, top], right)
        b.wait_recv()
        if hop < n_dp - 1:
            b = net.send(wkv.at[from_left], wkv.at[from_left], left)
        else:
            ob = net.send(o.at[low], wo.at[net.i, low], left)
        if hop == n_dp // 2:
            finish()
    for hop in range(1, n_dp):
        from_right, from_left = net.ring(p + n_dp - hop), net.ring(p + hop)
        oa.wait_recv()
        if hop < n_dp - 1:
            oa = net.send(wo.at[from_right, top], wo.at[from_right, top], right)
        ob.wait_recv()
        if hop < n_dp - 1:
            ob = net.send(wo.at[from_left, low], wo.at[from_left, low], left)
    net.close()


def head(n_dp, n_mp, q, kv, o, tok):
    full = lambda a: jax.ShapeDtypeStruct((n_dp,) + a.shape, BF)
    count = 4 * n_dp + 8
    return call(
        functools.partial(head_kernel, n_dp, n_mp),
        [full(q), full(kv), full(o), jax.ShapeDtypeStruct((4,) + tok.shape, BF)],
        [ANY] * 4, [ANY] * 4, [dma(count), dma(count), dma(8)], 2, 16,
    )(q, kv, o, tok)


def gather_pair_steps(net, own, group):
    far = net.send(own, group.at[2], net.x_n)
    zed = net.send(own, group.at[1], net.z_n)
    near = net.send(own, group.at[4], net.core_n)
    net.keep(own, group.at[0])

    def finish():
        zed.wait_recv()
        both = net.send(group.at[1], group.at[3], net.x_n)
        near_z = net.send(group.at[1], group.at[5], net.core_n)
        far.wait_recv()
        near_x = net.send(group.at[2], group.at[6], net.core_n)
        both.wait_recv()
        near_both = net.send(group.at[3], group.at[7], net.core_n)
        for copy in (near, near_z, near_x, near_both):
            copy.wait_recv()

    return finish


def weights_start(net, low, full, ks):
    nj = net.n_dp // 2
    width = full.shape[-1]
    half = lambda which: pl.ds(pl.multiple_of(which * width, width), width)
    flight = {}
    for k in ks:
        own = low.at[k, :, half(net.zl)]
        net.keep(own, full.at[k, net.i])
        flight[k, 0] = net.send(own, full.at[k, net.i], net.y_n)
        for d in sorted(range(1, nj), key=lambda d: -abs(d - nj // 2) * 0 - (d == nj // 2)):
            flight[k, d] = net.send(
                low.at[k, :, half(((net.j + d) % nj) % 2)], full.at[k, net.i], net.z_at(d)
            )
    return flight


def weights_relay(net, full, flight, k):
    nj = net.n_dp // 2
    relays = [flight[k, 0]]
    for d in range(1, nj):
        flight[k, d].wait_recv()
        at = ((net.j + nj - d) % nj) * 2 + net.y
        relays.append(net.send(full.at[k, at], full.at[k, at], net.y_n))
    return relays


def pair_partners(net, with_y):
    nj = net.n_dp // 2
    zs = [net.z_at(d) for d in range(1, nj)] if with_y else [net.z_n]
    return [net.core_n, net.x_n] + zs + ([net.y_n] if with_y else [])


def mid_kernel(
    n_dp, n_mp, near, far, inputs, gains, low, att, hid, group, full,
    r1, s2, r2, own, ss, rs, ls,
):
    net = Net(n_dp, n_mp, ss, rs, ls)
    net.meet(pair_partners(net, True))
    rows = inputs.shape[0]
    c1 = net.send(far.at[1], r1.at[1], net.core_n)
    c0 = net.send(far.at[0], r1.at[0], net.core_n)
    flight = weights_start(net, low, full, (0, 1))
    c1.wait_recv()

    def first(at, state):
        s2[at] = (near[1, at] + r1[1, at].astype(F32)).astype(BF)
        return state

    by_rows(rows, first)
    x = net.send(s2, r2, net.x_n)
    c0.wait_recv()
    x.wait_recv()
    g1, g2 = 1.0 + gains[1:2], 1.0 + gains[2:3]

    def second(at, state):
        total = near[0, at] + r1[0, at].astype(F32) + r2[at].astype(F32)
        att[at] = total
        hidden = inputs[at] + total * inv_root(total) * g1
        hid[at] = hidden
        own[at] = (hidden * inv_root(hidden) * g2).astype(BF)
        return state

    by_rows(rows, second)
    finish = gather_pair_steps(net, own, group)
    relays = weights_relay(net, full, flight, 0)
    finish()
    flight2 = weights_start(net, low, full, (2,))
    relays += weights_relay(net, full, flight, 1)
    relays += weights_relay(net, full, flight2, 2)
    for copy in relays:
        copy.wait_recv()
    net.close()


def mid(n_dp, n_mp, near, far, inputs, gains, low):
    rows = inputs.shape[0]
    nj = n_dp // 2
    count = 16 + 6 * nj
    block = (rows, D)
    width = low.shape[2] // 2
    return call(
        functools.partial(mid_kernel, n_dp, n_mp),
        [
            jax.ShapeDtypeStruct(block, F32), jax.ShapeDtypeStruct(block, F32),
            jax.ShapeDtypeStruct((8,) + block, BF),
            jax.ShapeDtypeStruct((3, n_dp, low.shape[1], width), BF),
        ],
        [VMEM, VMEM, ANY, ANY], [VMEM, ANY, VMEM, VMEM, ANY],
        [
            pltpu.VMEM((2,) + block, BF), pltpu.VMEM(block, BF), pltpu.VMEM(block, BF),
            pltpu.VMEM(block, BF), dma(count), dma(count), dma(8),
        ],
        3, 48,
    )(near, far, inputs, gains, low)


def reduce_pair_steps(net, near, far, r1, s2, r2, s3, r3, rows):
    cores = {k: net.send(far.at[k], r1.at[k], net.core_n) for k in (3, 2, 1, 0)}
    xs = {}
    for k in (3, 2):
        cores[k].wait_recv()

        def add(at, state, k=k):
            s2[k - 2, at] = (near[k, at] + r1[k, at].astype(F32)).astype(BF)
            return state

        by_rows(rows, add)
        xs[k] = net.send(s2.at[k - 2], r2.at[k - 2], net.x_n)
    cores[1].wait_recv()
    cores[0].wait_recv()
    xs[3].wait_recv()

    def zed(at, state):
        s3[at] = (near[1, at] + r1[1, at].astype(F32) + r2[1, at].astype(F32)).astype(BF)
        return state

    by_rows(rows, zed)
    z = net.send(s3, r3, net.z_n)
    xs[2].wait_recv()
    return z


def pair_scratch(rows):
    block = (rows, D)
    return [
        pltpu.VMEM((4,) + block, BF), pltpu.VMEM((2,) + block, BF), pltpu.VMEM((2,) + block, BF),
        pltpu.VMEM(block, BF), pltpu.VMEM(block, BF), pltpu.VMEM(block, BF),
    ]


def rms_back_rows(values, gain, grad):
    root = inv_root(values)
    scaled = grad * gain
    dot = jnp.mean(values * scaled, axis=-1, keepdims=True)
    return root * scaled - values * (root * root * root * dot), jnp.sum(values * root * grad, axis=0, keepdims=True)


def turn_kernel(
    n_dp, n_mp, near, far, hid, gains, out_grad, live, outputs, dgain, group,
    r1, s2, r2, s3, r3, own, ss, rs, ls,
):
    net = Net(n_dp, n_mp, ss, rs, ls)
    net.meet(pair_partners(net, False))
    rows = hid.shape[0]
    z = reduce_pair_steps(net, near, far, r1, s2, r2, s3, r3, rows)
    z.wait_recv()
    g3 = 1.0 + gains[3:4]

    def last(at, state):
        total = near[0, at] + r1[0, at].astype(F32) + r2[0, at].astype(F32) + r3[at].astype(F32)
        outputs[at] = hid[at] + total * inv_root(total) * g3
        grad, dg = rms_back_rows(total, g3, out_grad[at] * live[at])
        own[at] = grad.astype(BF)
        return state + dg

    dgain[...] = by_rows(rows, last, jnp.zeros((1, D), F32))
    gather_pair_steps(net, own, group)()
    net.close()


def turn(n_dp, n_mp, near, far, hid, gains, out_grad, live):
    rows = hid.shape[0]
    block = (rows, D)
    return call(
        functools.partial(turn_kernel, n_dp, n_mp),
        [jax.ShapeDtypeStruct(block, F32), jax.ShapeDtypeStruct((1, D), F32), jax.ShapeDtypeStruct((8,) + block, BF)],
        [VMEM, VMEM, ANY], [VMEM, ANY, VMEM, VMEM, VMEM, VMEM],
        pair_scratch(rows) + [dma(24), dma(24), dma(2)], 4, 56,
    )(near, far, hid, gains, out_grad, live)


def back_kernel(
    n_dp, n_mp, near, far, hid, att, gains, out_grad, live, grads,
    ghid, dg1, dg2, seq, sums, squares,
    r1, s2, r2, s3, r3, own, yr, zs, zr, total, ss, rs, ls,
):
    net = Net(n_dp, n_mp, ss, rs, ls)
    nj = n_dp // 2
    net.meet(pair_partners(net, True))
    rows = hid.shape[0]
    wrows, width = yr.shape[2], yr.shape[3]
    ks = (2, 0, 1)
    turns = list(range(1, nj)) + [0]
    moves, ys = {}, {}

    def y_start(k):
        for d in turns:
            at = (net.j + d) % nj
            ys[k, d] = net.send(grads.at[k, at, 1 - net.y], yr.at[k, d], net.y_n)
            moves[k, d] = net.move(grads.at[k, at, net.y], zs.at[k, d])

    z_flight = {}

    def z_step(k, d):
        ys[k, d].wait_recv()
        moves[k, d].wait()

        def add(at, state):
            zs[k, d, at] = (zs[k, d, at].astype(F32) + yr[k, d, at].astype(F32)).astype(BF)
            return state

        lax.fori_loop(
            0, wrows // 8,
            lambda t, state: add(pl.ds(pl.multiple_of(t * 8, 8), 8), state), 0,
        ) if wrows % 16 else lax.fori_loop(
            0, wrows // 16,
            lambda t, state: add(pl.ds(pl.multiple_of(t * 16, 16), 16), state), 0,
        )
        if d:
            z_flight[k, d] = net.send(zs.at[k, d], zr.at[k, d - 1], net.z_at(d))

    z = None
    cores = None
    y_start(2)
    z = reduce_pair_steps(net, near, far, r1, s2, r2, s3, r3, rows)
    y_start(0)
    y_start(1)
    z.wait_recv()
    g1, g2 = 1.0 + gains[1:2], 1.0 + gains[2:3]

    def last(at, state):
        grad = near[0, at] + r1[0, at].astype(F32) + r2[0, at].astype(F32) + r3[at].astype(F32)
        part, d2 = rms_back_rows(hid[at], g2, grad)
        grad_hidden = out_grad[at] * live[at] + part
        ghid[at] = grad_hidden
        grad_att, d1 = rms_back_rows(att[at], g1, grad_hidden)
        own[at] = grad_att.astype(BF)
        return state[0] + d1, state[1] + d2

    zero = jnp.zeros((1, D), F32)
    done1, done2 = by_rows(rows, last, (zero, zero))
    dg1[...] = done1
    dg2[...] = done2
    finish = gather_seq_steps(net, own, seq)
    for d in turns:
        z_step(2, d)
    finish()
    for k in (0, 1):
        for d in turns:
            z_step(k, d)

    square = jnp.zeros((8, width), F32)
    writes = []
    step = 16 if wrows % 16 == 0 else 8
    for turn_at, k in enumerate(ks):
        for d in range(1, nj):
            z_flight[k, d].wait_recv()
        slot = turn_at % 2
        if len(writes) >= 2:
            for w in writes[len(writes) - 2]:
                w.wait()

        def collect(t, state, k=k, slot=slot):
            at = pl.ds(pl.multiple_of(t * step, step), step)
            halves = [zs[k, 0, at].astype(F32), jnp.zeros((step, width), F32)]
            for d in range(1, nj):
                halves[d % 2] = halves[d % 2] + zr[k, d - 1, at].astype(F32)
            for parity in range(2):
                total[slot, parity, at] = halves[parity]
                sq = halves[parity] * halves[parity]
                for r in range(step // 8):
                    state = state + sq[r * 8 : r * 8 + 8]
            return state

        square = lax.fori_loop(0, wrows // step, collect, square)
        pair = []
        for parity in range(2):
            half = (net.zl + parity) % 2
            pair.append(
                net.move(total.at[slot, parity], sums.at[k, :, pl.ds(pl.multiple_of(half * width, width), width)])
            )
        writes.append(pair)
    for pair in writes[len(writes) - 2 :]:
        for w in pair:
            w.wait()
    squares[...] = square
    net.close()


def back(n_dp, n_mp, near, far, hid, att, gains, out_grad, live, grads):
    rows = hid.shape[0]
    block = (rows, D)
    nj = n_dp // 2
    _, _, _, wrows, width = grads.shape
    count = 24 + 6 * nj
    return call(
        functools.partial(back_kernel, n_dp, n_mp),
        [
            jax.ShapeDtypeStruct(block, F32), jax.ShapeDtypeStruct((1, D), F32), jax.ShapeDtypeStruct((1, D), F32),
            jax.ShapeDtypeStruct((4,) + block, BF), jax.ShapeDtypeStruct((3, wrows, 2 * width), F32),
            jax.ShapeDtypeStruct((8, width), F32),
        ],
        [VMEM, VMEM, VMEM, ANY, ANY, VMEM], [VMEM, ANY, VMEM, VMEM, VMEM, VMEM, VMEM, ANY],
        pair_scratch(rows)
        + [
            pltpu.VMEM((3, nj, wrows, width), BF), pltpu.VMEM((3, nj, wrows, width), BF),
            pltpu.VMEM((3, nj - 1, wrows, width), BF),
            pltpu.VMEM((2, 2, wrows, width), F32), dma(count), dma(count), dma(8 + 3 * nj),
        ],
        5, 60,
    )(near, far, hid, att, gains, out_grad, live, grads)


def tail_kernel(
    n_dp, n_mp, near, far, inputs, gains, ghid, gq, gkv, go, gin, dg0, sq_, skv, so,
    r1, s2, r2, tq, tkv, to, rq, rkv, roa, rob, bq, bkv, boa, bob, ss, rs, ls,
):
    net = Net(n_dp, n_mp, ss, rs, ls)
    p = net.place()
    right = (net.ring(p + 1), net.m)
    left = (net.ring(p + n_dp - 1), net.m)
    net.meet([right, left, net.x_n, net.core_n])
    rows = inputs.shape[0]
    wrows = go.shape[1]
    hr = upper(wrows)
    top, low = pl.ds(0, hr), pl.ds(hr, wrows - hr)

    def ready(offset):
        return net.ring(p + 2 * n_dp + offset)

    oa = net.send(go.at[ready(-1), top], roa.at[0], right)
    ob = net.send(go.at[ready(1), low], rob.at[0], left)
    a = net.send(gq.at[ready(-1)], rq.at[0], right)
    b = net.send(gkv.at[ready(1)], rkv.at[0], left)
    loads = [net.move(go, to), net.move(gq, tq), net.move(gkv, tkv)]
    c1 = net.send(far.at[1], r1.at[1], net.core_n)
    c0 = net.send(far.at[0], r1.at[0], net.core_n)
    c1.wait_recv()

    def first(at, state):
        s2[at] = (near[1, at] + r1[1, at].astype(F32)).astype(BF)
        return state

    by_rows(rows, first)
    x = net.send(s2, r2, net.x_n)
    for load in loads:
        load.wait()

    def hop_add(dst, got, term, count, dtype):
        step = 16 if count % 16 == 0 else (8 if count % 8 == 0 else count)

        def add(t, state):
            at = pl.ds(pl.multiple_of(t * step, step), step)
            dst[at] = (got[at].astype(F32) + term[at].astype(F32)).astype(dtype)
            return state

        lax.fori_loop(0, count // step, add, 0)

    def finish_rows():
        c0.wait_recv()
        x.wait_recv()
        g0 = 1.0 + gains[0:1]

        def second(at, state):
            grad = near[0, at] + r1[0, at].astype(F32) + r2[at].astype(F32)
            part, d0 = rms_back_rows(inputs[at], g0, grad)
            gin[at] = ghid[at] + part
            return state + d0

        dg0[...] = by_rows(rows, second, jnp.zeros((1, D), F32))

    for hop in range(1, n_dp):
        end = hop == n_dp - 1
        at_right, at_left = ready(-1 - hop), ready(1 + hop)
        oa.wait_recv()
        hop_add(so.at[top] if end else boa.at[hop - 1], roa.at[hop - 1], to.at[at_right, top], hr, F32 if end else BF)
        if not end:
            oa = net.send(boa.at[hop - 1], roa.at[hop], right)
        ob.wait_recv()
        hop_add(so.at[low] if end else bob.at[hop - 1], rob.at[hop - 1], to.at[at_left, low], wrows - hr, F32 if end else BF)
        if not end:
            ob = net.send(bob.at[hop - 1], rob.at[hop], left)
        a.wait_recv()
        hop_add(sq_ if end else bq.at[hop - 1], rq.at[hop - 1], tq.at[at_right], wrows, F32 if end else BF)
        if not end:
            a = net.send(bq.at[hop - 1], rq.at[hop], right)
        b.wait_recv()
        hop_add(skv if end else bkv.at[hop - 1], rkv.at[hop - 1], tkv.at[at_left], wrows, F32 if end else BF)
        if not end:
            b = net.send(bkv.at[hop - 1], rkv.at[hop], left)
        if hop == (n_dp * 5) // 8:
            finish_rows()
    net.close()


def tail(n_dp, n_mp, near, far, inputs, gains, ghid, gq, gkv, go):
    rows = inputs.shape[0]
    block = (rows, D)
    _, wrows, width = gq.shape
    full, half, rest = (wrows, width), (upper(wrows), width), (wrows - upper(wrows), width)
    hops = n_dp - 1
    count = 4 * n_dp + 8
    many = lambda n, shape: pltpu.VMEM((n,) + shape, BF)
    return call(
        functools.partial(tail_kernel, n_dp, n_mp),
        [
            jax.ShapeDtypeStruct(block, F32), jax.ShapeDtypeStruct((1, D), F32),
            jax.ShapeDtypeStruct(full, F32), jax.ShapeDtypeStruct(full, F32), jax.ShapeDtypeStruct(full, F32),
        ],
        [VMEM] * 5, [VMEM, ANY, VMEM, VMEM, VMEM, ANY, ANY, ANY],
        [
            many(2, block), pltpu.VMEM(block, BF), pltpu.VMEM(block, BF),
            many(n_dp, full), many(n_dp, full), many(n_dp, full),
            many(hops, full), many(hops, full), many(hops, half), many(hops, rest),
            many(hops, full), many(hops, full), many(hops, half), many(hops, rest),
            dma(count), dma(count), dma(8),
        ],
        6, 60,
    )(near, far, inputs, gains, ghid, gq, gkv, go)


def finish_kernel(n_dp, n_mp, terms, square, total_gain, total_square, got, sgot, mine, ss, rs, ls):
    net = Net(n_dp, n_mp, ss, rs, ls)
    others = everyone(n_dp, n_mp, net.i, net.m)
    net.meet(others)
    flat = net.i * n_mp + net.m
    copies = [
        net.send(terms.at[dp * n_mp + mp], got.at[flat], (dp, mp)) for dp, mp in others
    ]
    net.keep(terms.at[flat], got.at[flat])
    net.open.pop()()
    for copy in copies:
        copy.wait_recv()
    total = lax.fori_loop(0, n_dp * n_mp, lambda t, s: s + got[t], jnp.zeros(got.shape[1:], F32))
    total_gain[...] = total
    mine[...] = square[...] + jnp.sum(total * total) * (1.0 / (mine.shape[0] * mine.shape[1]))
    copies = [net.send(mine, sgot.at[flat], device) for device in others]
    net.keep(mine, sgot.at[flat])
    net.open.pop()()
    for copy in copies:
        copy.wait_recv()
    total_square[...] = lax.fori_loop(0, n_dp * n_mp, lambda t, s: s + sgot[t], jnp.zeros(mine.shape, F32))
    net.close()


def finish_all(n_dp, n_mp, terms, square):
    total = n_dp * n_mp
    shape = terms.shape[1:]
    return call(
        functools.partial(finish_kernel, n_dp, n_mp),
        [jax.ShapeDtypeStruct(shape, F32), jax.ShapeDtypeStruct(square.shape, F32)],
        [VMEM, VMEM], [VMEM, VMEM],
        [
            pltpu.VMEM((total,) + shape, F32), pltpu.VMEM((total,) + square.shape, F32),
            pltpu.VMEM(square.shape, F32), dma(2 * total), dma(2 * total), dma(2),
        ],
        7, 16,
    )(terms, square)


def build_local(n_dp, n_mp):
    nj = n_dp // 2

    def local(
        inputs, out_grad, segment_ids, pad_mask, bit_sel, w_qo, w_kv, w_mlp, norm_gains,
        m_qo, m_kv, m_mlp, m_gains, v_qo, v_kv, v_mlp, v_gains,
    ):
        m = lax.axis_index("mp")
        rows = inputs.shape[0]
        seq_len = segment_ids.shape[1]
        wrows = w_qo.shape[1]

        gain_rows = spread(n_dp, n_mp, norm_gains.reshape(1, -1)).reshape(NORMS, D)
        low_q = quantize(w_qo[0], D, bit_sel[0])
        low_o = quantize(w_qo[1], QW, bit_sel[0])
        low_kv = jnp.concatenate([quantize(w_kv[0], D, bit_sel[1]), quantize(w_kv[1], D, bit_sel[1])], 1)
        steps = jnp.array([1.0 / (32.0 * math.sqrt(fan)) for fan in (D, D, FF)], F32).reshape(3, 1, 1)
        low_mlp = quantize_by(w_mlp, steps, bit_sel[2])
        norm_in = rms_norm(inputs, gain_rows[0]).astype(BF)
        wq, wkv, wo, seq_normed = head(n_dp, n_mp, low_q, low_kv, low_o, norm_in)
        wq = wq.reshape(D, -1)
        wkv = wkv.reshape(D, -1)
        wo = wo.reshape(D, -1)
        seq_normed = seq_normed.reshape(seq_len, D)

        order = jnp.stack([m, m ^ 2, m ^ 1, m ^ 3])

        def in_order(vector):
            return vector.reshape(n_mp, rows)[order].reshape(-1)

        segments = segment_ids[0]
        positions = in_order(doc_positions(segments))
        slots = in_order(jnp.arange(seq_len, dtype=jnp.int32))
        segs = in_order(segments)
        pads = in_order(pad_mask[0])
        allowed = (
            (segs[:, None] == segs[None, :])
            & (slots[None, :] <= slots[:, None])
            & ((pads[None, :] == 1) | (slots[None, :] == slots[:, None]))
        )
        local_heads = wq.shape[1] // HEAD_WIDTH
        kv_heads = wkv.shape[1] // 2 // HEAD_WIDTH
        kv_cols = kv_heads * HEAD_WIDTH
        group = local_heads // kv_heads
        scale = HEAD_WIDTH ** (-0.5)
        half_dim = HEAD_WIDTH // 2
        frequency = ROPE_BASE ** (-jnp.arange(half_dim, dtype=F32) * 2.0 / HEAD_WIDTH)
        angles = positions.astype(F32)[:, None] * frequency[None, :]
        angles = jnp.concatenate([angles, angles], -1)
        cosine = jnp.cos(angles)[:, None, :]
        sine = jnp.sin(angles)[:, None, :]

        query_linear = mm(seq_normed, wq).reshape(seq_len, local_heads, HEAD_WIDTH)
        kv_linear = mm(seq_normed, wkv)
        key_linear = kv_linear[:, :kv_cols].reshape(seq_len, kv_heads, HEAD_WIDTH)
        value_bf = kv_linear[:, kv_cols:].astype(BF).reshape(seq_len, kv_heads, HEAD_WIDTH)
        query_bf = rotate(query_linear, cosine, sine).astype(BF).reshape(
            seq_len, kv_heads, group, HEAD_WIDTH
        )
        key_bf = rotate(key_linear, cosine, sine).astype(BF)

        def masked_scores():
            raw = (
                jnp.einsum("qkgd,pkd->kgqp", query_bf, key_bf, preferred_element_type=F32) * scale
            )
            bent = jnp.tanh(raw / SOFT_CAP)
            return bent, jnp.where(allowed[None, None], SOFT_CAP * bent, MASKED_SCORE)

        _, capped = masked_scores()
        row_top = jnp.max(capped, axis=-1, keepdims=True)
        log_total = row_top + jnp.log(jnp.sum(jnp.exp(capped - row_top), axis=-1, keepdims=True))
        probs_bf = jnp.exp(capped - log_total).astype(BF)
        mixed_bf = (
            jnp.einsum("kgqp,pkd->qkgd", probs_bf, value_bf, preferred_element_type=F32)
            .reshape(seq_len, -1)
            .astype(BF)
        )
        half_seq = seq_len // 2

        def parts_of(near, far):
            return near.reshape(-1, rows, D), far.astype(BF).reshape(-1, rows, D)

        near, far = parts_of(mm_cols(mixed_bf[:half_seq], wo), mm_cols(mixed_bf[half_seq:], wo))
        attended, hidden_in, group_ffn, w_full = mid(n_dp, n_mp, near, far, inputs, gain_rows, low_mlp)
        w_full = w_full.reshape(3, D, -1)
        group_ffn = group_ffn.reshape(8 * rows, D)
        half_tok = 4 * rows
        gate = mm(group_ffn, w_full[0])
        up = mm(group_ffn, w_full[1])
        activated_bf = (jax.nn.gelu(gate, approximate=True) * up).astype(BF)
        near, far = parts_of(
            mm_cols(activated_bf[:half_tok], w_full[2]), mm_cols(activated_bf[half_tok:], w_full[2])
        )
        live = lax.dynamic_slice_in_dim(pad_mask[0], m * rows, rows).astype(F32)[:, None]
        outputs, grad_gain_three, group_grad = turn(
            n_dp, n_mp, near, far, hidden_in, gain_rows, out_grad, live
        )
        group_grad = group_grad.reshape(8 * rows, D)
        grad_act = mm(group_grad, w_full[2])
        grad_down = mm_rows(group_grad, activated_bf)
        _, act_pull = jax.vjp(lambda a, b: jax.nn.gelu(a, approximate=True) * b, gate, up)
        grad_gate, grad_up = act_pull(grad_act)
        grad_gate = grad_gate.astype(BF)
        grad_up = grad_up.astype(BF)
        near, far = parts_of(
            mm_cols(grad_gate[:half_tok], w_full[0]) + mm_cols(grad_up[:half_tok], w_full[1]),
            mm_cols(grad_gate[half_tok:], w_full[0]) + mm_cols(grad_up[half_tok:], w_full[1]),
        )
        grads = jnp.stack(
            [mm_rows(group_ffn, grad_gate).astype(BF), mm_rows(group_ffn, grad_up).astype(BF), grad_down.astype(BF)]
        ).reshape(3, nj, 2, wrows, -1)
        grad_hidden, grad_gain_one, grad_gain_two, seq_grad, sum_mlp, square_mlp = back(
            n_dp, n_mp, near, far, hidden_in, attended, gain_rows, out_grad, live, grads
        )
        seq_grad = seq_grad.reshape(seq_len, D)
        grad_mixed = mm(seq_grad, wo).astype(BF).reshape(seq_len, kv_heads, group, HEAD_WIDTH)
        grad_out_w = mm_rows(seq_grad, mixed_bf).astype(BF).reshape(n_dp, wrows, -1)

        bent, capped = masked_scores()
        probs = jnp.exp(capped - log_total)
        probs_bf = probs.astype(BF)
        grad_value = jnp.einsum("kgqp,qkgd->pkd", probs_bf, grad_mixed, preferred_element_type=F32)
        grad_probs = jnp.einsum("qkgd,pkd->kgqp", grad_mixed, value_bf, preferred_element_type=F32)
        inner_sum = jnp.sum(probs * grad_probs, axis=-1, keepdims=True)
        grad_raw = (probs * (grad_probs - inner_sum) * (1.0 - bent * bent)).astype(BF)
        grad_query = (
            jnp.einsum("kgqp,pkd->qkgd", grad_raw, key_bf, preferred_element_type=F32) * scale
        ).reshape(seq_len, local_heads, HEAD_WIDTH)
        grad_key = (
            jnp.einsum("kgqp,qkgd->pkd", grad_raw, query_bf, preferred_element_type=F32) * scale
        )
        grad_q = rotate_back(grad_query, cosine, sine).reshape(seq_len, -1).astype(BF)
        grad_kv = jnp.concatenate(
            [
                rotate_back(grad_key, cosine, sine).reshape(seq_len, -1).astype(BF),
                grad_value.reshape(seq_len, -1).astype(BF),
            ],
            1,
        )
        near, far = parts_of(
            mm_cols(grad_q[:half_seq], wq) + mm_cols(grad_kv[:half_seq], wkv),
            mm_cols(grad_q[half_seq:], wq) + mm_cols(grad_kv[half_seq:], wkv),
        )
        gq = mm_rows(seq_normed, grad_q).astype(BF).reshape(n_dp, wrows, -1)
        gkv = mm_rows(seq_normed, grad_kv).astype(BF).reshape(n_dp, wrows, -1)
        grad_in, grad_gain_zero, sum_q, sum_kv, sum_o = tail(
            n_dp, n_mp, near, far, inputs, gain_rows, grad_hidden, gq, gkv, grad_out_w
        )
        terms = jnp.concatenate([grad_gain_zero, grad_gain_one, grad_gain_two, grad_gain_three])
        square = jnp.sum(square_mlp)
        for part in (sum_q, sum_kv, sum_o):
            square = square + jnp.sum(part * part)
        square = jnp.broadcast_to(square * (1.0 / 1024.0), (8, 128))
        sum_gains, squares = finish_all(n_dp, n_mp, terms.reshape(n_dp * n_mp, 1, -1), square)
        grad_norm = jnp.sqrt(jnp.sum(squares)).reshape(1)
        factor = jnp.minimum(1.0, CLIP_SCALE * math.sqrt(PARAMS) / grad_norm[0])

        new_w_qo, new_m_qo, new_v_qo = adam_update(w_qo, m_qo, v_qo, jnp.stack([sum_q, sum_o]), factor)
        new_w_kv, new_m_kv, new_v_kv = adam_update(
            w_kv, m_kv, v_kv, jnp.stack([sum_kv[:, :kv_cols], sum_kv[:, kv_cols:]]), factor
        )
        new_w_mlp, new_m_mlp, new_v_mlp = adam_update(w_mlp, m_mlp, v_mlp, sum_mlp, factor)
        new_gains, new_m_gains, new_v_gains = adam_update(
            norm_gains, m_gains, v_gains, sum_gains.reshape(-1), factor
        )
        return (
            outputs, grad_in, grad_norm, new_w_qo, new_w_kv, new_w_mlp, new_gains,
            new_m_qo, new_m_kv, new_m_mlp, new_m_gains, new_v_qo, new_v_kv, new_v_mlp, new_v_gains,
        )

    return local


def solution(mesh):
    tokens = P(("dp", "mp"), None)
    weight = P(None, "dp", "mp")
    flat = P(("dp", "mp"))
    per_weight = (weight, weight, weight, flat)
    return jax.shard_map(
        build_local(mesh.shape["dp"], mesh.shape["mp"]),
        mesh=mesh,
        in_specs=(tokens, tokens, P("dp", None), P("dp", None), P()) + per_weight * 3,
        out_specs=(tokens, tokens, P()) + per_weight * 3,
        check_vma=False,
    )
```

time: 2200 us -> 1120 us (0.51)
  waiting for transfers between devices: 1580 us -> 0 us
  Pallas kernels: 0 us -> 778 us
  other arithmetic: 223 us -> 71.2 us
  blocking collectives: 128 us -> 0 us
    reduce_scatter x7 -> x0, waiting for transfers between devices: 818 us -> none  [the longest x1 470 us: local(): lax.psum_scatter(jnp.concatenate([grad_gate_up_w, grad_down[None]], 0).as...]
    pallas_call x0 -> x7, Pallas kernels: none -> 778 us  [the longest x1 241 us: mid(): call(functools.partial(mid_kernel, n_dp, n_mp), [jax.ShapeDtypeStruct(blo...]
    all_gather x7 -> x0, waiting for transfers between devices: 757 us -> none  [the longest x1 606 us: local(): lax.all_gather(low_mlp, 'dp', axis=1, tiled=True)]
    convert_element_type x13 -> x11, other arithmetic: 131 us -> 16.3 us  [the longest x3 7.85 us: quantize_by(): return (sliced * spacing * step).astype(BF)]
    unnamed x2 -> x0, blocking collectives: 88.2 us -> none
    psum x1 -> x0, blocking collectives: 39.5 us -> none  [local(): grad_norm = jnp.sqrt(lax.psum(local_squares, ('dp', 'mp')))]
    dot_general x22 -> x28, matrix products: 208 us -> 208 us  [the longest x12 72.2 us: mm_cols(): lax.dot_general(left, right, (((1,), (1,)), ((), ())), preferred_element_...]
  transfers between devices with their start and end apart: 14 -> 0, of which waited for: 11 -> 0; matrix products, arithmetic and copies ran while one was open for 10% -> 0% of each run, Pallas kernels for 0% -> 0%
where the time goes in v1:
time: 1120 us; the launch traced here: 1110 us
  Pallas kernels  778 us (69%)
  matrix products  216 us (19%)
  other arithmetic  71.2 us (6%)
  local copies, waits for them, and re-layouts  36.5 us (3%)
    pallas_call x1, Pallas kernels, mid(): call(functools.partial(mid_kernel, n_dp, n_mp), [jax.ShapeDtypeStruct(blo...  241 us
    pallas_call x1, Pallas kernels, back(): call(functools.partial(back_kernel, n_dp, n_mp), [jax.ShapeDtypeStruct(bl...  226 us
    pallas_call x1, Pallas kernels, turn(): call(functools.partial(turn_kernel, n_dp, n_mp), [jax.ShapeDtypeStruct(bl...  110 us
    pallas_call x1, Pallas kernels, tail(): call(functools.partial(tail_kernel, n_dp, n_mp), [jax.ShapeDtypeStruct(bl...  88.5 us
    pallas_call x1, Pallas kernels, head(): call(functools.partial(head_kernel, n_dp, n_mp), [full(q), full(kv), full...  87.9 us
    dot_general x12, matrix products, mm_cols(): lax.dot_general(left, right, (((1,), (1,)), ((), ())), preferred_element_...  72.2 us
    dot_general x6, matrix products, mm(): lax.dot_general(left, right, (((1,), (0,)), ((), ())), preferred_element_...  71.1 us
    dot_general x6, matrix products, mm_rows(): lax.dot_general(left, right, (((0,), (0,)), ((), ())), preferred_element_...  55.2 us

profile of v1, /device:TPU:0, one launch (start us, length us, event | category | flops | bytes accessed | tf_op | source)
XLA Modules:
  0.0 1112.6 jit_solution(14637483493531895938)
XLA Ops:
  17.0 10.2 shard_map.289
  35.2 4.4 fusion.17.low
  39.6 87.9 %shard_map.290 = (bf16[8,288,512]{2,1,0:T(8,128)(2,1)S(1)}, bf16[8,288,512]{2,1,0:T(8,128)(2,1)S(1)}, bf16[8,288,512]{2,1,0:T(8,128)(2,1)S(1)}, bf16[4,224,2304]{2,1,0:T(8,128)(2,1)S(1)}) custom-call(bf16[288,512]{1,0:T(8,128)(2,1)S(1)} %get-tuple-element.87.q, bf16[288,512]{1,0:T(8,128)(2,1)S(1)} %pad_maximum_fusion.6.kv, ...), custom_call_target="tpu_custom_call" | custom-call | tf_op jit(solution)/shard_map/pallas_call | solution.py:283
  131.8 4.6 fusion.58
  138.9 5.6 fusion.109
  154.6 3.9 convolution_convert_fusion.7
  162.1 240.7 %shard_map.291 = (f32[224,2304]{1,0:T(8,128)S(1)}, f32[224,2304]{1,0:T(8,128)S(1)}, bf16[8,224,2304]{2,1,0:T(8,128)(2,1)}, bf16[3,8,288,1152]{3,2,1,0:T(8,128)(2,1)}) custom-call(f32[2,224,2304]{2,1,0:T(8,128)} %fusion.76.near, bf16[2,224,2304]{2,1,0:T(8,128)(2,1)} %bitcast.287, f32[224,2304]{1,0:T(8,128)} %inputs.3, f32[4,2304]{1,0:T(4,128)S(1)} %reshape.793.gains, ...), custom_call_target="tpu_custom_call" | custom-call | tf_op jit(solution)/shard_map/pallas_call | solution.py:390
  402.9 10.3 fusion.103
  415.6 14.9 %fusion.110 = f32[1792,1152]{1,0:T(8,128)} fusion(bf16[1792,2304]{1,0:T(8,128)(2,1)} %bitcast.292, bf16[2304,1152]{1,0:T(8,128)(2,1)S(1)} %bitcast.265), kind=kOutput, calls=%fused_computation.189 | convolution fusion | flops 9512681472 | bytes 21823488 | tf_op jit(solution)/shard_map/dot_general | solution.py:86
  430.5 18.1 %multiply_convert_fusion.1 = (bf16[1792,1152]{1,0:T(8,128)(2,1)}, f32[1792,1152]{1,0:T(8,128)}) fusion(f32[1792,1152]{1,0:T(8,128)} %fusion.110, bf16[1792,2304]{1,0:T(8,128)(2,1)} %bitcast.293, bf16[2304,1152]{1,0:T(8,128)(2,1)S(1)} %bitcast.262), kind=kOutput, calls=%fused_computation.20 | convolution fusion | flops 9533325312 | bytes 34209792 | tf_op jit(solution)/shard_map/dot_general | solution.py:86
  450.3 8.8 convolution_convert_fusion.3
  459.2 7.8 fusion.111.near
  467.0 109.5 %shard_map.292 = (f32[224,2304]{1,0:T(8,128)}, f32[1,2304]{1,0:T(1,128)}, bf16[8,224,2304]{2,1,0:T(8,128)(2,1)}) custom-call(f32[4,224,2304]{2,1,0:T(8,128)} %fusion.111.near, bf16[4,224,2304]{2,1,0:T(8,128)(2,1)} %bitcast.279, f32[224,2304]{1,0:T(8,128)} %copy-done.4, f32[4,2304]{1,0:T(4,128)} %copy-done.9, f32[224,2304]{1,0:T(8,128)} %out_grad.3, ...), custom_call_target="tpu_custom_call" | custom-call | tf_op jit(solution)/shard_map/pallas_call | solution.py:473
  576.5 24.9 %multiply_convert_fusion = (bf16[1792,1152]{1,0:T(8,128)(2,1)}, bf16[1792,1152]{1,0:T(8,128)(2,1)}) fusion(f32[1792,1152]{1,0:T(8,128)} %fusion.110, f32[1792,1152]{1,0:T(8,128)} %get-tuple-element.109, bf16[1792,2304]{1,0:T(8,128)(2,1)} %bitcast.296, bf16[2304,1152]{1,0:T(8,128)(2,1)} %bitcast.270), kind=kOutput, calls=%fused_computation.19 | convolution fusion | flops 9562226688 | bytes 38338560 | tf_op jit(solution)/shard_map/dot_general | solution.py:86
  601.4 14.6 %convolution_convert_fusion = bf16[2304,1152]{1,0:T(8,128)(2,1)S(1)} fusion(bf16[1792,2304]{1,0:T(8,128)(2,1)} %bitcast.297, bf16[1792,1152]{1,0:T(8,128)(2,1)} %get-tuple-element.108), kind=kOutput, calls=%fused_computation.8 | convolution fusion | flops 9515335680 | bytes 17694720 | tf_op jit(solution)/shard_map/dot_general | solution.py:90
  616.0 13.8 %convolution_convert_fusion.1 = bf16[2304,1152]{1,0:T(8,128)(2,1)S(1)} fusion(bf16[1792,2304]{1,0:T(8,128)(2,1)} %bitcast.294, bf16[1792,1152]{1,0:T(8,128)(2,1)S(1)} %copy-done.49), kind=kOutput, calls=%fused_computation.9 | convolution fusion | flops 9515335680 | bytes 17694720 | tf_op jit(solution)/shard_map/dot_general | solution.py:90
  629.8 14.5 %convolution_convert_fusion.2 = bf16[2304,1152]{1,0:T(8,128)(2,1)S(1)} fusion(bf16[1792,2304]{1,0:T(8,128)(2,1)} %bitcast.295, bf16[1792,1152]{1,0:T(8,128)(2,1)} %get-tuple-element.76), kind=kOutput, calls=%fused_computation.10 | convolution fusion | flops 9515335680 | bytes 17694720 | tf_op jit(solution)/shard_map/dot_general | solution.py:90
  644.3 7.1 pad_maximum_fusion.grads
  651.5 9.4 fusion.30
  660.8 9.4 add_convert_fusion
  670.2 9.2 fusion.33
  679.4 10.4 convolution_add_fusion
  689.7 225.6 %shard_map.293 = (f32[224,2304]{1,0:T(8,128)}, f32[1,2304]{1,0:T(1,128)}, f32[1,2304]{1,0:T(1,128)}, bf16[4,224,2304]{2,1,0:T(8,128)(2,1)}, f32[3,288,2304]{2,1,0:T(8,128)}, /*index=5*/f32[8,1152]{1,0:T(8,128)}) custom-call(f32[4,224,2304]{2,1,0:T(8,128)} %bitcast.260, bf16[4,224,2304]{2,1,0:T(8,128)(2,1)} %bitcast.278, f32[224,2304]{1,0:T(8,128)} %copy-done.4, ...), custom_call_target="tpu_custom_call" | custom-call | tf_op jit(solution)/shard_map/pallas_call | solution.py:595
  916.7 4.9 convolution_convert_fusion.9
  921.7 4.1 convolution_convert_fusion.4
  925.9 5.5 fusion.55
  948.2 3.9 convolution_convert_fusion.6
  952.1 4.3 convolution_convert_fusion.5
  966.3 88.5 %shard_map.294 = (f32[224,2304]{1,0:T(8,128)}, f32[1,2304]{1,0:T(1,128)}, f32[288,512]{1,0:T(8,128)}, f32[288,512]{1,0:T(8,128)}, f32[288,512]{1,0:T(8,128)}) custom-call(f32[2,224,2304]{2,1,0:T(8,128)} %bitcast.257, bf16[2,224,2304]{2,1,0:T(8,128)(2,1)} %bitcast.261, f32[224,2304]{1,0:T(8,128)} %inputs.3, f32[4,2304]{1,0:T(4,128)} %copy-done.9, ...), custom_call_target="tpu_custom_call" | custom-call | tf_op jit(solution)/shard_map/pallas_call | solution.py:703
  1064.2 15.2 %shard_map.295 = (f32[1,288]{1,0:T(1,128)S(1)}, f32[8,128]{1,0:T(8,128)S(1)}) custom-call(f32[32,1,288]{2,1,0:T(1,128)S(1)} %reshape.809.terms, f32[8,128]{1,0:T(8,128)S(1)} %broadcast_in_dim.25.square), custom_call_target="tpu_custom_call" | custom-call | tf_op jit(solution)/shard_map/pallas_call | solution.py:748
  1084.2 4.0 multiply_subtract_fusion.1
  1088.2 19.4 %multiply_subtract_fusion = (f32[3,288,2304]{2,1,0:T(8,128)}, f32[3,288,2304]{2,1,0:T(8,128)}, f32[3,288,2304]{2,1,0:T(8,128)}) fusion(f32[3,288,2304]{2,1,0:T(8,128)} %param.25, f32[3,288,2304]{2,1,0:T(8,128)} %get-tuple-element.61, f32[]{:T(128)S(6)} %min.95, f32[3,288,2304]{2,1,0:T(8,128)} %param.33, f32[3,288,2304]{2,1,0:T(8,128)} %param.29), kind=kLoop, calls=%fused_computation.33 | loop fusion | flops 27869184 | bytes 55738372 | tf_op jit(solution)/shard_map/sub | solution.py:101
  (201 shorter events, 86.1 us)
Async XLA Ops:
  0.6 34.3 %copy-start.12 = (f32[224,2304]{1,0:T(8,128)S(1)}, f32[224,2304]{1,0:T(8,128)}, u32[]{:S(2)}) copy-start(f32[224,2304]{1,0:T(8,128)} %inputs.3) | copy-start | bytes 6193156
  3.5 31.7 %copy-start.46 = (f32[3]{0:T(128)S(1)}, f32[3]{0:T(128)}, u32[]{:S(2)}) copy-start(f32[3]{0:T(128)} %constant.160) | copy-start | bytes 40
  3.5 31.7 %copy-start.47 = (f32[3]{0:T(128)S(1)}, f32[3]{0:T(128)}, u32[]{:S(2)}) copy-start(f32[3]{0:T(128)} %constant.157.clone) | copy-start | bytes 40
  27.5 134.6 %copy-start.9 = (f32[4,2304]{1,0:T(4,128)}, f32[4,2304]{1,0:T(4,128)S(1)}, u32[]{:S(2)}) copy-start(f32[4,2304]{1,0:T(4,128)S(1)} %reshape.793.gains) | copy-start | bytes 110596
  28.4 6.8 copy-start.13
  128.9 7.5 copy-start
  136.4 8.2 copy-start.15
  138.9 5.8 copy-start.17
  402.9 10.4 copy-start.4
  402.9 10.3 copy-start.8
  415.6 34.7 %slice-start.4 = ((s8[5308416]{0:T(1024)(128)(4,1)}), s8[4194304]{0:T(1024)(128)(4,1)S(1)}, s32[]{:S(2)}) async-start(s8[5308416]{0:T(1024)(128)(4,1)} %bitcast.271), calls=%async_computation.4 | async-start | bytes 8388608
  430.5 19.8 %slice-start.5 = ((s8[5308416]{0:T(1024)(128)(4,1)}), s8[1114112]{0:T(1024)(128)(4,1)S(1)}, s32[]{:S(2)}) async-start(s8[5308416]{0:T(1024)(128)(4,1)} %bitcast.271), calls=%async_computation.5 | async-start | bytes 2228224
  601.4 14.6 %copy-start.49 = (bf16[1792,1152]{1,0:T(8,128)(2,1)S(1)}, bf16[1792,1152]{1,0:T(8,128)(2,1)}, u32[]{:S(2)}) copy-start(bf16[1792,1152]{1,0:T(8,128)(2,1)} %get-tuple-element.75) | copy-start | bytes 12386308
  616.0 35.4 %slice-start.2 = ((s8[5308416]{0:T(1024)(128)(4,1)}), s8[4194304]{0:T(1024)(128)(4,1)S(1)}, s32[]{:S(2)}) async-start(s8[5308416]{0:T(1024)(128)(4,1)} %bitcast.266), calls=%async_computation.2 | async-start | bytes 8388608
  629.8 21.6 %slice-start.3 = ((s8[5308416]{0:T(1024)(128)(4,1)}), s8[1114112]{0:T(1024)(128)(4,1)S(1)}, s32[]{:S(2)}) async-start(s8[5308416]{0:T(1024)(128)(4,1)} %bitcast.266), calls=%async_computation.3 | async-start | bytes 2228224
  651.5 9.4 copy-start.50
  689.7 226.9 %copy-start.7 = (bf16[8,288,512]{2,1,0:T(8,128)(2,1)S(1)}, bf16[8,288,512]{2,1,0:T(8,128)(2,1)}, u32[]{:S(2)}) copy-start(bf16[8,288,512]{2,1,0:T(8,128)(2,1)} %copy-done.5) | copy-start | bytes 7077892
  916.7 5.0 copy-start.48
  921.7 9.8 slice-start
  925.9 5.6 slice-start.1
  925.9 5.6 copy-start.35
  966.3 97.0 %copy-start.40 = (f32[1,2304]{1,0:T(1,128)S(1)}, f32[1,2304]{1,0:T(1,128)}, u32[]{:S(2)}) copy-start(f32[1,2304]{1,0:T(1,128)} %get-tuple-element.55) | copy-start | bytes 27652
  966.3 97.0 %copy-start.41 = (f32[1,2304]{1,0:T(1,128)S(1)}, f32[1,2304]{1,0:T(1,128)}, u32[]{:S(2)}) copy-start(f32[1,2304]{1,0:T(1,128)} %get-tuple-element.53) | copy-start | bytes 27652
  966.3 97.0 %copy-start.42 = (f32[1,2304]{1,0:T(1,128)S(1)}, f32[1,2304]{1,0:T(1,128)}, u32[]{:S(2)}) copy-start(f32[1,2304]{1,0:T(1,128)} %get-tuple-element.54) | copy-start | bytes 27652
  966.3 114.5 %copy-start.43 = (f32[288]{0:T(512)S(1)}, f32[288]{0:T(512)}, u32[]{:S(2)}) copy-start(f32[288]{0:T(512)} %param.26) | copy-start | bytes 3460
  966.3 114.5 %copy-start.44 = (f32[288]{0:T(512)S(1)}, f32[288]{0:T(512)}, u32[]{:S(2)}) copy-start(f32[288]{0:T(512)} %param.34) | copy-start | bytes 3460
  966.3 114.5 %copy-start.45 = (f32[288]{0:T(512)S(1)}, f32[288]{0:T(512)}, u32[]{:S(2)}) copy-start(f32[288]{0:T(512)} %param.30) | copy-start | bytes 3460
  966.3 115.1 %copy-start.26 = (f32[2,288,256]{2,1,0:T(8,128)S(1)}, f32[2,288,256]{2,1,0:T(8,128)}, u32[]{:S(2)}) copy-start(f32[2,288,256]{2,1,0:T(8,128)} %param.24) | copy-start | bytes 1769476
  1054.9 29.3 %copy-start.22 = (f32[2,288,512]{2,1,0:T(8,128)S(1)}, f32[2,288,512]{2,1,0:T(8,128)}, u32[]{:S(2)}) copy-start(f32[2,288,512]{2,1,0:T(8,128)} %param.23) | copy-start | bytes 3538948
  1054.9 29.3 %copy-start.27 = (f32[288,512]{1,0:T(8,128)S(1)}, f32[288,512]{1,0:T(8,128)}, u32[]{:S(2)}) copy-start(f32[288,512]{1,0:T(8,128)} %get-tuple-element.57) | copy-start | bytes 1769476
  1054.9 29.3 %copy-start.28 = (f32[288,512]{1,0:T(8,128)S(1)}, f32[288,512]{1,0:T(8,128)}, u32[]{:S(2)}) copy-start(f32[288,512]{1,0:T(8,128)} %get-tuple-element.59) | copy-start | bytes 1769476
  1088.2 19.4 %copy-start.29 = (f32[224,2304]{1,0:T(8,128)S(1)}, f32[224,2304]{1,0:T(8,128)}, u32[]{:S(2)}) copy-start(f32[224,2304]{1,0:T(8,128)} %get-tuple-element.133) | copy-start | bytes 6193156
  (25 other events, 72.9 us)

commit v2 on v1

v2 whole, which is shorter than its diff:
```python
import functools
import math

import jax
import jax.numpy as jnp
from jax import lax
from jax.experimental import pallas as pl
from jax.experimental.pallas import tpu as pltpu
from jax.sharding import PartitionSpec as P

D = 2304
HEAD_WIDTH = 256
FF = 9216
NORMS = 4
QW = 2048
PARAMS = 77865984

EPSILON = 1e-06
SOFT_CAP = 50.0
ROPE_BASE = 10000.0
MASKED_SCORE = -1e30
FIRST_DECAY = 0.9
SECOND_DECAY = 0.95
LEARN_RATE = 0.04
WEIGHT_DECAY = 0.1
ADAM_EPSILON = 1e-08
CLIP_SCALE = 0.5

BF = jnp.bfloat16
F32 = jnp.float32


def quantize(master, fan_in, selector):
    return quantize_by(master, jnp.float32(1.0 / (32.0 * math.sqrt(fan_in))), selector)


def quantize_by(master, step, selector):
    spacing = jnp.where(selector == 0, 1.0, jnp.where(selector == 1, 16.0, 64.0)).astype(F32)
    half = jnp.floor(spacing * 0.5)
    inverse = 1.0 / spacing
    codes = jnp.clip(jnp.floor(master / step + 0.5), -128.0, 127.0)
    top = 128.0 * inverse
    sliced = jnp.clip(jnp.floor((codes + half) * inverse), -top, top - 1.0)
    return ((sliced * spacing) * step).astype(BF)


def inv_root(values):
    return lax.rsqrt(jnp.mean(values * values, axis=-1, keepdims=True) + EPSILON)


def rms_norm(values, norm_gain):
    return values * inv_root(values) * (1.0 + norm_gain)


def rms_back(values, norm_gain, grad):
    root = inv_root(values)
    scaled = grad * (1.0 + norm_gain)
    dot = jnp.mean(values * scaled, axis=-1, keepdims=True)
    grad_values = root * scaled - values * (root * root * root * dot)
    grad_gain = jnp.sum(values * root * grad, axis=0)
    return grad_values, grad_gain


def doc_positions(segments):
    slot_index = jnp.arange(segments.shape[0], dtype=jnp.int32)
    previous = jnp.concatenate([segments[:1] - 1, segments[:-1]])
    starts = segments != previous
    doc_begin = lax.cummax(jnp.where(starts, slot_index, 0), axis=0)
    return slot_index - doc_begin


def rotate(values, cosine, sine):
    half_dim = HEAD_WIDTH // 2
    turned = jnp.concatenate([-values[..., half_dim:], values[..., :half_dim]], -1)
    return values * cosine + turned * sine


def rotate_back(grads, cosine, sine):
    half_dim = HEAD_WIDTH // 2
    scaled = grads * sine
    turned = jnp.concatenate([scaled[..., half_dim:], -scaled[..., :half_dim]], -1)
    return grads * cosine + turned


def mm(left, right):
    return lax.dot_general(left, right, (((1,), (0,)), ((), ())), preferred_element_type=F32)


def mm_rows(left, right):
    return lax.dot_general(left, right, (((0,), (0,)), ((), ())), preferred_element_type=F32)


def mm_cols(left, right):
    return lax.dot_general(left, right, (((1,), (1,)), ((), ())), preferred_element_type=F32)


def adam_update(master, first_moment, second_moment, gradient, factor):
    clipped = gradient * factor
    new_first = FIRST_DECAY * first_moment + (1.0 - FIRST_DECAY) * clipped
    new_second = SECOND_DECAY * second_moment + (1.0 - SECOND_DECAY) * clipped * clipped
    new_master = master - LEARN_RATE * (
        new_first / (jnp.sqrt(new_second) + ADAM_EPSILON) + WEIGHT_DECAY * master
    )
    return (new_master, new_first, new_second)


MESH = pl.DeviceIdType.MESH
ANY = pl.BlockSpec(memory_space=pl.ANY)
VMEM = pl.BlockSpec(memory_space=pltpu.VMEM)
ROWS = 32


class Net:
    def __init__(self, n_dp, n_mp, send_sems, recv_sems, local_sems=None):
        self.n_dp, self.n_mp = n_dp, n_mp
        self.send_sems, self.recv_sems, self.local_sems = send_sems, recv_sems, local_sems
        self.used, self.used_local, self.open = 0, 0, []
        self.i, self.m = lax.axis_index("dp"), lax.axis_index("mp")
        self.y, self.j = self.i % 2, self.i // 2
        self.zl = self.j % 2
        self.c, self.x = self.m % 2, self.m // 2
        self.core_n = (self.i, self.m + 1 - 2 * self.c)
        self.x_n = (self.i, (self.m + 2) % 4)
        self.y_n = (self.i + 1 - 2 * self.y, self.m)
        self.z_n = (self.i + 2 - 4 * self.zl, self.m)

    def z_at(self, d):
        nj = self.n_dp // 2
        return (((self.j + d) % nj) * 2 + self.y, self.m)

    def place(self):
        return (1 - self.y) * self.j + self.y * (self.n_dp - 1 - self.j)

    def ring(self, at):
        n, nj = self.n_dp, self.n_dp // 2
        at = at % n
        late = at // nj
        return (1 - late) * 2 * at + late * (2 * (n - 1 - at) + 1)

    def meet(self, devices):
        barrier = pltpu.get_barrier_semaphore()
        for device in devices:
            pl.semaphore_signal(barrier, inc=1, device_id=device, device_id_type=MESH)
        pl.semaphore_wait(barrier, len(devices))

    def send(self, src, dst, device):
        at = self.used
        self.used += 1
        copy = pltpu.make_async_remote_copy(
            src_ref=src, dst_ref=dst, send_sem=self.send_sems.at[at], recv_sem=self.recv_sems.at[at],
            device_id=device, device_id_type=MESH,
        )
        copy.start()
        self.open.append(copy.wait_send)
        return copy

    def move(self, src, dst):
        at = self.used_local
        self.used_local += 1
        copy = pltpu.make_async_copy(src, dst, self.local_sems.at[at])
        copy.start()
        return copy

    def keep(self, src, dst):
        self.open.append(self.move(src, dst).wait)

    def close(self):
        for wait in self.open:
            wait()


def upper(count):
    return count // 16 * 8


def dma(n):
    return pltpu.SemaphoreType.DMA((n,))


def call(kernel, outs, out_specs, in_specs, scratch, cid, mb, flops=0):
    return pl.pallas_call(
        kernel,
        out_shape=outs,
        in_specs=in_specs,
        out_specs=out_specs,
        scratch_shapes=scratch,
        compiler_params=pltpu.CompilerParams(
            collective_id=cid, has_side_effects=True, vmem_limit_bytes=mb << 20
        ),
    )


def by_rows(total, body, carry=0):
    return lax.fori_loop(
        0, total // ROWS, lambda t, state: body(pl.ds(pl.multiple_of(t * ROWS, ROWS), ROWS), state), carry
    )


def everyone(n_dp, n_mp, i, m):
    flat = i * n_mp + m
    total = n_dp * n_mp
    return [(((flat + t) % total) // n_mp, (flat + t) % n_mp) for t in range(1, total)]


def spread_kernel(n_dp, n_mp, own, full, ss, rs, ls):
    net = Net(n_dp, n_mp, ss, rs, ls)
    others = everyone(n_dp, n_mp, net.i, net.m)
    net.meet(others)
    flat = net.i * n_mp + net.m
    copies = [net.send(own, full.at[flat], device) for device in others]
    net.keep(own, full.at[flat])
    for copy in copies:
        copy.wait_recv()
    net.close()


def spread(n_dp, n_mp, own):
    total = n_dp * n_mp
    return call(
        functools.partial(spread_kernel, n_dp, n_mp),
        jax.ShapeDtypeStruct((total,) + own.shape, own.dtype), VMEM, [VMEM],
        [dma(total), dma(total), dma(1)], 1, 16,
    )(own)


def gather_seq_steps(net, own, seq):
    far = net.send(own, seq.at[1], net.x_n)
    near = net.send(own, seq.at[2], net.core_n)
    net.keep(own, seq.at[0])

    def finish():
        far.wait_recv()
        both = net.send(seq.at[1], seq.at[3], net.core_n)
        near.wait_recv()
        both.wait_recv()

    return finish


def head_kernel(n_dp, n_mp, q, kv, o, tok, wq, wkv, wo, seq, ss, rs, ls):
    net = Net(n_dp, n_mp, ss, rs, ls)
    p = net.place()
    right = (net.ring(p + 1), net.m)
    left = (net.ring(p + n_dp - 1), net.m)
    net.meet([right, left, net.x_n, net.core_n])
    wrows = o.shape[0]
    hr = upper(wrows)
    top, low = pl.ds(0, hr), pl.ds(hr, wrows - hr)
    a = net.send(q, wq.at[net.i], right)
    b = net.send(kv, wkv.at[net.i], left)
    finish = gather_seq_steps(net, tok, seq)
    net.keep(q, wq.at[net.i])
    net.keep(kv, wkv.at[net.i])
    net.keep(o, wo.at[net.i])
    for hop in range(1, n_dp):
        from_right, from_left = net.ring(p + n_dp - hop), net.ring(p + hop)
        a.wait_recv()
        if hop < n_dp - 1:
            a = net.send(wq.at[from_right], wq.at[from_right], right)
        else:
            oa = net.send(o.at[top], wo.at[net.i, top], right)
        b.wait_recv()
        if hop < n_dp - 1:
            b = net.send(wkv.at[from_left], wkv.at[from_left], left)
        else:
            ob = net.send(o.at[low], wo.at[net.i, low], left)
        if hop == n_dp // 2:
            finish()
    for hop in range(1, n_dp):
        from_right, from_left = net.ring(p + n_dp - hop), net.ring(p + hop)
        oa.wait_recv()
        if hop < n_dp - 1:
            oa = net.send(wo.at[from_right, top], wo.at[from_right, top], right)
        ob.wait_recv()
        if hop < n_dp - 1:
            ob = net.send(wo.at[from_left, low], wo.at[from_left, low], left)
    net.close()


def head(n_dp, n_mp, q, kv, o, tok):
    full = lambda a: jax.ShapeDtypeStruct((n_dp,) + a.shape, BF)
    count = 4 * n_dp + 8
    return call(
        functools.partial(head_kernel, n_dp, n_mp),
        [full(q), full(kv), full(o), jax.ShapeDtypeStruct((4,) + tok.shape, BF)],
        [ANY] * 4, [ANY] * 4, [dma(count), dma(count), dma(8)], 2, 16,
    )(q, kv, o, tok)


def gather_pair_steps(net, own, group, split=False):
    far = net.send(own, group.at[2], net.x_n)
    zed = net.send(own, group.at[1], net.z_n)
    near = net.send(own, group.at[4], net.core_n)
    net.keep(own, group.at[0])

    def finish(between=lambda: None):
        head = pl.ds(0, D // 2) if split else pl.ds(0, D)
        rest = pl.ds(D // 2, D // 2)
        zed.wait_recv()
        both = net.send(group.at[1, :, head], group.at[3, :, head], net.x_n)
        far.wait_recv()
        if split:
            other = net.send(group.at[2, :, rest], group.at[3, :, rest], net.z_n)
        near_z = net.send(group.at[1], group.at[5], net.core_n)
        near_x = net.send(group.at[2], group.at[6], net.core_n)
        between()
        both.wait_recv()
        if split:
            other.wait_recv()
        near_both = net.send(group.at[3], group.at[7], net.core_n)
        for copy in (near, near_z, near_x, near_both):
            copy.wait_recv()

    return finish


def pair_partners(net, with_y):
    nj = net.n_dp // 2
    zs = [net.z_at(d) for d in range(1, nj)] if with_y else [net.z_n]
    return [net.core_n, net.x_n] + zs + ([net.y_n] if with_y else [])


def row_tiles(total, size, body):
    lax.fori_loop(
        0, total // size, lambda t, state: (body(pl.ds(pl.multiple_of(t * size, size), size)), state)[1], 0
    )


def project(seq, wq, wkv, cosine, sine, q, k, v):
    total = seq.shape[0]
    kv_cols = k.shape[1]
    half = HEAD_WIDTH // 2

    def body(at):
        tokens = seq[at]
        c, s = cosine[at], sine[at]

        def turn(lin, out, cols):
            for h in range(0, cols, HEAD_WIDTH):
                a, b = lin[:, h : h + half], lin[:, h + half : h + HEAD_WIDTH]
                out[at, h : h + half] = (a * c - b * s).astype(BF)
                out[at, h + half : h + HEAD_WIDTH] = (b * c + a * s).astype(BF)

        turn(mm(tokens, wq[...]), q, q.shape[1])
        lin = mm(tokens, wkv[...])
        turn(lin, k, kv_cols)
        v[at] = lin[:, kv_cols:].astype(BF)

    row_tiles(total, total // 2, body)


def allowed_tile(marks_col, marks_row, at):
    segs, slots = marks_col[at, 0:1], marks_col[at, 1:2]
    seg_row, slot_row, pad_row = marks_row[0:1], marks_row[1:2], marks_row[2:3]
    same_slot = slot_row == slots
    return (seg_row == segs) & (slot_row <= slots) & ((pad_row == 1) | same_slot)


def tile_probs(q, k, allowed, at, head, group):
    cols = slice(head * HEAD_WIDTH, (head + 1) * HEAD_WIDTH)
    kv = head // group
    kv_at = slice(kv * HEAD_WIDTH, (kv + 1) * HEAD_WIDTH)
    bent = jnp.tanh(mm_cols(q[at, cols], k[:, kv_at]) * (HEAD_WIDTH**-0.5 / SOFT_CAP))
    raised = jnp.where(allowed, jnp.exp(SOFT_CAP * bent), 0.0)
    return bent, raised / jnp.sum(raised, axis=-1, keepdims=True)


def attend(q, k, v, marks_col, marks_row, mixed):
    total = q.shape[0]
    heads, group = q.shape[1] // HEAD_WIDTH, q.shape[1] // k.shape[1]

    def body(at):
        allowed = allowed_tile(marks_col, marks_row, at)
        for head in range(heads):
            _, probs = tile_probs(q, k, allowed, at, head, group)
            kv = head // group
            kv_at = slice(kv * HEAD_WIDTH, (kv + 1) * HEAD_WIDTH)
            mixed[at, head * HEAD_WIDTH : (head + 1) * HEAD_WIDTH] = mm(
                probs.astype(BF), v[:, kv_at]
            ).astype(BF)

    row_tiles(total, 128, body)


def out_project(mixed, wo, part):
    blocks, rows, _ = part.shape
    wide = D // 3
    for pair in range(blocks // 2 - 1, -1, -1):
        for n in range(0, D, wide):
            got = mm_cols(mixed[pair * 2 * rows : (pair + 1) * 2 * rows], wo[n : n + wide]).astype(BF)
            part[pair * 2, :, n : n + wide] = got[:rows]
            part[pair * 2 + 1, :, n : n + wide] = got[rows:]


def chunks(wrows):
    return ((0, upper(wrows)), (upper(wrows), wrows - upper(wrows)))


def mid_kernel(
    n_dp, n_mp, seq, wq, wkv, wo, cosine, sine, marks_col, marks_row, inputs, gains, low,
    q, k, v, mixed, att, hid, group, full0, full1,
    part, r1, s2, r2, own, ss, rs, ls,
):
    net = Net(n_dp, n_mp, ss, rs, ls)
    net.meet(pair_partners(net, True))
    nj = n_dp // 2
    full = (full0, full1)
    rows = inputs.shape[0]
    wrows, width = full0.shape[1:]
    half = lambda which: pl.ds(pl.multiple_of(which * width, width), width)
    pieces = [(w, pl.ds(first, count)) for w in (0, 1) for first, count in chunks(wrows)]
    flight, relays = {}, []

    def weights_out(n):
        w, at = pieces[n]
        own_half = low.at[w, at, half(net.zl)]
        net.keep(own_half, full[w].at[net.i, at])
        relays.append(net.send(own_half, full[w].at[net.i, at], net.y_n))
        for d in range(1, nj):
            flight[n, d] = net.send(
                low.at[w, at, half(((net.j + d) % nj) % 2)], full[w].at[net.i, at], net.z_at(d)
            )

    def weights_on(n):
        w, at = pieces[n]
        for d in range(1, nj):
            flight[n, d].wait_recv()
            source = ((net.j + nj - d) % nj) * 2 + net.y
            relays.append(net.send(full[w].at[source, at], full[w].at[source, at], net.y_n))

    weights_out(0)
    weights_out(1)
    project(seq, wq, wkv, cosine, sine, q, k, v)
    attend(q, k, v, marks_col, marks_row, mixed)
    out_project(mixed, wo, part)
    c1 = net.send(part.at[3], r1.at[1], net.core_n)
    c0 = net.send(part.at[2], r1.at[0], net.core_n)
    c1.wait_recv()

    def first(at, state):
        s2[at] = (part[1, at].astype(F32) + r1[1, at].astype(F32)).astype(BF)
        return state

    by_rows(rows, first)
    x = net.send(s2, r2, net.x_n)
    c0.wait_recv()
    weights_on(0)
    weights_out(2)
    x.wait_recv()
    g1, g2 = 1.0 + gains[1:2], 1.0 + gains[2:3]

    def second(at, state):
        total = part[0, at].astype(F32) + r1[0, at].astype(F32) + r2[at].astype(F32)
        att[at] = total
        hidden = inputs[at] + total * inv_root(total) * g1
        hid[at] = hidden
        own[at] = (hidden * inv_root(hidden) * g2).astype(BF)
        return state

    by_rows(rows, second)
    finish = gather_pair_steps(net, own, group)
    weights_on(1)
    weights_out(3)
    finish(lambda: weights_on(2))
    weights_on(3)
    for copy in relays:
        copy.wait_recv()
    net.close()


def mid(n_dp, n_mp, seq, wq, wkv, wo, cosine, sine, marks_col, marks_row, inputs, gains, low):
    rows = inputs.shape[0]
    nj = n_dp // 2
    count = 16 + 8 * nj
    block = (rows, D)
    wrows, width = low.shape[1], low.shape[2] // 2
    kv_cols = wkv.shape[1] // 2
    many = lambda n: pltpu.VMEM((n,) + block, BF)
    bf = lambda *shape: jax.ShapeDtypeStruct(shape, BF)
    total = seq.shape[0]
    return call(
        functools.partial(mid_kernel, n_dp, n_mp),
        [
            bf(total, wq.shape[1]), bf(total, kv_cols), bf(total, kv_cols), bf(total, wq.shape[1]),
            jax.ShapeDtypeStruct(block, F32), jax.ShapeDtypeStruct(block, F32),
            bf(8, *block), bf(n_dp, wrows, width), bf(n_dp, wrows, width),
        ],
        [VMEM] * 6 + [ANY] * 3, [VMEM] * 10 + [ANY],
        [many(4), many(2), pltpu.VMEM(block, BF), pltpu.VMEM(block, BF), pltpu.VMEM(block, BF),
         dma(count), dma(count), dma(8)],
        3, 56,
    )(seq, wq, wkv, wo, cosine, sine, marks_col, marks_row, inputs, gains, low)


def reduce_pair_steps(net, near, far, r1, s2, r2, s3, r3, rows, loaded, split=False):
    cores = {k: net.send(far.at[k], r1.at[k], net.core_n) for k in (3, 2, 1, 0)}
    plan = [(pl.ds(0, D // 2 if split else D), (3, 2), net.x_n, 1, net.z_n)]
    if split:
        plan.append((pl.ds(D // 2, D // 2), (3, 1), net.z_n, 2, net.x_n))
    firsts = {}
    loaded.wait()
    for k in (3, 2, 1) if split else (3, 2):
        cores[k].wait_recv()
        for part, (cols, blocks, device, _, _) in enumerate(plan):
            if k not in blocks:
                continue
            at_block = blocks.index(k)

            def add(at, state, k=k, cols=cols, at_block=at_block):
                s2[at_block, at, cols] = (near[k, at, cols].astype(F32) + r1[k, at, cols].astype(F32)).astype(BF)
                return state

            by_rows(rows, add)
            firsts[part, at_block] = net.send(s2.at[at_block, :, cols], r2.at[at_block, :, cols], device)
    for k in (0,) if split else (1, 0):
        cores[k].wait_recv()
    last = []
    for part, (cols, blocks, _, second, device) in enumerate(plan):
        firsts[part, 0].wait_recv()

        def add(at, state, cols=cols, second=second):
            s3[at, cols] = (
                near[second, at, cols].astype(F32) + r1[second, at, cols].astype(F32) + r2[0, at, cols].astype(F32)
            ).astype(BF)
            return state

        by_rows(rows, add)
        last.append(net.send(s3.at[:, cols], r3.at[:, cols], device))
    for part in range(len(plan)):
        firsts[part, 1].wait_recv()
    return last


def pair_sum(near, r1, r2, r3, at):
    return near[0, at].astype(F32) + r1[0, at].astype(F32) + r2[1, at].astype(F32) + r3[at].astype(F32)


def pair_scratch(rows):
    block = (rows, D)
    return [
        pltpu.VMEM((4,) + block, BF),
        pltpu.VMEM((4,) + block, BF), pltpu.VMEM((2,) + block, BF), pltpu.VMEM((2,) + block, BF),
        pltpu.VMEM(block, BF), pltpu.VMEM(block, BF), pltpu.VMEM(block, BF),
    ]


def rms_back_rows(values, gain, grad):
    root = inv_root(values)
    scaled = grad * gain
    dot = jnp.mean(values * scaled, axis=-1, keepdims=True)
    return root * scaled - values * (root * root * root * dot), jnp.sum(values * root * grad, axis=0, keepdims=True)


def turn_kernel(
    n_dp, n_mp, part, hid, gains, out_grad, live, outputs, dgain, group,
    near, r1, s2, r2, s3, r3, own, ss, rs, ls,
):
    net = Net(n_dp, n_mp, ss, rs, ls)
    net.meet(pair_partners(net, False))
    rows = hid.shape[0]
    far = part.at[pl.ds(4, 4)]
    loaded = net.move(part.at[pl.ds(0, 4)], near)
    for copy in reduce_pair_steps(net, near, far, r1, s2, r2, s3, r3, rows, loaded, True):
        copy.wait_recv()
    g3 = 1.0 + gains[3:4]

    def last(at, state):
        total = pair_sum(near, r1, r2, r3, at)
        outputs[at] = hid[at] + total * inv_root(total) * g3
        grad, dg = rms_back_rows(total, g3, out_grad[at] * live[at])
        own[at] = grad.astype(BF)
        return state + dg

    dgain[...] = by_rows(rows, last, jnp.zeros((1, D), F32))
    gather_pair_steps(net, own, group, True)()
    net.close()


def turn(n_dp, n_mp, part, hid, gains, out_grad, live):
    rows = hid.shape[0]
    block = (rows, D)
    return call(
        functools.partial(turn_kernel, n_dp, n_mp),
        [jax.ShapeDtypeStruct(block, F32), jax.ShapeDtypeStruct((1, D), F32), jax.ShapeDtypeStruct((8,) + block, BF)],
        [VMEM, VMEM, ANY], [ANY, VMEM, VMEM, VMEM, VMEM],
        pair_scratch(rows) + [dma(32), dma(32), dma(4)], 4, 48,
    )(part, hid, gains, out_grad, live)


def in_steps(count, body, carry=0, first=0):
    step = 16 if count % 16 == 0 else 8
    return lax.fori_loop(
        0, count // step,
        lambda t, state: body(pl.ds(pl.multiple_of(first + t * step, 8), step), state, step), carry,
    )


class Scatter:
    def __init__(self, net, grads, stay, came, last):
        self.net, self.grads, self.stay, self.came, self.last = net, grads, stay, came, last
        self.nj, self.wrows, self.width = came.shape
        self.turns = list(range(1, self.nj)) + [0]
        self.ys, self.moves, self.zs = {}, {}, {}

    def along_y(self):
        net = self.net
        for d in self.turns:
            at = (net.j + d) % self.nj
            self.ys[d] = net.send(self.grads.at[at, 1 - net.y], self.came.at[d], net.y_n)
            self.moves[d] = net.move(self.grads.at[at, net.y], self.stay.at[d])

    def along_z(self, turns):
        for d in turns:
            self.ys[d].wait_recv()
            self.moves[d].wait()

            def add(at, state, step, d=d):
                self.stay[d, at] = (self.stay[d, at].astype(F32) + self.came[d, at].astype(F32)).astype(BF)
                return state

            in_steps(self.wrows, add)
            if d:
                self.zs[d] = self.net.send(self.stay.at[d], self.last.at[d - 1], self.net.z_at(d))

    def landed(self):
        for d in range(1, self.nj):
            self.zs[d].wait_recv()

    def halves(self, total, sums):
        self.landed()

        def collect(at, state, step):
            both = [self.stay[0, at].astype(F32), jnp.zeros((step, self.width), F32)]
            for d in range(1, self.nj):
                both[d % 2] = both[d % 2] + self.last[d - 1, at].astype(F32)
            for parity in range(2):
                total[parity, at] = both[parity]
                sq = both[parity] * both[parity]
                for r in range(0, step, 8):
                    state = state + sq[r : r + 8]
            return state

        square = in_steps(self.wrows, collect, jnp.zeros((8, self.width), F32))
        for parity in range(2):
            half = (self.net.zl + parity) % 2
            self.net.keep(total.at[parity], sums.at[:, pl.ds(pl.multiple_of(half * self.width, self.width), self.width)])
        return square

    def whole(self, out):
        self.landed()

        def collect(at, state, step):
            value = self.stay[0, at].astype(F32)
            for d in range(1, self.nj):
                value = value + self.last[d - 1, at].astype(F32)
            out[at] = value
            return state

        in_steps(self.wrows, collect)


def scatter_scratch(nj, wrows, width):
    return [
        pltpu.VMEM((nj, wrows, width), BF), pltpu.VMEM((nj, wrows, width), BF),
        pltpu.VMEM((nj - 1, wrows, width), BF),
    ]


def back_kernel(
    n_dp, n_mp, part, hid, att, gains, out_grad, live, grads,
    ghid, dg1, dg2, seq, sums, squares,
    near, r1, s2, r2, s3, r3, own, stay, came, last, total, ss, rs, ls,
):
    net = Net(n_dp, n_mp, ss, rs, ls)
    nj = n_dp // 2
    net.meet(pair_partners(net, True))
    rows = hid.shape[0]
    far = part.at[pl.ds(4, 4)]
    loaded = net.move(part.at[pl.ds(0, 4)], near)
    weight = Scatter(net, grads, stay, came, last)
    weight.along_y()
    last_sums = reduce_pair_steps(net, near, far, r1, s2, r2, s3, r3, rows, loaded)
    weight.along_z(weight.turns[:2])
    for copy in last_sums:
        copy.wait_recv()
    g1, g2 = 1.0 + gains[1:2], 1.0 + gains[2:3]

    def rows_back(at, state):
        grad = pair_sum(near, r1, r2, r3, at)
        part_hid, d2 = rms_back_rows(hid[at], g2, grad)
        grad_hidden = out_grad[at] * live[at] + part_hid
        ghid[at] = grad_hidden
        grad_att, d1 = rms_back_rows(att[at], g1, grad_hidden)
        own[at] = grad_att.astype(BF)
        return state[0] + d1, state[1] + d2

    zero = jnp.zeros((1, D), F32)
    done1, done2 = by_rows(rows, rows_back, (zero, zero))
    dg1[...] = done1
    dg2[...] = done2
    finish = gather_seq_steps(net, own, seq)
    weight.along_z(weight.turns[2:])
    finish()
    squares[...] = weight.halves(total, sums)
    net.close()


def back(n_dp, n_mp, part, hid, att, gains, out_grad, live, grads):
    rows = hid.shape[0]
    block = (rows, D)
    nj = n_dp // 2
    _, _, wrows, width = grads.shape
    count = 24 + 3 * nj
    return call(
        functools.partial(back_kernel, n_dp, n_mp),
        [
            jax.ShapeDtypeStruct(block, F32), jax.ShapeDtypeStruct((1, D), F32), jax.ShapeDtypeStruct((1, D), F32),
            jax.ShapeDtypeStruct((4,) + block, BF), jax.ShapeDtypeStruct((wrows, 2 * width), F32),
            jax.ShapeDtypeStruct((8, width), F32),
        ],
        [VMEM, VMEM, VMEM, ANY, ANY, VMEM], [ANY, VMEM, VMEM, VMEM, VMEM, VMEM, ANY],
        pair_scratch(rows) + scatter_scratch(nj, wrows, width)
        + [pltpu.VMEM((2, wrows, width), F32), dma(count), dma(count), dma(10 + nj)],
        5, 58,
    )(part, hid, att, gains, out_grad, live, grads)


def attend_back(q, k, v, gm, marks_col, marks_row, cosine, sine, dq, dk, dv, tiles):
    total = q.shape[0]
    heads, group = q.shape[1] // HEAD_WIDTH, q.shape[1] // k.shape[1]
    size = total // 4
    half = HEAD_WIDTH // 2
    scale = HEAD_WIDTH**-0.5

    def body(t, state):
        at = pl.ds(pl.multiple_of(t * size, size), size)
        allowed = allowed_tile(marks_col, marks_row, at)
        c, s = cosine[at], sine[at]
        for head in range(heads):
            kv = head // group
            cols = slice(head * HEAD_WIDTH, (head + 1) * HEAD_WIDTH)
            kv_at = slice(kv * HEAD_WIDTH, (kv + 1) * HEAD_WIDTH)
            bent, probs = tile_probs(q, k, allowed, at, head, group)
            grad = gm[at, cols]
            dv[:, kv_at] += mm_rows(probs.astype(BF), grad)
            gp = mm_cols(grad, v[:, kv_at])
            inner = jnp.sum(probs * gp, axis=-1, keepdims=True)
            ds = (probs * (gp - inner) * (1.0 - bent * bent)).astype(BF)
            dk[:, kv_at] += mm_rows(ds, q[at, cols]) * scale
            turned = mm(ds, k[:, kv_at]) * scale
            a, b = turned[:, :half], turned[:, half:]
            first = head * HEAD_WIDTH
            dq[at, first : first + half] = (a * c + b * s).astype(BF)
            dq[at, first + half : first + HEAD_WIDTH] = (b * c - a * s).astype(BF)
        return state

    lax.fori_loop(tiles[0], tiles[1], body, 0)


def weight_grad(tokens, grads, out):
    wide = D // 3
    for n in range(0, D, wide):
        out[n : n + wide] = mm_rows(tokens[:, n : n + wide], grads[...]).astype(BF)


def close_kernel(
    n_dp, n_mp, seq_grad, seq_normed, q, k, v, mixed, wo, wq, wkv, cosine, sine, marks_col, marks_row,
    inputs, gains, ghid, grads,
    gin, dg0, sum_q, sum_kv, sum_o, sums, squares,
    tokens, normed, wa, gm, dq, dk, dv, dkv, go, gq, gkv, got_q, got_kv, r1, r2,
    stay, came, last, total, ostay, ocame, olast, ss, rs, ls,
):
    net = Net(n_dp, n_mp, ss, rs, ls)
    p = net.place()
    right = (net.ring(p + 1), net.m)
    left = (net.ring(p + n_dp - 1), net.m)
    nj = n_dp // 2
    rows = inputs.shape[0]
    seq_len, wrows = tokens.shape[0], sum_q.shape[0]
    net.meet(
        [net.x_n, net.core_n] + [((net.i + t) % n_dp, net.m) for t in range(1, n_dp)]
    )
    weight = Scatter(net, grads, stay, came, last)
    weight.along_y()
    token_load = net.move(seq_grad, tokens)
    wa_load = net.move(wo, wa)
    normed_load = net.move(seq_normed, normed)
    ghid_load = net.move(ghid, gin)
    dk[...] = jnp.zeros_like(dk)
    dv[...] = jnp.zeros_like(dv)
    token_load.wait()
    wa_load.wait()

    def mix(at):
        gm[at] = mm(tokens[at], wa[...]).astype(BF)

    row_tiles(seq_len, seq_len // 2, mix)
    wa_load = net.move(wq, wa)
    weight_grad(tokens, mixed, go.reshape(D, go.shape[-1]))
    out = Scatter(net, go, ostay, ocame, olast)
    out.along_y()
    attend_back(q, k, v, gm, marks_col, marks_row, cosine, sine, dq, dk, dv, (0, 2))
    weight.along_z(weight.turns[:2])
    attend_back(q, k, v, gm, marks_col, marks_row, cosine, sine, dq, dk, dv, (2, 4))
    weight.along_z(weight.turns[2:])
    kv_cols = k.shape[1]
    half = HEAD_WIDTH // 2

    def turn_keys(at):
        c, s = cosine[at], sine[at]
        for h in range(0, kv_cols, HEAD_WIDTH):
            a, b = dk[at, h : h + half], dk[at, h + half : h + HEAD_WIDTH]
            dkv[at, h : h + half] = (a * c + b * s).astype(BF)
            dkv[at, h + half : h + HEAD_WIDTH] = (b * c - a * s).astype(BF)
        dkv[at, kv_cols:] = dv[at].astype(BF)

    row_tiles(seq_len, 128, turn_keys)
    normed_load.wait()
    weight_grad(normed, dq, gq)
    weight_grad(normed, dkv, gkv)

    def block(at):
        return pl.ds(pl.multiple_of(net.ring(p + 2 * n_dp + at) * wrows, 8), wrows)

    lanes = ((gq, got_q, sum_q, right, -1), (gkv, got_kv, sum_kv, left, 1))
    flight = [net.send(terms.at[block(way)], got.at[0], device) for terms, got, _, device, way in lanes]

    def hop(n):
        end = n == n_dp - 1
        for lane, (terms, got, result, device, way) in enumerate(lanes):
            flight[lane].wait_recv()
            first = net.ring(p + 2 * n_dp + way * (1 + n)) * wrows

            def add(t, state, step):
                at = pl.ds(pl.multiple_of(first + t * step, 8), step)
                here = pl.ds(pl.multiple_of(t * step, 8), step)
                value = got[n - 1, here].astype(F32) + terms[at].astype(F32)
                if end:
                    result[here] = value
                else:
                    terms[at] = value.astype(BF)
                return state

            step = 16 if wrows % 16 == 0 else 8
            lax.fori_loop(0, wrows // step, lambda t, state: add(t, state, step), 0)
            if not end:
                flight[lane] = net.send(terms.at[block(way * (1 + n))], got.at[n], device)

    wa_load.wait()
    wide = D // 3
    copies = []
    for pair in (1, 0):
        at = pl.ds(pair * 2 * rows, 2 * rows)
        for n in range(0, D, wide):
            tokens[at, n : n + wide] = (
                mm_cols(dq[at], wa[n : n + wide]) + mm_cols(dkv[at], wkv[n : n + wide])
            ).astype(BF)
        if pair:
            c1 = net.send(tokens.at[pl.ds(3 * rows, rows)], r1.at[1], net.core_n)
            c0 = net.send(tokens.at[pl.ds(2 * rows, rows)], r1.at[0], net.core_n)
            hop(1)
    c1.wait_recv()

    def add_far(at, state):
        here = pl.ds(pl.multiple_of(rows + at.start, ROWS), ROWS)
        tokens[here] = (tokens[here].astype(F32) + r1[1, at].astype(F32)).astype(BF)
        return state

    by_rows(rows, add_far)
    x = net.send(tokens.at[pl.ds(rows, rows)], r2, net.x_n)
    c0.wait_recv()
    hop(2)
    out.along_z(out.turns)
    hop(3)
    x.wait_recv()
    ghid_load.wait()
    g0 = 1.0 + gains[0:1]

    def rows_in(at, state):
        grad = tokens[at].astype(F32) + r1[0, at].astype(F32) + r2[at].astype(F32)
        part, d0 = rms_back_rows(inputs[at], g0, grad)
        gin[at] = gin[at] + part
        return state + d0

    dg0[...] = by_rows(rows, rows_in, jnp.zeros((1, D), F32))
    for n in range(4, n_dp - 1):
        hop(n)
    squares[...] = weight.halves(total, sums)
    hop(n_dp - 1)
    out.whole(sum_o)
    net.close()


def close(n_dp, n_mp, seq_grad, seq_normed, q, k, v, mixed, wo, wq, wkv, cosine, sine, marks_col, marks_row,
          inputs, gains, ghid, grads):
    rows = inputs.shape[0]
    nj = n_dp // 2
    _, _, wrows, width = grads.shape
    cols, kv_cols = q.shape[1], k.shape[1]
    seq_len = q.shape[0]
    count = 16 + 6 * nj + 2 * n_dp
    vm = lambda *shape: pltpu.VMEM(shape, BF)
    small = jax.ShapeDtypeStruct((wrows, cols), F32)
    return call(
        functools.partial(close_kernel, n_dp, n_mp),
        [
            jax.ShapeDtypeStruct((rows, D), F32), jax.ShapeDtypeStruct((1, D), F32), small,
            jax.ShapeDtypeStruct((wrows, 2 * kv_cols), F32), small,
            jax.ShapeDtypeStruct((wrows, 2 * width), F32), jax.ShapeDtypeStruct((8, width), F32),
        ],
        [VMEM] * 5 + [ANY, VMEM],
        [ANY, ANY] + [VMEM] * 4 + [ANY, ANY] + [VMEM] * 7 + [ANY, ANY],
        [
            vm(seq_len, D), vm(seq_len, D), vm(D, cols), vm(seq_len, cols), vm(seq_len, cols),
            pltpu.VMEM((seq_len, kv_cols), F32), pltpu.VMEM((seq_len, kv_cols), F32), vm(seq_len, 2 * kv_cols),
            vm(nj, 2, wrows, cols), vm(D, cols), vm(D, 2 * kv_cols),
            vm(n_dp - 1, wrows, cols), vm(n_dp - 1, wrows, 2 * kv_cols), vm(2, rows, D), vm(rows, D),
        ]
        + scatter_scratch(nj, wrows, width) + [pltpu.VMEM((2, wrows, width), F32)]
        + scatter_scratch(nj, wrows, cols) + [dma(count), dma(count), dma(10 + 2 * nj)],
        6, 60,
    )(seq_grad, seq_normed, q, k, v, mixed, wo, wq, wkv, cosine, sine, marks_col, marks_row,
      inputs, gains, ghid, grads)


def plain(kernel, grid, outs, out_specs, in_specs, mb, flops):
    return pl.pallas_call(
        kernel,
        out_shape=outs,
        grid=grid,
        in_specs=in_specs,
        out_specs=out_specs,
        compiler_params=pltpu.CompilerParams(
            dimension_semantics=("arbitrary",) * len(grid), vmem_limit_bytes=mb << 20
        ),
        cost_estimate=pl.CostEstimate(flops=flops, bytes_accessed=40 << 20, transcendentals=0),
    )


def whole(shape):
    return pl.BlockSpec(shape, lambda t: (0,) * len(shape), pipeline_mode=pl.Buffered(1))


def tile(rows, cols):
    return pl.BlockSpec((None, rows, cols), lambda t: (t, 0, 0))


GELU = math.sqrt(2.0 / math.pi)


def up_kernel(x, wg, wu, gate, up, act):
    g = mm(x[...], wg[...])
    u = mm(x[...], wu[...])
    gate[...] = g
    up[...] = u
    bend = jnp.tanh(GELU * (g + 0.044715 * (g * g * g)))
    act[...] = (0.5 * g * (1.0 + bend) * u).astype(BF)


def mlp_up(x, wg, wu):
    blocks, rows, _ = x.shape
    width = wg.shape[1]
    shape = (blocks, rows, width)
    return plain(
        up_kernel, (blocks,),
        [jax.ShapeDtypeStruct(shape, F32), jax.ShapeDtypeStruct(shape, F32), jax.ShapeDtypeStruct(shape, BF)],
        [tile(rows, width)] * 3, [tile(rows, D), whole(wg.shape), whole(wu.shape)], 48,
        4 * blocks * rows * D * width,
    )(x, wg, wu)


def down_kernel(act, wd, part):
    part[...] = mm_cols(act[...], wd[...]).astype(BF)


def mlp_down(act, wd):
    blocks, rows, width = act.shape
    return plain(
        down_kernel, (blocks,), jax.ShapeDtypeStruct((blocks, rows, D), BF),
        tile(rows, D), [tile(rows, width), whole(wd.shape)], 32, 2 * blocks * rows * D * width,
    )(act, wd)


def down_back_kernel(grad, gate, up, wg, wu, wd, dgate, dup, part):
    ga = mm(grad[...], wd[...])
    g = gate[...]
    square = g * g
    bend = jnp.tanh(GELU * (g + 0.044715 * (square * g)))
    halved = 0.5 * (1.0 + bend)
    slope = halved + (0.5 * GELU) * g * (1.0 - bend * bend) * (1.0 + (3.0 * 0.044715) * square)
    dg = (ga * up[...] * slope).astype(BF)
    du = (ga * (g * halved)).astype(BF)
    dgate[...] = dg
    dup[...] = du
    part[...] = (mm_cols(dg, wg[...]) + mm_cols(du, wu[...])).astype(BF)


def mlp_back(grad, gate, up, wg, wu, wd):
    blocks, rows, _ = grad.shape
    width = wg.shape[1]
    shape = (blocks, rows, width)
    return plain(
        down_back_kernel, (blocks,),
        [jax.ShapeDtypeStruct(shape, BF), jax.ShapeDtypeStruct(shape, BF), jax.ShapeDtypeStruct((blocks, rows, D), BF)],
        [tile(rows, width), tile(rows, width), tile(rows, D)],
        [tile(rows, D), tile(rows, width), tile(rows, width)] + [whole(wg.shape)] * 3, 56,
        6 * blocks * rows * D * width,
    )(grad, gate, up, wg, wu, wd)


def finish_kernel(n_dp, n_mp, terms, square, total_gain, total_square, got, sgot, mine, ss, rs, ls):
    net = Net(n_dp, n_mp, ss, rs, ls)
    others = everyone(n_dp, n_mp, net.i, net.m)
    net.meet(others)
    flat = net.i * n_mp + net.m
    copies = [
        net.send(terms.at[dp * n_mp + mp], got.at[flat], (dp, mp)) for dp, mp in others
    ]
    net.keep(terms.at[flat], got.at[flat])
    net.open.pop()()
    for copy in copies:
        copy.wait_recv()
    total = lax.fori_loop(0, n_dp * n_mp, lambda t, s: s + got[t], jnp.zeros(got.shape[1:], F32))
    total_gain[...] = total
    mine[...] = square[...] + jnp.sum(total * total) * (1.0 / (mine.shape[0] * mine.shape[1]))
    copies = [net.send(mine, sgot.at[flat], device) for device in others]
    net.keep(mine, sgot.at[flat])
    net.open.pop()()
    for copy in copies:
        copy.wait_recv()
    total_square[...] = lax.fori_loop(0, n_dp * n_mp, lambda t, s: s + sgot[t], jnp.zeros(mine.shape, F32))
    net.close()


def finish_all(n_dp, n_mp, terms, square):
    total = n_dp * n_mp
    shape = terms.shape[1:]
    return call(
        functools.partial(finish_kernel, n_dp, n_mp),
        [jax.ShapeDtypeStruct(shape, F32), jax.ShapeDtypeStruct(square.shape, F32)],
        [VMEM, VMEM], [VMEM, VMEM],
        [
            pltpu.VMEM((total,) + shape, F32), pltpu.VMEM((total,) + square.shape, F32),
            pltpu.VMEM(square.shape, F32), dma(2 * total), dma(2 * total), dma(2),
        ],
        7, 16,
    )(terms, square)


def build_local(n_dp, n_mp):
    nj = n_dp // 2

    def y_swap(value):
        return lax.ppermute(value, "dp", [(k, k ^ 1) for k in range(n_dp)])

    def z_shift(value, d):
        pairs = [(a * 2 + b, ((a + d) % nj) * 2 + b) for a in range(nj) for b in range(2)]
        return lax.ppermute(value, "dp", pairs)

    def scatter_first(grad, y):
        away = lax.dynamic_index_in_dim(grad, 1 - y, 1, keepdims=False)
        stay = lax.dynamic_index_in_dim(grad, y, 1, keepdims=False)
        return stay, y_swap(away)

    def scatter_second(stay, came, j):
        both = (stay.astype(F32) + came.astype(F32)).astype(BF)
        both = [lax.dynamic_index_in_dim(both, (j + d) % nj, 0, keepdims=False) for d in range(nj)]
        return both[0], [z_shift(both[d], d) for d in range(1, nj)]

    def local(
        inputs, out_grad, segment_ids, pad_mask, bit_sel, w_qo, w_kv, w_mlp, norm_gains,
        m_qo, m_kv, m_mlp, m_gains, v_qo, v_kv, v_mlp, v_gains,
    ):
        i, m = lax.axis_index("dp"), lax.axis_index("mp")
        y, j = i % 2, i // 2
        zl = j % 2
        rows = inputs.shape[0]
        seq_len = segment_ids.shape[1]
        wrows = w_qo.shape[1]

        gain_rows = spread(n_dp, n_mp, norm_gains.reshape(1, -1)).reshape(NORMS, D)
        low_q = quantize(w_qo[0], D, bit_sel[0])
        low_o = quantize(w_qo[1], QW, bit_sel[0])
        low_kv = jnp.concatenate([quantize(w_kv[0], D, bit_sel[1]), quantize(w_kv[1], D, bit_sel[1])], 1)
        low_up = quantize(w_mlp[:2], D, bit_sel[2])
        low_down = quantize(w_mlp[2], FF, bit_sel[2])
        norm_in = rms_norm(inputs, gain_rows[0]).astype(BF)
        wq, wkv, wo, seq_normed = head(n_dp, n_mp, low_q, low_kv, low_o, norm_in)
        wq = wq.reshape(D, -1)
        wkv = wkv.reshape(D, -1)
        wo = wo.reshape(D, -1)
        seq_normed = seq_normed.reshape(seq_len, D)

        seq_normed, low_down = lax.optimization_barrier((seq_normed, low_down))
        halves = low_down.reshape(wrows, 2, -1)
        same = jnp.where(zl == 0, halves[:, 0], halves[:, 1])
        other = jnp.where(zl == 0, halves[:, 1], halves[:, 0])
        down_blocks = {0: y_swap(same)}
        for d in range(1, nj):
            down_blocks[d] = z_shift(other if d % 2 else same, d)

        order = jnp.stack([m, m ^ 2, m ^ 1, m ^ 3])

        def in_order(vector):
            return vector.reshape(n_mp, rows)[order].reshape(-1)

        segments = segment_ids[0]
        positions = in_order(doc_positions(segments))
        slots = in_order(jnp.arange(seq_len, dtype=jnp.int32))
        segs = in_order(segments)
        pads = in_order(pad_mask[0])
        kv_cols = wkv.shape[1] // 2
        half_dim = HEAD_WIDTH // 2
        frequency = ROPE_BASE ** (-jnp.arange(half_dim, dtype=F32) * 2.0 / HEAD_WIDTH)
        angles = positions.astype(F32)[:, None] * frequency[None, :]
        cosine = jnp.cos(angles)
        sine = jnp.sin(angles)
        marks = jnp.stack([segs, slots, pads] + [segs] * 5)
        query_bf, key_bf, value_bf, mixed_bf, attended, hidden_in, group_ffn, w_gate, w_up = mid(
            n_dp, n_mp, seq_normed, wq, wkv, wo, cosine, sine, marks.T, marks, inputs, gain_rows, low_up
        )
        w_gate = w_gate.reshape(D, -1)
        w_up = w_up.reshape(D, -1)
        w_down = jnp.zeros((n_dp,) + same.shape, BF)

        def put(block, at):
            return lax.dynamic_update_index_in_dim(w_down, block, at, 0)

        w_down = put(same, i)
        w_down = put(down_blocks[0], i + 1 - 2 * y)
        for d in range(1, nj):
            got, group_ffn = lax.optimization_barrier((down_blocks[d], group_ffn))
            at = ((j + nj - d) % nj) * 2
            w_down = put(got, at + y)
            w_down = put(y_swap(got), at + 1 - y)
        w_down = w_down.reshape(D, -1)
        gate, up, activated = mlp_up(group_ffn, w_gate, w_up)
        part = mlp_down(activated, w_down)
        live = lax.dynamic_slice_in_dim(pad_mask[0], m * rows, rows).astype(F32)[:, None]
        outputs, grad_gain_three, group_grad = turn(
            n_dp, n_mp, part, hidden_in, gain_rows, out_grad, live
        )
        tokens = 8 * rows
        grad_down = mm_rows(group_grad.reshape(tokens, D), activated.reshape(tokens, -1))
        grad_down = grad_down.astype(BF).reshape(nj, 2, wrows, -1)
        grad_down, group_grad = lax.optimization_barrier((grad_down, group_grad))
        down_stay, down_came = scatter_first(grad_down, y)
        grad_gate, grad_up, part = mlp_back(group_grad, gate, up, w_gate, w_up, w_down)
        flat_ffn = group_ffn.reshape(tokens, D)
        grads_gate = mm_rows(flat_ffn, grad_gate.reshape(tokens, -1)).astype(BF).reshape(nj, 2, wrows, -1)
        grads_gate, grad_up, down_came = lax.optimization_barrier((grads_gate, grad_up, down_came))
        down_own, down_shifted = scatter_second(down_stay, down_came, j)
        grads_up = mm_rows(flat_ffn, grad_up.reshape(tokens, -1)).astype(BF).reshape(nj, 2, wrows, -1)
        grad_hidden, grad_gain_one, grad_gain_two, seq_grad, sum_gate, square_gate = back(
            n_dp, n_mp, part, hidden_in, attended, gain_rows, out_grad, live, grads_gate
        )
        seq_grad, down_shifted = lax.optimization_barrier((seq_grad, down_shifted))
        sums = [down_own.astype(F32), 0.0]
        for d in range(1, nj):
            sums[d % 2] = sums[d % 2] + down_shifted[d - 1].astype(F32)
        sum_down = jnp.concatenate(
            [jnp.where(zl == 0, sums[0], sums[1]), jnp.where(zl == 0, sums[1], sums[0])], 1
        )
        grad_in, grad_gain_zero, sum_q, sum_kv, sum_o, sum_up, square_up = close(
            n_dp, n_mp, seq_grad.reshape(seq_len, D), seq_normed, query_bf, key_bf, value_bf, mixed_bf,
            wo, wq, wkv, cosine, sine, marks.T, marks, inputs, gain_rows, grad_hidden, grads_up,
        )
        terms = jnp.concatenate([grad_gain_zero, grad_gain_one, grad_gain_two, grad_gain_three])
        square = jnp.sum(square_gate + square_up)
        for part in (sum_q, sum_kv, sum_o, sum_down):
            square = square + jnp.sum(part * part)
        square = jnp.broadcast_to(square * (1.0 / 1024.0), (8, 128))
        sum_gains, squares = finish_all(n_dp, n_mp, terms.reshape(n_dp * n_mp, 1, -1), square)
        grad_norm = jnp.sqrt(jnp.sum(squares)).reshape(1)
        factor = jnp.minimum(1.0, CLIP_SCALE * math.sqrt(PARAMS) / grad_norm[0])

        new_w_qo, new_m_qo, new_v_qo = adam_update(w_qo, m_qo, v_qo, jnp.stack([sum_q, sum_o]), factor)
        new_w_kv, new_m_kv, new_v_kv = adam_update(
            w_kv, m_kv, v_kv, jnp.stack([sum_kv[:, :kv_cols], sum_kv[:, kv_cols:]]), factor
        )
        new_w_mlp, new_m_mlp, new_v_mlp = adam_update(
            w_mlp, m_mlp, v_mlp, jnp.stack([sum_gate, sum_up, sum_down]), factor
        )
        new_gains, new_m_gains, new_v_gains = adam_update(
            norm_gains, m_gains, v_gains, sum_gains.reshape(-1), factor
        )
        return (
            outputs, grad_in, grad_norm, new_w_qo, new_w_kv, new_w_mlp, new_gains,
            new_m_qo, new_m_kv, new_m_mlp, new_m_gains, new_v_qo, new_v_kv, new_v_mlp, new_v_gains,
        )

    return local


def solution(mesh):
    tokens = P(("dp", "mp"), None)
    weight = P(None, "dp", "mp")
    flat = P(("dp", "mp"))
    per_weight = (weight, weight, weight, flat)
    return jax.shard_map(
        build_local(mesh.shape["dp"], mesh.shape["mp"]),
        mesh=mesh,
        in_specs=(tokens, tokens, P("dp", None), P("dp", None), P()) + per_weight * 3,
        out_specs=(tokens, tokens, P()) + per_weight * 3,
        check_vma=False,
    )
```

time: 1120 us -> 958 us (0.86)
  matrix products: 216 us -> 45.1 us
  other arithmetic: 71.2 us -> 56.3 us
  waiting for transfers between devices: 0 us -> 13 us
  starting transfers between devices: 0 us -> 11.8 us
    dot_general x24 -> x0, matrix products: 161 us -> none  [the longest x12 72.2 us: mm_cols(): lax.dot_general(left, right, (((1,), (1,)), ((), ())), preferred_element_...]
    pallas_call x2 -> x5, Pallas kernels: 329 us -> 463 us  [the longest x1 196 us: mid(): call(functools.partial(mid_kernel, n_dp, n_mp), [bf(total, wq.shape[1]),...]
    pallas_call x1, Pallas kernels: 226 us -> 112 us  [back(): call(functools.partial(back_kernel, n_dp, n_mp), [jax.ShapeDtypeStruct(bl...]
    pallas_call x1, Pallas kernels: 110 us -> 83.1 us  [turn(): call(functools.partial(turn_kernel, n_dp, n_mp), [jax.ShapeDtypeStruct(bl...]
    ppermute x0 -> x11, waiting for transfers between devices: none -> 13 us  [the longest x5 13 us: y_swap(): return lax.ppermute(value, 'dp', [(k, k ^ 1) for k in range(n_dp)])]
    ppermute x0 -> x11, starting transfers between devices: none -> 11.8 us  [the longest x6 7.89 us: z_shift(): return lax.ppermute(value, 'dp', pairs)]
    slice x5 -> x3, local copies, waits for them, and re-layouts: 14.6 us -> 3.34 us  [the longest x1 1.84 us: local(): other = jnp.where(zl == 0, halves[:, 1], halves[:, 0])]
    dot_general x6 -> x3, matrix products: 55.2 us -> 45.1 us  [mm_rows(): lax.dot_general(left, right, (((0,), (0,)), ((), ())), preferred_element_...]
  transfers between devices with their start and end apart: 0 -> 11, of which waited for: 0 -> 1; matrix products, arithmetic and copies ran while one was open for 0% -> 5% of each run, Pallas kernels for 0% -> 40%
where the time goes in v2:
time: 958 us; the launch traced here: 951 us
  Pallas kernels  773 us (81%)
  other arithmetic  56.3 us (6%)
  matrix products  45.1 us (5%)
  local copies, waits for them, and re-layouts  40.4 us (4%)
  waiting for transfers between devices  13 us (1%)
  starting transfers between devices  11.8 us (1%)
  between operations  11.5 us (1%)
    pallas_call x1, Pallas kernels, mid(): call(functools.partial(mid_kernel, n_dp, n_mp), [bf(total, wq.shape[1]),...  196 us
    pallas_call x1, Pallas kernels, close(): call(functools.partial(close_kernel, n_dp, n_mp), [jax.ShapeDtypeStruct((...  173 us
    pallas_call x1, Pallas kernels, back(): call(functools.partial(back_kernel, n_dp, n_mp), [jax.ShapeDtypeStruct(bl...  112 us
    pallas_call x1, Pallas kernels, head(): call(functools.partial(head_kernel, n_dp, n_mp), [full(q), full(kv), full...  87.9 us
    pallas_call x1, Pallas kernels, turn(): call(functools.partial(turn_kernel, n_dp, n_mp), [jax.ShapeDtypeStruct(bl...  83.1 us
    pallas_call x1, Pallas kernels, mlp_back(): plain(down_back_kernel, (blocks,), [jax.ShapeDtypeStruct(shape, BF), jax....  47.9 us
    dot_general x3, matrix products, mm_rows(): lax.dot_general(left, right, (((0,), (0,)), ((), ())), preferred_element_...  45.1 us
    pallas_call x1, Pallas kernels, mlp_up(): plain(up_kernel, (blocks,), [jax.ShapeDtypeStruct(shape, F32), jax.ShapeD...  28.5 us
  transfers between devices with their start and end apart: 11, of which 1 were waited for; matrix products, arithmetic and copies ran while one was open for 5% of the time, Pallas kernels for 40%

profile of v2, /device:TPU:0, one launch (start us, length us, event | category | flops | bytes accessed | tf_op | source)
XLA Modules:
  0.0 951.5 jit_solution(4869352871672405214)
XLA Ops:
  8.7 9.9 %shard_map.280 = f32[32,1,288]{2,1,0:T(1,128)S(1)} custom-call(f32[1,288]{1,0:T(1,128)S(1)} %reshape.408.own), custom_call_target="tpu_custom_call" | custom-call | tf_op jit(solution)/shard_map/pallas_call | solution.py:219
  20.8 2.7 fusion.6
  23.5 87.9 %shard_map.281 = (bf16[8,288,512]{2,1,0:T(8,128)(2,1)S(1)}, bf16[8,288,512]{2,1,0:T(8,128)(2,1)S(1)}, bf16[8,288,512]{2,1,0:T(8,128)(2,1)S(1)}, bf16[4,224,2304]{2,1,0:T(8,128)(2,1)S(1)}) custom-call(bf16[288,512]{1,0:T(8,128)(2,1)S(1)} %get-tuple-element.147.q, bf16[288,512]{1,0:T(8,128)(2,1)S(1)} %pad_maximum_fusion.1.kv, ...), custom_call_target="tpu_custom_call" | custom-call | tf_op jit(solution)/shard_map/pallas_call | solution.py:283
  111.5 2.0 copy-done
  118.0 1.8 fusion.25
  119.9 2.8 broadcast_in_dim.43
  128.2 2.9 collective-permute-start
  138.0 2.8 multiply_sine_fusion
  140.9 4.8 multiply_convert_fusion.low
  145.7 196.3 %shard_map.282 = (bf16[896,512]{1,0:T(8,128)(2,1)}, bf16[896,256]{1,0:T(8,128)(2,1)}, bf16[896,256]{1,0:T(8,128)(2,1)}, bf16[896,512]{1,0:T(8,128)(2,1)}, f32[22...) custom-call(bf16[896,2304]{1,0:T(8,128)(2,1)} %bitcast.107, ...), custom_call_target="tpu_custom_call" | custom-call | tf_op jit(solution)/shard_map/pallas_call | solution.py:481
  342.1 2.0 collective-permute-start.5
  344.2 28.5 %shard_map.283 = (f32[8,224,1152]{2,1,0:T(8,128)}, f32[8,224,1152]{2,1,0:T(8,128)}, bf16[8,224,1152]{2,1,0:T(8,128)(2,1)S(1)}) custom-call(bf16[8,224,2304]{2,1,0:T(8,128)(2,1)} %get-tuple-element.78.x, bf16[2304,1152]{1,0:T(8,128)(2,1)} %bitcast.127, bf16[2304,1152]{1,0:T(8,128)(2,1)} %bitcast.129), custom_call_target="tpu_custom_call" | custom-call | flops 19025362944 | bytes 41943040 | tf_op jit(solution)/shard_map/pallas_call | solution.py:964
  374.5 13.0 %collective-permute-done.4 = bf16[288,1152]{1,0:T(8,128)(2,1)S(1)} collective-permute-done((bf16[288,1152]{1,0:T(8,128)(2,1)S(1)}, bf16[288,1152]{1,0:T(8,128)(2,1)S(1)}, u32[]{:S(2)}, u32[]{:S(2)}) %collective-permute-start.4) | collective-permute-done | bytes 663584 | tf_op jit(solution)/shard_map/ppermute | solution.py:1054
  392.0 16.9 %shard_map.284.part = bf16[8,224,2304]{2,1,0:T(8,128)(2,1)S(1)} custom-call(bf16[8,224,1152]{2,1,0:T(8,128)(2,1)S(1)} %get-tuple-element.81.act, bf16[2304,1152]{1,0:T(8,128)(2,1)} %bitcast.32.wd), custom_call_target="tpu_custom_call" | custom-call | flops 9512681472 | bytes 41943040 | tf_op jit(solution)/shard_map/pallas_call | solution.py:978
  408.9 3.2 copy-done.4
  412.1 83.1 %shard_map.285 = (f32[224,2304]{1,0:T(8,128)S(1)}, f32[1,2304]{1,0:T(1,128)S(1)}, bf16[8,224,2304]{2,1,0:T(8,128)(2,1)}) custom-call(bf16[8,224,2304]{2,1,0:T(8,128)(2,1)} %copy-done.4, f32[224,2304]{1,0:T(8,128)S(1)} %copy-done.5, f32[4,2304]{1,0:T(4,128)S(1)} %copy-done.7, f32[224,2304]{1,0:T(8,128)} %out_grad.3, f32[224,1]{1,0:T(8,128)S(1)} %copy.39.live), custom_call_target="tpu_custom_call" | custom-call | tf_op jit(solution)/shard_map/pallas_call | solution.py:582
  495.1 13.6 %fusion = bf16[2304,1152]{1,0:T(8,128)(2,1)S(1)} fusion(bf16[8,224,2304]{2,1,0:T(8,128)(2,1)} %get-tuple-element.88.grad, bf16[8,224,1152]{2,1,0:T(8,128)(2,1)S(1)} %get-tuple-element.81.act), kind=kOutput, calls=%fused_computation.8 | convolution fusion | flops 9515335680 | bytes 17694720 | tf_op jit(solution)/shard_map/dot_general | solution.py:90
  508.8 2.4 copy-done.11
  511.7 47.9 %shard_map.286 = (bf16[8,224,1152]{2,1,0:T(8,128)(2,1)}, bf16[8,224,1152]{2,1,0:T(8,128)(2,1)}, bf16[8,224,2304]{2,1,0:T(8,128)(2,1)}) custom-call(bf16[8,224,2304]{2,1,0:T(8,128)(2,1)} %get-tuple-element.88.grad, f32[8,224,1152]{2,1,0:T(8,128)} %get-tuple-element.89.gate, f32[8,224,1152]{2,1,0:T(8,128)} %get-tuple-element.90.up, ...), custom_call_target="tpu_custom_call" | custom-call | flops 28538044416 | bytes 41943040 | tf_op jit(solution)/shard_map/pallas_call | solution.py:1002
  559.6 16.2 %fusion.1 = bf16[2304,1152]{1,0:T(8,128)(2,1)} fusion(bf16[8,224,2304]{2,1,0:T(8,128)(2,1)} %get-tuple-element.78.x, bf16[8,224,1152]{2,1,0:T(8,128)(2,1)} %get-tuple-element.93), kind=kOutput, calls=%fused_computation.9 | convolution fusion | flops 9515335680 | bytes 17694720 | tf_op jit(solution)/shard_map/dot_general | solution.py:90
  575.9 2.6 fusion.4
  580.2 2.8 collective-permute-start.9
  583.0 15.2 %fusion.2 = bf16[2304,1152]{1,0:T(8,128)(2,1)} fusion(bf16[8,224,2304]{2,1,0:T(8,128)(2,1)} %get-tuple-element.78.x, bf16[8,224,1152]{2,1,0:T(8,128)(2,1)S(1)} %copy-done.31), kind=kOutput, calls=%fused_computation.10 | convolution fusion | flops 9515335680 | bytes 17694720 | tf_op jit(solution)/shard_map/dot_general | solution.py:90
  598.3 112.4 %shard_map.287 = (f32[224,2304]{1,0:T(8,128)}, f32[1,2304]{1,0:T(1,128)}, f32[1,2304]{1,0:T(1,128)}, bf16[4,224,2304]{2,1,0:T(8,128)(2,1)}, f32[288,2304]{1,0:T(8,128)}, /*index=5*/f32[8,1152]{1,0:T(8,128)}) custom-call(bf16[8,224,2304]{2,1,0:T(8,128)(2,1)} %get-tuple-element.91.part, f32[224,2304]{1,0:T(8,128)} %get-tuple-element.85.hid, ...), custom_call_target="tpu_custom_call" | custom-call | tf_op jit(solution)/shard_map/pallas_call | solution.py:714
  710.7 173.4 %shard_map.288 = (f32[224,2304]{1,0:T(8,128)}, f32[1,2304]{1,0:T(1,128)}, f32[288,512]{1,0:T(8,128)}, f32[288,512]{1,0:T(8,128)}, f32[288,512]{1,0:T(8,128)}, /*index=5*/f32[288,2304]{1,0:T(8,128)}, f32[8,1152]{1,0:T(8,128)}) custom-call(bf16[896,2304]{1,0:T(8,128)(2,1)} %bitcast.119, bf16[896,2304]{1,0:T(8,128)(2,1)} %bitcast.108, ...), custom_call_target="tpu_custom_call" | custom-call | tf_op jit(solution)/shard_map/pallas_call | solution.py:904
  885.9 1.9 slice_bitcast_fusion.1
  887.8 2.0 multiply_reduce_fusion.2
  895.1 2.7 fusion.5
  899.8 17.0 %shard_map.289 = (f32[1,288]{1,0:T(1,128)S(1)}, f32[8,128]{1,0:T(8,128)S(1)}) custom-call(f32[32,1,288]{2,1,0:T(1,128)S(1)} %reshape.423.terms, f32[8,128]{1,0:T(8,128)S(1)} %broadcast_in_dim.51.square), custom_call_target="tpu_custom_call" | custom-call | tf_op jit(solution)/shard_map/pallas_call | solution.py:1038
  918.9 3.4 multiply_subtract_fusion.2
  922.3 2.4 multiply_subtract_fusion.1
  926.9 19.4 %multiply_subtract_fusion = (f32[3,288,2304]{2,1,0:T(8,128)}, f32[3,288,2304]{2,1,0:T(8,128)}, f32[3,288,2304]{2,1,0:T(8,128)}) fusion(f32[3,288,2304]{2,1,0:T(8,128)} %param.24, f32[]{:T(128)S(6)} %min.118, f32[1,288,2304]{2,1,0:T(8,128)S(1)} %copy-done.9, f32[1,288,2304]{2,1,0:T(8,128)S(1)} %bitcast.121, f32[1,288,2304]{2,1,0:T(8,128)S(1)} %bitcast.120, ...), kind=kLoop, calls=%fused_computation.13 | loop fusion | flops 31850496 | bytes 55738372 | tf_op jit(solution)/shard_map/sub | solution.py:101
  (145 shorter events, 44.0 us)
Async XLA Ops:
  0.6 19.4 %copy-start.8 = (f32[224,2304]{1,0:T(8,128)S(1)}, f32[224,2304]{1,0:T(8,128)}, u32[]{:S(2)}) copy-start(f32[224,2304]{1,0:T(8,128)} %inputs.3) | copy-start | bytes 6193156
  0.7 19.7 %copy-start.13 = (f32[2,288,512]{2,1,0:T(8,128)S(1)}, f32[2,288,512]{2,1,0:T(8,128)}, u32[]{:S(2)}) copy-start(f32[2,288,512]{2,1,0:T(8,128)} %param.22) | copy-start | bytes 3538948
  122.7 8.4 copy-start.24
  122.7 9.0 copy-start.28
  123.7 249.1 %collective-permute-start.3 = (bf16[288,1152]{1,0:T(8,128)(2,1)S(1)}, bf16[288,1152]{1,0:T(8,128)(2,1)S(1)}, u32[]{:S(2)}, u32[]{:S(2)}) collective-permute-start(bf16[288,1152]{1,0:T(8,128)(2,1)S(1)} %bitcast.124), channel_id=1, source_target_pairs={{0,4},{4,0},{8,12},{12,8},{16,20},{20,16},{24,28},{28,24},{1,5},{5... | collective-permute-start | bytes 1990664 | tf_op jit(solution)/shard_map/ppermute | solution.py:1054
  125.0 217.0 %collective-permute-start.1 = (bf16[288,1152]{1,0:T(8,128)(2,1)S(1)}, bf16[288,1152]{1,0:T(8,128)(2,1)S(1)}, u32[]{:S(2)}, u32[]{:S(2)}) collective-permute-start(bf16[288,1152]{1,0:T(8,128)(2,1)S(1)} %bitcast.125), channel_id=1, source_target_pairs={{0,16},{4,20},{8,24},{12,28},{16,0},{20,4},{24,8},{28,12},{1,17},{... | collective-permute-start | bytes 1990664 | tf_op jit(solution)/shard_map/ppermute | solution.py:1058
  127.2 214.8 %collective-permute-start.2 = (bf16[288,1152]{1,0:T(8,128)(2,1)}, bf16[288,1152]{1,0:T(8,128)(2,1)S(1)}, u32[]{:S(2)}, u32[]{:S(2)}) collective-permute-start(bf16[288,1152]{1,0:T(8,128)(2,1)} %select_bitcast_fusion), channel_id=1, source_target_pairs={{0,8},{4,12},{8,16},{12,20},{16,24},{20,28},{24,0},{28,4},{1,9},{5... | collective-permute-start | bytes 1990664 | tf_op jit(solution)/shard_map/ppermute | solution.py:1058
  128.2 213.9 %collective-permute-start = (bf16[288,1152]{1,0:T(8,128)(2,1)}, bf16[288,1152]{1,0:T(8,128)(2,1)S(1)}, u32[]{:S(2)}, u32[]{:S(2)}) collective-permute-start(bf16[288,1152]{1,0:T(8,128)(2,1)} %select_bitcast_fusion), channel_id=1, source_target_pairs={{0,24},{4,28},{8,0},{12,4},{16,8},{20,12},{24,16},{28,20},{1,25},{... | collective-permute-start | bytes 1990664 | tf_op jit(solution)/shard_map/ppermute | solution.py:1058
  137.0 275.1 %copy-start.6 = (f32[224,1]{1,0:T(8,128)}, f32[224,1]{1,0:T(8,128)S(1)}, u32[]{:S(2)}) copy-start(f32[224,1]{1,0:T(8,128)S(1)} %copy.39.live) | copy-start | bytes 2692
  137.1 8.6 copy-start.22
  342.0 49.0 %collective-permute-start.6 = (bf16[288,1152]{1,0:T(8,128)(2,1)S(1)}, bf16[288,1152]{1,0:T(8,128)(2,1)S(1)}, u32[]{:S(2)}, u32[]{:S(2)}) collective-permute-start(bf16[288,1152]{1,0:T(8,128)(2,1)S(1)} %collective-permute-done), channel_id=1, source_target_pairs={{0,4},{4,0},{8,12},{12,8},{16,20},{20,16},{24,28},{28,24},{1,5},{5... | collective-permute-start | bytes 1990664 | tf_op jit(solution)/shard_map/ppermute | solution.py:1054
  342.1 47.2 %collective-permute-start.5 = (bf16[288,1152]{1,0:T(8,128)(2,1)S(1)}, bf16[288,1152]{1,0:T(8,128)(2,1)S(1)}, u32[]{:S(2)}, u32[]{:S(2)}) collective-permute-start(bf16[288,1152]{1,0:T(8,128)(2,1)S(1)} %collective-permute-done.1), channel_id=1, source_target_pairs={{0,4},{4,0},{8,12},{12,8},{16,20},{20,16},{24,28},{28,24},{1,5},{5... | collective-permute-start | bytes 1990664 | tf_op jit(solution)/shard_map/ppermute | solution.py:1054
  344.1 43.4 %collective-permute-start.4 = (bf16[288,1152]{1,0:T(8,128)(2,1)S(1)}, bf16[288,1152]{1,0:T(8,128)(2,1)S(1)}, u32[]{:S(2)}, u32[]{:S(2)}) collective-permute-start(bf16[288,1152]{1,0:T(8,128)(2,1)S(1)} %collective-permute-done.2), channel_id=1, source_target_pairs={{0,4},{4,0},{8,12},{12,8},{16,20},{20,16},{24,28},{28,24},{1,5},{5... | collective-permute-start | bytes 1990664 | tf_op jit(solution)/shard_map/ppermute | solution.py:1054
  392.0 20.1 %copy-start.5 = (f32[224,2304]{1,0:T(8,128)S(1)}, f32[224,2304]{1,0:T(8,128)}, u32[]{:S(2)}) copy-start(f32[224,2304]{1,0:T(8,128)} %get-tuple-element.85.hid) | copy-start | bytes 6193156
  392.0 20.1 %copy-start.7 = (f32[4,2304]{1,0:T(4,128)S(1)}, f32[4,2304]{1,0:T(4,128)}, u32[]{:S(2)}) copy-start(f32[4,2304]{1,0:T(4,128)} %reshape.415.gains) | copy-start | bytes 110596
  511.3 64.5 %collective-permute-start.7 = (bf16[4,288,1152]{2,1,0:T(8,128)(2,1)S(1)}, bf16[4,288,1152]{2,1,0:T(8,128)(2,1)}, u32[]{:S(2)}, u32[]{:S(2)}) collective-permute-start(bf16[4,288,1152]{2,1,0:T(8,128)(2,1)S(1)} %dynamic-slice_bitcast_fusion), channel_id=1, source_target_pairs={{0,4},{4,0},{8,12},{12,8},{16,20},{20,16},{24,28},{28,24},{1,5},{5... | collective-permute-start | bytes 7962632 | tf_op jit(solution)/shard_map/ppermute | solution.py:1054
  559.6 16.3 %copy-start.12 = (bf16[2304,1152]{1,0:T(8,128)(2,1)S(1)}, bf16[2304,1152]{1,0:T(8,128)(2,1)}, u32[]{:S(2)}) copy-start(bf16[2304,1152]{1,0:T(8,128)(2,1)} %copy-done.11) | copy-start | bytes 15925252
  575.9 7.2 copy-start.31
  580.1 130.5 %collective-permute-start.10 = (bf16[288,1152]{1,0:T(8,128)(2,1)S(1)}, bf16[288,1152]{1,0:T(8,128)(2,1)S(1)}, u32[]{:S(2)}, u32[]{:S(2)}) collective-permute-start(bf16[288,1152]{1,0:T(8,128)(2,1)S(1)} %get-tuple-element.141), channel_id=1, source_target_pairs={{0,24},{4,28},{8,0},{12,4},{16,8},{20,12},{24,16},{28,20},{1,25},{... | collective-permute-start | bytes 1990664 | tf_op jit(solution)/shard_map/ppermute | solution.py:1058
  580.2 130.4 %collective-permute-start.9 = (bf16[288,1152]{1,0:T(8,128)(2,1)S(1)}, bf16[288,1152]{1,0:T(8,128)(2,1)S(1)}, u32[]{:S(2)}, u32[]{:S(2)}) collective-permute-start(bf16[288,1152]{1,0:T(8,128)(2,1)S(1)} %get-tuple-element.142), channel_id=1, source_target_pairs={{0,16},{4,20},{8,24},{12,28},{16,0},{20,4},{24,8},{28,12},{1,17},{... | collective-permute-start | bytes 1990664 | tf_op jit(solution)/shard_map/ppermute | solution.py:1058
  583.0 127.6 %collective-permute-start.8 = (bf16[288,1152]{1,0:T(8,128)(2,1)S(1)}, bf16[288,1152]{1,0:T(8,128)(2,1)}, u32[]{:S(2)}, u32[]{:S(2)}) collective-permute-start(bf16[288,1152]{1,0:T(8,128)(2,1)S(1)} %get-tuple-element.143), channel_id=1, source_target_pairs={{0,8},{4,12},{8,16},{12,20},{16,24},{20,28},{24,0},{28,4},{1,9},{5... | collective-permute-start | bytes 1990664 | tf_op jit(solution)/shard_map/ppermute | solution.py:1058
  710.7 179.2 %copy-start.25 = (f32[1,2304]{1,0:T(1,128)S(1)}, f32[1,2304]{1,0:T(1,128)}, u32[]{:S(2)}) copy-start(f32[1,2304]{1,0:T(1,128)} %get-tuple-element.108) | copy-start | bytes 27652
  710.7 179.2 %copy-start.26 = (f32[1,2304]{1,0:T(1,128)S(1)}, f32[1,2304]{1,0:T(1,128)}, u32[]{:S(2)}) copy-start(f32[1,2304]{1,0:T(1,128)} %get-tuple-element.109) | copy-start | bytes 27652
  710.7 180.1 %copy-start.23 = (f32[8,1152]{1,0:T(8,128)S(1)}, f32[8,1152]{1,0:T(8,128)}, u32[]{:S(2)}) copy-start(f32[8,1152]{1,0:T(8,128)} %get-tuple-element.111) | copy-start | bytes 110596
  893.4 24.8 %copy-start.27 = (f32[288]{0:T(512)S(1)}, f32[288]{0:T(512)}, u32[]{:S(2)}) copy-start(f32[288]{0:T(512)} %param.25) | copy-start | bytes 3460
  893.4 24.8 %copy-start.29 = (f32[288]{0:T(512)S(1)}, f32[288]{0:T(512)}, u32[]{:S(2)}) copy-start(f32[288]{0:T(512)} %param.33) | copy-start | bytes 3460
  893.4 24.8 %copy-start.30 = (f32[288]{0:T(512)S(1)}, f32[288]{0:T(512)}, u32[]{:S(2)}) copy-start(f32[288]{0:T(512)} %param.29) | copy-start | bytes 3460
  895.1 27.1 %copy-start.14 = (f32[2,288,512]{2,1,0:T(8,128)S(1)}, f32[2,288,512]{2,1,0:T(8,128)}, u32[]{:S(2)}) copy-start(f32[2,288,512]{2,1,0:T(8,128)} %param.22) | copy-start | bytes 3538948
  918.2 4.1 copy-start.17
  918.2 4.1 copy-start.18
  918.2 4.1 copy-start.20
  922.3 4.6 copy-start.16
  (11 other events, 26.2 us)

commit v3 on v2

--- a/solution.py
+++ b/solution.py
@@ -30,18 +30,22 @@
 F32 = jnp.float32
 
 
-def quantize(master, fan_in, selector):
-    return quantize_by(master, jnp.float32(1.0 / (32.0 * math.sqrt(fan_in))), selector)
-
-
-def quantize_by(master, step, selector):
-    spacing = jnp.where(selector == 0, 1.0, jnp.where(selector == 1, 16.0, 64.0)).astype(F32)
+def code_spacing(selector):
+    return jnp.where(selector == 0, 1.0, jnp.where(selector == 1, 16.0, 64.0)).astype(F32)
+
+
+def quantize_values(master, step, spacing):
     half = jnp.floor(spacing * 0.5)
-    inverse = 1.0 / spacing
+    inverse = jnp.where(spacing > 32.0, 1.0 / 64.0, jnp.where(spacing > 8.0, 1.0 / 16.0, 1.0))
     codes = jnp.clip(jnp.floor(master / step + 0.5), -128.0, 127.0)
     top = 128.0 * inverse
     sliced = jnp.clip(jnp.floor((codes + half) * inverse), -top, top - 1.0)
-    return ((sliced * spacing) * step).astype(BF)
+    return (sliced * spacing) * step
+
+
+def quantize(master, fan_in, selector):
+    step = jnp.float32(1.0 / (32.0 * math.sqrt(fan_in)))
+    return quantize_values(master, step, code_spacing(selector)).astype(BF)
 
 
 def inv_root(values):
@@ -151,8 +155,12 @@
             device_id=device, device_id_type=MESH,
         )
         copy.start()
-        self.open.append(copy.wait_send)
+        self.open.append((copy, copy.wait_send))
         return copy
+
+    def sent(self, copy):
+        copy.wait_send()
+        self.open = [entry for entry in self.open if entry[0] is not copy]
 
     def move(self, src, dst):
         at = self.used_local
@@ -162,10 +170,11 @@
         return copy
 
     def keep(self, src, dst):
-        self.open.append(self.move(src, dst).wait)
+        copy = self.move(src, dst)
+        self.open.append((copy, copy.wait))
 
     def close(self):
-        for wait in self.open:
+        for _, wait in self.open:
             wait()
 
 
@@ -202,27 +211,6 @@
     return [(((flat + t) % total) // n_mp, (flat + t) % n_mp) for t in range(1, total)]
 
 
-def spread_kernel(n_dp, n_mp, own, full, ss, rs, ls):
-    net = Net(n_dp, n_mp, ss, rs, ls)
-    others = everyone(n_dp, n_mp, net.i, net.m)
-    net.meet(others)
-    flat = net.i * n_mp + net.m
-    copies = [net.send(own, full.at[flat], device) for device in others]
-    net.keep(own, full.at[flat])
-    for copy in copies:
-        copy.wait_recv()
-    net.close()
-
-
-def spread(n_dp, n_mp, own):
-    total = n_dp * n_mp
-    return call(
-        functools.partial(spread_kernel, n_dp, n_mp),
-        jax.ShapeDtypeStruct((total,) + own.shape, own.dtype), VMEM, [VMEM],
-        [dma(total), dma(total), dma(1)], 1, 16,
-    )(own)
-
-
 def gather_seq_steps(net, own, seq):
     far = net.send(own, seq.at[1], net.x_n)
     near = net.send(own, seq.at[2], net.core_n)
@@ -235,56 +223,6 @@
         both.wait_recv()
 
     return finish
-
-
-def head_kernel(n_dp, n_mp, q, kv, o, tok, wq, wkv, wo, seq, ss, rs, ls):
-    net = Net(n_dp, n_mp, ss, rs, ls)
-    p = net.place()
-    right = (net.ring(p + 1), net.m)
-    left = (net.ring(p + n_dp - 1), net.m)
-    net.meet([right, left, net.x_n, net.core_n])
-    wrows = o.shape[0]
-    hr = upper(wrows)
-    top, low = pl.ds(0, hr), pl.ds(hr, wrows - hr)
-    a = net.send(q, wq.at[net.i], right)
-    b = net.send(kv, wkv.at[net.i], left)
-    finish = gather_seq_steps(net, tok, seq)
-    net.keep(q, wq.at[net.i])
-    net.keep(kv, wkv.at[net.i])
-    net.keep(o, wo.at[net.i])
-    for hop in range(1, n_dp):
-        from_right, from_left = net.ring(p + n_dp - hop), net.ring(p + hop)
-        a.wait_recv()
-        if hop < n_dp - 1:
-            a = net.send(wq.at[from_right], wq.at[from_right], right)
-        else:
-            oa = net.send(o.at[top], wo.at[net.i, top], right)
-        b.wait_recv()
-        if hop < n_dp - 1:
-            b = net.send(wkv.at[from_left], wkv.at[from_left], left)
-        else:
-            ob = net.send(o.at[low], wo.at[net.i, low], left)
-        if hop == n_dp // 2:
-            finish()
-    for hop in range(1, n_dp):
-        from_right, from_left = net.ring(p + n_dp - hop), net.ring(p + hop)
-        oa.wait_recv()
-        if hop < n_dp - 1:
-            oa = net.send(wo.at[from_right, top], wo.at[from_right, top], right)
-        ob.wait_recv()
-        if hop < n_dp - 1:
-            ob = net.send(wo.at[from_left, low], wo.at[from_left, low], left)
-    net.close()
-
-
-def head(n_dp, n_mp, q, kv, o, tok):
-    full = lambda a: jax.ShapeDtypeStruct((n_dp,) + a.shape, BF)
-    count = 4 * n_dp + 8
-    return call(
-        functools.partial(head_kernel, n_dp, n_mp),
-        [full(q), full(kv), full(o), jax.ShapeDtypeStruct((4,) + tok.shape, BF)],
-        [ANY] * 4, [ANY] * 4, [dma(count), dma(count), dma(8)], 2, 16,
-    )(q, kv, o, tok)
 
 
 def gather_pair_steps(net, own, group, split=False):
@@ -362,7 +300,7 @@
     kv_at = slice(kv * HEAD_WIDTH, (kv + 1) * HEAD_WIDTH)
     bent = jnp.tanh(mm_cols(q[at, cols], k[:, kv_at]) * (HEAD_WIDTH**-0.5 / SOFT_CAP))
     raised = jnp.where(allowed, jnp.exp(SOFT_CAP * bent), 0.0)
-    return bent, raised / jnp.sum(raised, axis=-1, keepdims=True)
+    return bent, raised * (1.0 / jnp.sum(raised, axis=-1, keepdims=True))
 
 
 def attend(q, k, v, marks_col, marks_row, mixed):
@@ -393,59 +331,165 @@
 
 
 def chunks(wrows):
+    if wrows % 48 == 0:
+        return tuple((n * wrows // 3, wrows // 3) for n in range(3))
     return ((0, upper(wrows)), (upper(wrows), wrows - upper(wrows)))
 
 
-def mid_kernel(
-    n_dp, n_mp, seq, wq, wkv, wo, cosine, sine, marks_col, marks_row, inputs, gains, low,
-    q, k, v, mixed, att, hid, group, full0, full1,
-    part, r1, s2, r2, own, ss, rs, ls,
+def two_parts(wrows):
+    return ((0, upper(wrows)), (upper(wrows), wrows - upper(wrows)))
+
+
+class Gather:
+    def __init__(self, net, pieces):
+        self.net, self.pieces, self.nj = net, pieces, net.n_dp // 2
+        self.flight, self.relays, self.own = {}, {}, {}
+
+    def out(self, n):
+        net = self.net
+        source, place, parity = self.pieces[n]
+        self.own[n] = net.move(source(net.zl), place(net.i))
+        self.relays[n] = [net.send(source(net.zl), place(net.i), net.y_n)]
+        for d in range(1, self.nj):
+            self.flight[n, d] = net.send(source((net.j + d) % self.nj % 2), place(net.i), net.z_at(d))
+
+    def on(self, n):
+        net = self.net
+        _, place, _ = self.pieces[n]
+        for d in range(1, self.nj):
+            self.flight[n, d].wait_recv()
+            at = ((net.j + self.nj - d) % self.nj) * 2 + net.y
+            self.relays[n].append(net.send(place(at), place(at), net.y_n))
+
+    def done(self, n):
+        self.own.pop(n).wait()
+        for copy in self.relays.pop(n):
+            copy.wait_recv()
+
+
+def all_of_dp(net):
+    return [net.x_n, net.core_n] + [((net.i + t) % net.n_dp, net.m) for t in range(1, net.n_dp)]
+
+
+def open_kernel(
+    n_dp, n_mp, low_q, low_kv, low_o, w_mlp, width_mlp, cosine, sine, marks_col, marks_row, inputs, own_gains,
+    q, k, v, mixed, att, hid, gains, group, full0, full1, full2, out_q, out_kv, out_o, out_seq,
+    wq, wkv, wo, seq, part, r1, r2, own, got_gains, masters, lows, ss, rs, ls,
 ):
     net = Net(n_dp, n_mp, ss, rs, ls)
-    net.meet(pair_partners(net, True))
-    nj = n_dp // 2
-    full = (full0, full1)
+    p = net.place()
+    right = (net.ring(p + 1), net.m)
+    left = (net.ring(p + n_dp - 1), net.m)
     rows = inputs.shape[0]
     wrows, width = full0.shape[1:]
+    others = everyone(n_dp, n_mp, net.i, net.m)
+    net.meet(others)
+    flat = net.i * n_mp + net.m
+    loads = [net.move(w_mlp.at[n], masters.at[n]) for n in range(3)]
+
+    def block(ref, at):
+        return ref.at[pl.ds(pl.multiple_of(at * wrows, 8), wrows)]
+
+    def lot(n):
+        return seq.at[pl.ds(n * rows, rows)]
+
+    def piece(ref, at, part):
+        first, count = part
+        return ref.at[pl.ds(pl.multiple_of(at * wrows + first, 8), count)]
+
+    parts = two_parts(wrows)
+    flight = {}
+    for cut in parts:
+        for lane, (ref, low, device) in enumerate(((wq, low_q, right), (wkv, low_kv, left))):
+            flight[cut, lane] = net.send(low.at[pl.ds(*cut)], piece(ref, net.i, cut), device)
+    spread = [net.send(own_gains, got_gains.at[flat], device) for device in others]
+    net.move(own_gains, got_gains.at[flat]).wait()
+    for copy in spread:
+        copy.wait_recv()
+    per_norm = n_dp * n_mp // NORMS
+    for n in range(NORMS):
+        gains[n : n + 1] = jnp.concatenate([got_gains[n * per_norm + t] for t in range(per_norm)], 1)
+    g0 = 1.0 + gains[0:1]
+
+    def norm_rows(at, state):
+        own[at] = (inputs[at] * inv_root(inputs[at]) * g0).astype(BF)
+        return state
+
+    by_rows(rows, norm_rows)
+    far = net.send(own, lot(1), net.x_n)
+    near = net.send(own, lot(2), net.core_n)
+
+    def quantize_part(n):
+        loads[n].wait()
+        spacing = width_mlp[...]
+        step = jnp.float32(1.0 / (32.0 * math.sqrt(FF if n == 2 else D)))
+
+        def body(at, state, count):
+            lows[n, at] = quantize_values(masters[n, at], step, spacing).astype(BF)
+            return state
+
+        in_steps(wrows, body)
+
+    own_parts = [net.move(own, lot(0)), net.move(low_q, block(wq, net.i)), net.move(low_kv, block(wkv, net.i))]
     half = lambda which: pl.ds(pl.multiple_of(which * width, width), width)
-    pieces = [(w, pl.ds(first, count)) for w in (0, 1) for first, count in chunks(wrows)]
-    flight, relays = {}, []
-
-    def weights_out(n):
-        w, at = pieces[n]
-        own_half = low.at[w, at, half(net.zl)]
-        net.keep(own_half, full[w].at[net.i, at])
-        relays.append(net.send(own_half, full[w].at[net.i, at], net.y_n))
-        for d in range(1, nj):
-            flight[n, d] = net.send(
-                low.at[w, at, half(((net.j + d) % nj) % 2)], full[w].at[net.i, at], net.z_at(d)
-            )
-
-    def weights_on(n):
-        w, at = pieces[n]
-        for d in range(1, nj):
-            flight[n, d].wait_recv()
-            source = ((net.j + nj - d) % nj) * 2 + net.y
-            relays.append(net.send(full[w].at[source, at], full[w].at[source, at], net.y_n))
-
-    weights_out(0)
-    weights_out(1)
+    pieces = [(lambda which: low_o, lambda at: block(wo, at), 1)]
+
+    def add_piece(ref, full, first, count):
+        rows_at = pl.ds(first, count)
+        pieces.append((lambda which: ref.at[rows_at, half(which)], lambda at: full.at[at, rows_at], 2))
+
+    for ref, full in ((lows.at[0], full0), (lows.at[1], full1), (lows.at[2], full2)):
+        for first, count in chunks(wrows):
+            add_piece(ref, full, first, count)
+    weights = Gather(net, pieces)
+    for hop in range(1, n_dp):
+        from_right, from_left = net.ring(p + n_dp - hop), net.ring(p + hop)
+        for cut in parts:
+            for lane, (ref, at, device) in enumerate(((wq, from_right, right), (wkv, from_left, left))):
+                flight[cut, lane].wait_recv()
+                if hop < n_dp - 1:
+                    flight[cut, lane] = net.send(piece(ref, at, cut), piece(ref, at, cut), device)
+        if hop == n_dp // 2:
+            far.wait_recv()
+            both = net.send(lot(1), lot(3), net.core_n)
+        if hop in (1, 2, 3):
+            quantize_part(hop - 1)
+        if hop == n_dp - 2:
+            weights.out(0)
+    weights.out(1)
+    weights.out(2)
+    near.wait_recv()
+    both.wait_recv()
+    for copy in own_parts:
+        copy.wait()
+    net.sent(far)
+    net.sent(near)
+    for ref, result in ((wq, out_q), (wkv, out_kv), (seq, out_seq)):
+        net.keep(ref, result)
     project(seq, wq, wkv, cosine, sine, q, k, v)
     attend(q, k, v, marks_col, marks_row, mixed)
+    def step(n):
+        if n < len(pieces):
+            weights.on(n)
+            if n + 3 < len(pieces):
+                weights.out(n + 3)
+
+    step(0)
+    weights.done(0)
+    net.keep(wo, out_o)
     out_project(mixed, wo, part)
     c1 = net.send(part.at[3], r1.at[1], net.core_n)
     c0 = net.send(part.at[2], r1.at[0], net.core_n)
     c1.wait_recv()
 
-    def first(at, state):
-        s2[at] = (part[1, at].astype(F32) + r1[1, at].astype(F32)).astype(BF)
+    def first_rows(at, state):
+        part[1, at] = (part[1, at].astype(F32) + r1[1, at].astype(F32)).astype(BF)
         return state
 
-    by_rows(rows, first)
-    x = net.send(s2, r2, net.x_n)
+    by_rows(rows, first_rows)
+    x = net.send(part.at[1], r2, net.x_n)
     c0.wait_recv()
-    weights_on(0)
-    weights_out(2)
+    step(1)
     x.wait_recv()
     g1, g2 = 1.0 + gains[1:2], 1.0 + gains[2:3]
 
@@ -459,40 +503,47 @@
 
     by_rows(rows, second)
     finish = gather_pair_steps(net, own, group)
-    weights_on(1)
-    weights_out(3)
-    finish(lambda: weights_on(2))
-    weights_on(3)
-    for copy in relays:
-        copy.wait_recv()
+    step(2)
+    step(3)
+    finish(lambda: (step(4), step(5)))
+    for n in range(6, len(pieces)):
+        step(n)
+    for n in range(1, len(pieces)):
+        weights.done(n)
     net.close()
 
 
-def mid(n_dp, n_mp, seq, wq, wkv, wo, cosine, sine, marks_col, marks_row, inputs, gains, low):
+def open_layer(n_dp, n_mp, low_q, low_kv, low_o, w_mlp, width_mlp, cosine, sine, marks_col, marks_row, inputs, gains):
     rows = inputs.shape[0]
     nj = n_dp // 2
-    count = 16 + 8 * nj
+    total_devices = n_dp * n_mp
+    count = 24 + 4 * n_dp + 20 * nj + total_devices
     block = (rows, D)
-    wrows, width = low.shape[1], low.shape[2] // 2
-    kv_cols = wkv.shape[1] // 2
-    many = lambda n: pltpu.VMEM((n,) + block, BF)
+    wrows, width = w_mlp.shape[1], w_mlp.shape[2] // 2
+    cols, kv_cols = low_q.shape[1], low_kv.shape[1] // 2
+    vm = lambda *shape: pltpu.VMEM(shape, BF)
     bf = lambda *shape: jax.ShapeDtypeStruct(shape, BF)
-    total = seq.shape[0]
+    total = 4 * rows
+    f32 = jax.ShapeDtypeStruct(block, F32)
+    full = bf(n_dp, wrows, width)
     return call(
-        functools.partial(mid_kernel, n_dp, n_mp),
+        functools.partial(open_kernel, n_dp, n_mp),
         [
-            bf(total, wq.shape[1]), bf(total, kv_cols), bf(total, kv_cols), bf(total, wq.shape[1]),
-            jax.ShapeDtypeStruct(block, F32), jax.ShapeDtypeStruct(block, F32),
-            bf(8, *block), bf(n_dp, wrows, width), bf(n_dp, wrows, width),
+            bf(total, cols), bf(total, kv_cols), bf(total, kv_cols), bf(total, cols), f32, f32,
+            jax.ShapeDtypeStruct((NORMS, D), F32),
+            bf(8, *block), full, full, full, bf(D, cols), bf(D, 2 * kv_cols), bf(D, cols), bf(total, D),
         ],
-        [VMEM] * 6 + [ANY] * 3, [VMEM] * 10 + [ANY],
-        [many(4), many(2), pltpu.VMEM(block, BF), pltpu.VMEM(block, BF), pltpu.VMEM(block, BF),
-         dma(count), dma(count), dma(8)],
-        3, 56,
-    )(seq, wq, wkv, wo, cosine, sine, marks_col, marks_row, inputs, gains, low)
-
-
-def reduce_pair_steps(net, near, far, r1, s2, r2, s3, r3, rows, loaded, split=False):
+        [VMEM] * 7 + [ANY] * 8, [ANY] * 4 + [VMEM] * 7,
+        [
+            vm(D, cols), vm(D, 2 * kv_cols), vm(D, cols), vm(total, D), vm(4, *block), vm(2, *block), vm(*block),
+            vm(*block), pltpu.VMEM((total_devices,) + gains.shape, F32), pltpu.VMEM(w_mlp.shape, F32),
+            vm(*w_mlp.shape), dma(count), dma(count), dma(32),
+        ],
+        2, 60,
+    )(low_q, low_kv, low_o, w_mlp, width_mlp, cosine, sine, marks_col, marks_row, inputs, gains)
+
+
+def reduce_pair_steps(net, near, far, r1, s2, r2, s3, r3, rows, loaded, split=False, hooks=()):
     cores = {k: net.send(far.at[k], r1.at[k], net.core_n) for k in (3, 2, 1, 0)}
     plan = [(pl.ds(0, D // 2 if split else D), (3, 2), net.x_n, 1, net.z_n)]
     if split:
@@ -515,6 +566,8 @@
     for k in (0,) if split else (1, 0):
         cores[k].wait_recv()
     last = []
+    if hooks:
+        hooks[0]()
     for part, (cols, blocks, _, second, device) in enumerate(plan):
         firsts[part, 0].wait_recv()
 
@@ -526,6 +579,8 @@
 
         by_rows(rows, add)
         last.append(net.send(s3.at[:, cols], r3.at[:, cols], device))
+    if hooks:
+        hooks[1]()
     for part in range(len(plan)):
         firsts[part, 1].wait_recv()
     return last
@@ -599,12 +654,12 @@
     def __init__(self, net, grads, stay, came, last):
         self.net, self.grads, self.stay, self.came, self.last = net, grads, stay, came, last
         self.nj, self.wrows, self.width = came.shape
-        self.turns = list(range(1, self.nj)) + [0]
+        self.turns = sorted(range(1, self.nj), key=lambda d: abs(d - self.nj // 2)) + [0]
         self.ys, self.moves, self.zs = {}, {}, {}
 
-    def along_y(self):
+    def along_y(self, turns=None):
         net = self.net
-        for d in self.turns:
+        for d in self.turns if turns is None else turns:
             at = (net.j + d) % self.nj
             self.ys[d] = net.send(self.grads.at[at, 1 - net.y], self.came.at[d], net.y_n)
             self.moves[d] = net.move(self.grads.at[at, net.y], self.stay.at[d])
@@ -635,16 +690,12 @@
                 both[d % 2] = both[d % 2] + self.last[d - 1, at].astype(F32)
             for parity in range(2):
                 total[parity, at] = both[parity]
-                sq = both[parity] * both[parity]
-                for r in range(0, step, 8):
-                    state = state + sq[r : r + 8]
             return state
 
-        square = in_steps(self.wrows, collect, jnp.zeros((8, self.width), F32))
+        in_steps(self.wrows, collect)
         for parity in range(2):
             half = (self.net.zl + parity) % 2
             self.net.keep(total.at[parity], sums.at[:, pl.ds(pl.multiple_of(half * self.width, self.width), self.width)])
-        return square
 
     def whole(self, out):
         self.landed()
@@ -667,9 +718,9 @@
 
 
 def back_kernel(
-    n_dp, n_mp, part, hid, att, gains, out_grad, live, grads,
-    ghid, dg1, dg2, seq, sums, squares,
-    near, r1, s2, r2, s3, r3, own, stay, came, last, total, ss, rs, ls,
+    n_dp, n_mp, part, hid, att, gains, out_grad, live, grads, grads_up,
+    ghid, dg1, dg2, seq, sums, sums_up,
+    near, r1, s2, r2, s3, r3, own, stay, came, last, ustay, ucame, ulast, total, ss, rs, ls,
 ):
     net = Net(n_dp, n_mp, ss, rs, ls)
     nj = n_dp // 2
@@ -678,9 +729,13 @@
     far = part.at[pl.ds(4, 4)]
     loaded = net.move(part.at[pl.ds(0, 4)], near)
     weight = Scatter(net, grads, stay, came, last)
+    weight_up = Scatter(net, grads_up, ustay, ucame, ulast)
     weight.along_y()
-    last_sums = reduce_pair_steps(net, near, far, r1, s2, r2, s3, r3, rows, loaded)
-    weight.along_z(weight.turns[:2])
+    last_sums = reduce_pair_steps(
+        net, near, far, r1, s2, r2, s3, r3, rows, loaded, False,
+        (lambda: weight.along_z(weight.turns[:1]), lambda: weight.along_z(weight.turns[1:2])),
+    )
+    weight_up.along_y()
     for copy in last_sums:
         copy.wait_recv()
     g1, g2 = 1.0 + gains[1:2], 1.0 + gains[2:3]
@@ -700,29 +755,33 @@
     dg2[...] = done2
     finish = gather_seq_steps(net, own, seq)
     weight.along_z(weight.turns[2:])
+    weight_up.along_z(weight_up.turns[:1])
     finish()
-    squares[...] = weight.halves(total, sums)
+    weight_up.along_z(weight_up.turns[1:2])
+    weight.halves(total.at[0], sums)
+    weight_up.along_z(weight_up.turns[2:])
+    weight_up.halves(total.at[1], sums_up)
     net.close()
 
 
-def back(n_dp, n_mp, part, hid, att, gains, out_grad, live, grads):
+def back(n_dp, n_mp, part, hid, att, gains, out_grad, live, grads, grads_up):
     rows = hid.shape[0]
     block = (rows, D)
     nj = n_dp // 2
     _, _, wrows, width = grads.shape
-    count = 24 + 3 * nj
+    count = 24 + 6 * nj
     return call(
         functools.partial(back_kernel, n_dp, n_mp),
         [
             jax.ShapeDtypeStruct(block, F32), jax.ShapeDtypeStruct((1, D), F32), jax.ShapeDtypeStruct((1, D), F32),
             jax.ShapeDtypeStruct((4,) + block, BF), jax.ShapeDtypeStruct((wrows, 2 * width), F32),
-            jax.ShapeDtypeStruct((8, width), F32),
+            jax.ShapeDtypeStruct((wrows, 2 * width), F32),
         ],
-        [VMEM, VMEM, VMEM, ANY, ANY, VMEM], [ANY, VMEM, VMEM, VMEM, VMEM, VMEM, ANY],
-        pair_scratch(rows) + scatter_scratch(nj, wrows, width)
-        + [pltpu.VMEM((2, wrows, width), F32), dma(count), dma(count), dma(10 + nj)],
-        5, 58,
-    )(part, hid, att, gains, out_grad, live, grads)
+        [VMEM, VMEM, VMEM, ANY, ANY, ANY], [ANY, VMEM, VMEM, VMEM, VMEM, VMEM, ANY, ANY],
+        pair_scratch(rows) + scatter_scratch(nj, wrows, width) * 2
+        + [pltpu.VMEM((2, 2, wrows, width), F32), dma(count), dma(count), dma(12 + 2 * nj)],
+        5, 60,
+    )(part, hid, att, gains, out_grad, live, grads, grads_up)
 
 
 def attend_back(q, k, v, gm, marks_col, marks_row, cosine, sine, dq, dk, dv, tiles):
@@ -765,10 +824,10 @@
 
 def close_kernel(
     n_dp, n_mp, seq_grad, seq_normed, q, k, v, mixed, wo, wq, wkv, cosine, sine, marks_col, marks_row,
-    inputs, gains, ghid, grads,
-    gin, dg0, sum_q, sum_kv, sum_o, sums, squares,
+    inputs, gains, ghid,
+    gin, dg0, sum_q, sum_kv, sum_o,
     tokens, normed, wa, gm, dq, dk, dv, dkv, go, gq, gkv, got_q, got_kv, r1, r2,
-    stay, came, last, total, ostay, ocame, olast, ss, rs, ls,
+    ostay, ocame, olast, ss, rs, ls,
 ):
     net = Net(n_dp, n_mp, ss, rs, ls)
     p = net.place()
@@ -777,11 +836,7 @@
     nj = n_dp // 2
     rows = inputs.shape[0]
     seq_len, wrows = tokens.shape[0], sum_q.shape[0]
-    net.meet(
-        [net.x_n, net.core_n] + [((net.i + t) % n_dp, net.m) for t in range(1, n_dp)]
-    )
-    weight = Scatter(net, grads, stay, came, last)
-    weight.along_y()
+    net.meet(all_of_dp(net))
     token_load = net.move(seq_grad, tokens)
     wa_load = net.move(wo, wa)
     normed_load = net.move(seq_normed, normed)
@@ -800,9 +855,9 @@
     out = Scatter(net, go, ostay, ocame, olast)
     out.along_y()
     attend_back(q, k, v, gm, marks_col, marks_row, cosine, sine, dq, dk, dv, (0, 2))
-    weight.along_z(weight.turns[:2])
+    out.along_z(out.turns[:1])
     attend_back(q, k, v, gm, marks_col, marks_row, cosine, sine, dq, dk, dv, (2, 4))
-    weight.along_z(weight.turns[2:])
+    out.along_z(out.turns[1:])
     kv_cols = k.shape[1]
     half = HEAD_WIDTH // 2
 
@@ -819,32 +874,37 @@
     weight_grad(normed, dq, gq)
     weight_grad(normed, dkv, gkv)
 
-    def block(at):
-        return pl.ds(pl.multiple_of(net.ring(p + 2 * n_dp + at) * wrows, 8), wrows)
+    def block(at, part):
+        return pl.ds(pl.multiple_of(net.ring(p + 2 * n_dp + at) * wrows + part[0], 8), part[1])
 
     lanes = ((gq, got_q, sum_q, right, -1), (gkv, got_kv, sum_kv, left, 1))
-    flight = [net.send(terms.at[block(way)], got.at[0], device) for terms, got, _, device, way in lanes]
+    parts = two_parts(wrows)
+    flight = {}
+    for part in parts:
+        for lane, (terms, got, _, device, way) in enumerate(lanes):
+            flight[lane, part] = net.send(terms.at[block(way, part)], got.at[0, pl.ds(*part)], device)
 
     def hop(n):
         end = n == n_dp - 1
-        for lane, (terms, got, result, device, way) in enumerate(lanes):
-            flight[lane].wait_recv()
-            first = net.ring(p + 2 * n_dp + way * (1 + n)) * wrows
-
-            def add(t, state, step):
-                at = pl.ds(pl.multiple_of(first + t * step, 8), step)
-                here = pl.ds(pl.multiple_of(t * step, 8), step)
-                value = got[n - 1, here].astype(F32) + terms[at].astype(F32)
-                if end:
-                    result[here] = value
-                else:
-                    terms[at] = value.astype(BF)
-                return state
-
-            step = 16 if wrows % 16 == 0 else 8
-            lax.fori_loop(0, wrows // step, lambda t, state: add(t, state, step), 0)
-            if not end:
-                flight[lane] = net.send(terms.at[block(way * (1 + n))], got.at[n], device)
+        for part in parts:
+            for lane, (terms, got, result, device, way) in enumerate(lanes):
+                flight[lane, part].wait_recv()
+                first = net.ring(p + 2 * n_dp + way * (1 + n)) * wrows
+
+                def add(here, state, step, first=first, terms=terms, got=got, result=result):
+                    at = pl.ds(pl.multiple_of(first + here.start, 8), step)
+                    value = got[n - 1, here].astype(F32) + terms[at].astype(F32)
+                    if end:
+                        result[here] = value
+                    else:
+                        terms[at] = value.astype(BF)
+                    return state
+
+                in_steps(part[1], add, 0, part[0])
+                if not end:
+                    flight[lane, part] = net.send(
+                        terms.at[block(way * (1 + n), part)], got.at[n, pl.ds(*part)], device
+                    )
 
     wa_load.wait()
     wide = D // 3
@@ -870,7 +930,6 @@
     x = net.send(tokens.at[pl.ds(rows, rows)], r2, net.x_n)
     c0.wait_recv()
     hop(2)
-    out.along_z(out.turns)
     hop(3)
     x.wait_recv()
     ghid_load.wait()
@@ -885,20 +944,19 @@
     dg0[...] = by_rows(rows, rows_in, jnp.zeros((1, D), F32))
     for n in range(4, n_dp - 1):
         hop(n)
-    squares[...] = weight.halves(total, sums)
+    out.whole(sum_o)
     hop(n_dp - 1)
-    out.whole(sum_o)
     net.close()
 
 
 def close(n_dp, n_mp, seq_grad, seq_normed, q, k, v, mixed, wo, wq, wkv, cosine, sine, marks_col, marks_row,
-          inputs, gains, ghid, grads):
+          inputs, gains, ghid):
     rows = inputs.shape[0]
     nj = n_dp // 2
-    _, _, wrows, width = grads.shape
+    wrows = D // n_dp
     cols, kv_cols = q.shape[1], k.shape[1]
     seq_len = q.shape[0]
-    count = 16 + 6 * nj + 2 * n_dp
+    count = 16 + 6 * nj + 4 * n_dp
     vm = lambda *shape: pltpu.VMEM(shape, BF)
     small = jax.ShapeDtypeStruct((wrows, cols), F32)
     return call(
@@ -906,21 +964,19 @@
         [
             jax.ShapeDtypeStruct((rows, D), F32), jax.ShapeDtypeStruct((1, D), F32), small,
             jax.ShapeDtypeStruct((wrows, 2 * kv_cols), F32), small,
-            jax.ShapeDtypeStruct((wrows, 2 * width), F32), jax.ShapeDtypeStruct((8, width), F32),
         ],
-        [VMEM] * 5 + [ANY, VMEM],
-        [ANY, ANY] + [VMEM] * 4 + [ANY, ANY] + [VMEM] * 7 + [ANY, ANY],
+        [VMEM] * 5,
+        [ANY, ANY] + [VMEM] * 4 + [ANY, ANY] + [VMEM] * 7 + [ANY],
         [
             vm(seq_len, D), vm(seq_len, D), vm(D, cols), vm(seq_len, cols), vm(seq_len, cols),
             pltpu.VMEM((seq_len, kv_cols), F32), pltpu.VMEM((seq_len, kv_cols), F32), vm(seq_len, 2 * kv_cols),
             vm(nj, 2, wrows, cols), vm(D, cols), vm(D, 2 * kv_cols),
             vm(n_dp - 1, wrows, cols), vm(n_dp - 1, wrows, 2 * kv_cols), vm(2, rows, D), vm(rows, D),
         ]
-        + scatter_scratch(nj, wrows, width) + [pltpu.VMEM((2, wrows, width), F32)]
         + scatter_scratch(nj, wrows, cols) + [dma(count), dma(count), dma(10 + 2 * nj)],
         6, 60,
     )(seq_grad, seq_normed, q, k, v, mixed, wo, wq, wkv, cosine, sine, marks_col, marks_row,
-      inputs, gains, ghid, grads)
+      inputs, gains, ghid)
 
 
 def plain(kernel, grid, outs, out_specs, in_specs, mb, flops):
@@ -948,37 +1004,30 @@
 GELU = math.sqrt(2.0 / math.pi)
 
 
-def up_kernel(x, wg, wu, gate, up, act):
+def mlp_kernel(x, wg, wu, wd, gate, up, act, part):
     g = mm(x[...], wg[...])
     u = mm(x[...], wu[...])
     gate[...] = g
     up[...] = u
     bend = jnp.tanh(GELU * (g + 0.044715 * (g * g * g)))
-    act[...] = (0.5 * g * (1.0 + bend) * u).astype(BF)
-
-
-def mlp_up(x, wg, wu):
+    a = (0.5 * g * (1.0 + bend) * u).astype(BF)
+    act[...] = a
+    part[...] = mm_cols(a, wd[...]).astype(BF)
+
+
+def mlp(x, wg, wu, wd):
     blocks, rows, _ = x.shape
     width = wg.shape[1]
     shape = (blocks, rows, width)
     return plain(
-        up_kernel, (blocks,),
-        [jax.ShapeDtypeStruct(shape, F32), jax.ShapeDtypeStruct(shape, F32), jax.ShapeDtypeStruct(shape, BF)],
-        [tile(rows, width)] * 3, [tile(rows, D), whole(wg.shape), whole(wu.shape)], 48,
-        4 * blocks * rows * D * width,
-    )(x, wg, wu)
-
-
-def down_kernel(act, wd, part):
-    part[...] = mm_cols(act[...], wd[...]).astype(BF)
-
-
-def mlp_down(act, wd):
-    blocks, rows, width = act.shape
-    return plain(
-        down_kernel, (blocks,), jax.ShapeDtypeStruct((blocks, rows, D), BF),
-        tile(rows, D), [tile(rows, width), whole(wd.shape)], 32, 2 * blocks * rows * D * width,
-    )(act, wd)
+        mlp_kernel, (blocks,),
+        [
+            jax.ShapeDtypeStruct(shape, F32), jax.ShapeDtypeStruct(shape, F32), jax.ShapeDtypeStruct(shape, BF),
+            jax.ShapeDtypeStruct((blocks, rows, D), BF),
+        ],
+        [tile(rows, width)] * 3 + [tile(rows, D)], [tile(rows, D)] + [whole(wg.shape)] * 3, 56,
+        6 * blocks * rows * D * width,
+    )(x, wg, wu, wd)
 
 
 def down_back_kernel(grad, gate, up, wg, wu, wd, dgate, dup, part):
@@ -1008,43 +1057,95 @@
     )(grad, gate, up, wg, wu, wd)
 
 
-def finish_kernel(n_dp, n_mp, terms, square, total_gain, total_square, got, sgot, mine, ss, rs, ls):
+def norm_kernel(
+    n_dp, n_mp, terms, g_gate, g_up, g_down, g_q, g_o, g_kv, gain_sum, norm, *refs,
+):
+    grads, (got, sgot, mine, ss, rs, ls) = refs[:6], refs[6:]
     net = Net(n_dp, n_mp, ss, rs, ls)
     others = everyone(n_dp, n_mp, net.i, net.m)
+    loads = [net.move(src, dst) for src, dst in zip((g_gate, g_up, g_down, g_q, g_o, g_kv), grads)]
     net.meet(others)
     flat = net.i * n_mp + net.m
-    copies = [
-        net.send(terms.at[dp * n_mp + mp], got.at[flat], (dp, mp)) for dp, mp in others
-    ]
-    net.keep(terms.at[flat], got.at[flat])
-    net.open.pop()()
+    copies = [net.send(terms.at[dp * n_mp + mp], got.at[flat], (dp, mp)) for dp, mp in others]
+    own = net.move(terms.at[flat], got.at[flat])
+    square = jnp.zeros((8, 128), F32)
+    for load, grad in zip(loads, grads):
+        load.wait()
+        rows, cols = grad.shape
+
+        def add(t, state, grad=grad, cols=cols):
+            value = grad[pl.ds(pl.multiple_of(t * 8, 8), 8)]
+            value = value * value
+            for n in range(0, cols, 128):
+                state = state + value[:, n : n + 128]
+            return state
+
+        square = lax.fori_loop(0, rows // 8, add, square)
+    own.wait()
     for copy in copies:
         copy.wait_recv()
-    total = lax.fori_loop(0, n_dp * n_mp, lambda t, s: s + got[t], jnp.zeros(got.shape[1:], F32))
-    total_gain[...] = total
-    mine[...] = square[...] + jnp.sum(total * total) * (1.0 / (mine.shape[0] * mine.shape[1]))
+    gain = lax.fori_loop(0, n_dp * n_mp, lambda t, s: s + got[t], jnp.zeros(got.shape[1:], F32))
+    gain_sum[...] = gain
+    mine[...] = square + jnp.sum(gain * gain) * (1.0 / 1024.0)
     copies = [net.send(mine, sgot.at[flat], device) for device in others]
-    net.keep(mine, sgot.at[flat])
-    net.open.pop()()
+    own = net.move(mine, sgot.at[flat])
+    own.wait()
     for copy in copies:
         copy.wait_recv()
-    total_square[...] = lax.fori_loop(0, n_dp * n_mp, lambda t, s: s + sgot[t], jnp.zeros(mine.shape, F32))
+    total = lax.fori_loop(0, n_dp * n_mp, lambda t, s: s + sgot[t], jnp.zeros((8, 128), F32))
+    norm[...] = jnp.broadcast_to(jnp.sqrt(jnp.sum(total, axis=(0, 1), keepdims=True)), (8, 128))
     net.close()
 
 
-def finish_all(n_dp, n_mp, terms, square):
+def norm_all(n_dp, n_mp, terms, grads):
     total = n_dp * n_mp
     shape = terms.shape[1:]
     return call(
-        functools.partial(finish_kernel, n_dp, n_mp),
-        [jax.ShapeDtypeStruct(shape, F32), jax.ShapeDtypeStruct(square.shape, F32)],
-        [VMEM, VMEM], [VMEM, VMEM],
-        [
-            pltpu.VMEM((total,) + shape, F32), pltpu.VMEM((total,) + square.shape, F32),
-            pltpu.VMEM(square.shape, F32), dma(2 * total), dma(2 * total), dma(2),
+        functools.partial(norm_kernel, n_dp, n_mp),
+        [jax.ShapeDtypeStruct(shape, F32), jax.ShapeDtypeStruct((8, 128), F32)],
+        [VMEM] * 2, [VMEM] + [ANY] * 6,
+        [pltpu.VMEM(a.shape, F32) for a in grads]
+        + [
+            pltpu.VMEM((total,) + shape, F32), pltpu.VMEM((total, 8, 128), F32), pltpu.VMEM((8, 128), F32),
+            dma(2 * total), dma(2 * total), dma(8),
         ],
-        7, 16,
-    )(terms, square)
+        7, 32,
+    )(terms, *grads)
+
+
+def adam_kernel(norm, gain_grad, gw, gm, gv, g_gate, g_up, g_down, g_q, g_o, g_kv, *refs):
+    ins, gain_outs, outs = refs[:9], refs[9:12], refs[12:]
+    factor = jnp.minimum(1.0, CLIP_SCALE * math.sqrt(PARAMS) / norm[0:1, 0:1])
+    news = adam_update(gw[...], gm[...], gv[...], gain_grad[...], factor)
+    for out, new in zip(gain_outs, news):
+        out[...] = new
+    kv_cols = ins[6].shape[2]
+    grads = (
+        (lambda: g_gate[...], lambda: g_up[...], lambda: g_down[...]),
+        (lambda: g_q[...], lambda: g_o[...]),
+        (lambda: g_kv[:, :kv_cols], lambda: g_kv[:, kv_cols:]),
+    )
+    for n, group in enumerate(grads):
+        w, m, v = ins[3 * n : 3 * n + 3]
+        for k, grad in enumerate(group):
+            news = adam_update(w[k], m[k], v[k], grad(), factor)
+            for out, new in zip(outs[3 * n : 3 * n + 3], news):
+                out[k] = new
+
+
+def adam_all(norm, gain_grad, gains, grads, states):
+    wrows = grads[0].shape[0]
+    step = 16 if wrows % 16 == 0 else 8
+    like = lambda a: jax.ShapeDtypeStruct(a.shape, F32)
+    fixed = lambda a: pl.BlockSpec(a.shape, lambda t: (0, 0))
+    flat = lambda a: pl.BlockSpec((step, a.shape[1]), lambda t: (t, 0))
+    deep = lambda a: pl.BlockSpec((a.shape[0], step, a.shape[2]), lambda t: (0, t, 0))
+    return plain(
+        adam_kernel, (wrows // step,), [like(a) for a in gains] + [like(a) for a in states],
+        [fixed(a) for a in gains] + [deep(a) for a in states],
+        [fixed(a) for a in (norm, gain_grad) + tuple(gains)] + [flat(a) for a in grads] + [deep(a) for a in states],
+        32, 100,
+    )(norm, gain_grad, *gains, *grads, *states)
 
 
 def build_local(n_dp, n_mp):
@@ -1078,27 +1179,9 @@
         seq_len = segment_ids.shape[1]
         wrows = w_qo.shape[1]
 
-        gain_rows = spread(n_dp, n_mp, norm_gains.reshape(1, -1)).reshape(NORMS, D)
         low_q = quantize(w_qo[0], D, bit_sel[0])
         low_o = quantize(w_qo[1], QW, bit_sel[0])
         low_kv = jnp.concatenate([quantize(w_kv[0], D, bit_sel[1]), quantize(w_kv[1], D, bit_sel[1])], 1)
-        low_up = quantize(w_mlp[:2], D, bit_sel[2])
-        low_down = quantize(w_mlp[2], FF, bit_sel[2])
-        norm_in = rms_norm(inputs, gain_rows[0]).astype(BF)
-        wq, wkv, wo, seq_normed = head(n_dp, n_mp, low_q, low_kv, low_o, norm_in)
-        wq = wq.reshape(D, -1)
-        wkv = wkv.reshape(D, -1)
-        wo = wo.reshape(D, -1)
-        seq_normed = seq_normed.reshape(seq_len, D)
-
-        seq_normed, low_down = lax.optimization_barrier((seq_normed, low_down))
-        halves = low_down.reshape(wrows, 2, -1)
-        same = jnp.where(zl == 0, halves[:, 0], halves[:, 1])
-        other = jnp.where(zl == 0, halves[:, 1], halves[:, 0])
-        down_blocks = {0: y_swap(same)}
-        for d in range(1, nj):
-            down_blocks[d] = z_shift(other if d % 2 else same, d)
-
         order = jnp.stack([m, m ^ 2, m ^ 1, m ^ 3])
 
         def in_order(vector):
@@ -1109,33 +1192,22 @@
         slots = in_order(jnp.arange(seq_len, dtype=jnp.int32))
         segs = in_order(segments)
         pads = in_order(pad_mask[0])
-        kv_cols = wkv.shape[1] // 2
+        kv_cols = w_kv.shape[2]
         half_dim = HEAD_WIDTH // 2
         frequency = ROPE_BASE ** (-jnp.arange(half_dim, dtype=F32) * 2.0 / HEAD_WIDTH)
         angles = positions.astype(F32)[:, None] * frequency[None, :]
         cosine = jnp.cos(angles)
         sine = jnp.sin(angles)
         marks = jnp.stack([segs, slots, pads] + [segs] * 5)
-        query_bf, key_bf, value_bf, mixed_bf, attended, hidden_in, group_ffn, w_gate, w_up = mid(
-            n_dp, n_mp, seq_normed, wq, wkv, wo, cosine, sine, marks.T, marks, inputs, gain_rows, low_up
+        (
+            query_bf, key_bf, value_bf, mixed_bf, attended, hidden_in, gain_rows, group_ffn, w_gate, w_up, w_down,
+            wq, wkv, wo, seq_normed,
+        ) = open_layer(
+            n_dp, n_mp, low_q, low_kv, low_o, w_mlp, code_spacing(bit_sel[2]).reshape(1, 1), cosine, sine,
+            marks.T, marks, inputs, norm_gains.reshape(1, -1),
         )
-        w_gate = w_gate.reshape(D, -1)
-        w_up = w_up.reshape(D, -1)
-        w_down = jnp.zeros((n_dp,) + same.shape, BF)
-
-        def put(block, at):
-            return lax.dynamic_update_index_in_dim(w_down, block, at, 0)
-
-        w_down = put(same, i)
-        w_down = put(down_blocks[0], i + 1 - 2 * y)
-        for d in range(1, nj):
-            got, group_ffn = lax.optimization_barrier((down_blocks[d], group_ffn))
-            at = ((j + nj - d) % nj) * 2
-            w_down = put(got, at + y)
-            w_down = put(y_swap(got), at + 1 - y)
-        w_down = w_down.reshape(D, -1)
-        gate, up, activated = mlp_up(group_ffn, w_gate, w_up)
-        part = mlp_down(activated, w_down)
+        w_gate, w_up, w_down = w_gate.reshape(D, -1), w_up.reshape(D, -1), w_down.reshape(D, -1)
+        gate, up, activated, part = mlp(group_ffn, w_gate, w_up, w_down)
         live = lax.dynamic_slice_in_dim(pad_mask[0], m * rows, rows).astype(F32)[:, None]
         outputs, grad_gain_three, group_grad = turn(
             n_dp, n_mp, part, hidden_in, gain_rows, out_grad, live
@@ -1151,8 +1223,8 @@
         grads_gate, grad_up, down_came = lax.optimization_barrier((grads_gate, grad_up, down_came))
         down_own, down_shifted = scatter_second(down_stay, down_came, j)
         grads_up = mm_rows(flat_ffn, grad_up.reshape(tokens, -1)).astype(BF).reshape(nj, 2, wrows, -1)
-        grad_hidden, grad_gain_one, grad_gain_two, seq_grad, sum_gate, square_gate = back(
-            n_dp, n_mp, part, hidden_in, attended, gain_rows, out_grad, live, grads_gate
+        grad_hidden, grad_gain_one, grad_gain_two, seq_grad, sum_gate, sum_up = back(
+            n_dp, n_mp, part, hidden_in, attended, gain_rows, out_grad, live, grads_gate, grads_up
         )
         seq_grad, down_shifted = lax.optimization_barrier((seq_grad, down_shifted))
         sums = [down_own.astype(F32), 0.0]
@@ -1161,29 +1233,20 @@
         sum_down = jnp.concatenate(
             [jnp.where(zl == 0, sums[0], sums[1]), jnp.where(zl == 0, sums[1], sums[0])], 1
         )
-        grad_in, grad_gain_zero, sum_q, sum_kv, sum_o, sum_up, square_up = close(
+        grad_in, grad_gain_zero, sum_q, sum_kv, sum_o = close(
             n_dp, n_mp, seq_grad.reshape(seq_len, D), seq_normed, query_bf, key_bf, value_bf, mixed_bf,
-            wo, wq, wkv, cosine, sine, marks.T, marks, inputs, gain_rows, grad_hidden, grads_up,
+            wo, wq, wkv, cosine, sine, marks.T, marks, inputs, gain_rows, grad_hidden,
         )
         terms = jnp.concatenate([grad_gain_zero, grad_gain_one, grad_gain_two, grad_gain_three])
-        square = jnp.sum(square_gate + square_up)
-        for part in (sum_q, sum_kv, sum_o, sum_down):
-            square = square + jnp.sum(part * part)
-        square = jnp.broadcast_to(square * (1.0 / 1024.0), (8, 128))
-        sum_gains, squares = finish_all(n_dp, n_mp, terms.reshape(n_dp * n_mp, 1, -1), square)
-        grad_norm = jnp.sqrt(jnp.sum(squares)).reshape(1)
-        factor = jnp.minimum(1.0, CLIP_SCALE * math.sqrt(PARAMS) / grad_norm[0])
-
-        new_w_qo, new_m_qo, new_v_qo = adam_update(w_qo, m_qo, v_qo, jnp.stack([sum_q, sum_o]), factor)
-        new_w_kv, new_m_kv, new_v_kv = adam_update(
-            w_kv, m_kv, v_kv, jnp.stack([sum_kv[:, :kv_cols], sum_kv[:, kv_cols:]]), factor
+        flat_gains = [a.reshape(1, -1) for a in (norm_gains, m_gains, v_gains)]
+        sums = [sum_gate, sum_up, sum_down, sum_q, sum_o, sum_kv]
+        sum_gains, norm = norm_all(n_dp, n_mp, terms.reshape(n_dp * n_mp, 1, -1), sums)
+        news = adam_all(
+            norm, sum_gains, flat_gains, sums, [w_mlp, m_mlp, v_mlp, w_qo, m_qo, v_qo, w_kv, m_kv, v_kv]
         )
-        new_w_mlp, new_m_mlp, new_v_mlp = adam_update(
-            w_mlp, m_mlp, v_mlp, jnp.stack([sum_gate, sum_up, sum_down]), factor
-        )
-        new_gains, new_m_gains, new_v_gains = adam_update(
-            norm_gains, m_gains, v_gains, sum_gains.reshape(-1), factor
-        )
+        grad_norm = norm[0, :1]
+        new_gains, new_m_gains, new_v_gains = [a.reshape(-1) for a in news[:3]]
+        new_w_mlp, new_m_mlp, new_v_mlp, new_w_qo, new_m_qo, new_v_qo, new_w_kv, new_m_kv, new_v_kv = news[3:]
         return (
             outputs, grad_in, grad_norm, new_w_qo, new_w_kv, new_w_mlp, new_gains,
             new_m_qo, new_m_kv, new_m_mlp, new_m_gains, new_v_qo, new_v_kv, new_v_mlp, new_v_gains,

time: 958 us -> 880 us (0.919)
  other arithmetic: 56.3 us -> 15.9 us
  local copies, waits for them, and re-layouts: 40.4 us -> 17.6 us
  waiting for transfers between devices: 13 us -> 0.01 us
    pallas_call x1, Pallas kernels: 173 us -> 116 us  [close(): call(functools.partial(close_kernel, n_dp, n_mp), [jax.ShapeDtypeStruct((...]
    pallas_call x1, Pallas kernels: 112 us -> 153 us  [back(): call(functools.partial(back_kernel, n_dp, n_mp), [jax.ShapeDtypeStruct(bl...]
    sub x4 -> x0, other arithmetic: 25.7 us -> none  [adam_update(): master - LEARN_RATE * (new_first / (jnp.sqrt(new_second) + ADAM_EPSILON)...]
    pallas_call x6 -> x4, Pallas kernels: 357 us -> 376 us  [the longest x1 291 us: open_layer(): call(functools.partial(open_kernel, n_dp, n_mp), [bf(total, cols), bf(tot...]
    unnamed x66 -> x56, local copies, waits for them, and re-layouts: 19.3 us -> 5.09 us
    ppermute x5 -> x1, waiting for transfers between devices: 13 us -> 0.01 us  [y_swap(): return lax.ppermute(value, 'dp', [(k, k ^ 1) for k in range(n_dp)])]
  transfers between devices with their start and end apart: 11 -> 4, of which waited for: 1 -> 0; matrix products, arithmetic and copies ran while one was open for 5% -> 4% of each run, Pallas kernels for 40% -> 23%
where the time goes in v3:
time: 880 us; the launch traced here: 869 us
  Pallas kernels  776 us (88%)
  matrix products  47.5 us (5%)
  local copies, waits for them, and re-layouts  17.6 us (2%)
  other arithmetic  15.9 us (2%)
    pallas_call x1, Pallas kernels, open_layer(): call(functools.partial(open_kernel, n_dp, n_mp), [bf(total, cols), bf(tot...  291 us
    pallas_call x1, Pallas kernels, back(): call(functools.partial(back_kernel, n_dp, n_mp), [jax.ShapeDtypeStruct(bl...  153 us
    pallas_call x1, Pallas kernels, close(): call(functools.partial(close_kernel, n_dp, n_mp), [jax.ShapeDtypeStruct((...  116 us
    pallas_call x1, Pallas kernels, turn(): call(functools.partial(turn_kernel, n_dp, n_mp), [jax.ShapeDtypeStruct(bl...  83.2 us
    pallas_call x1, Pallas kernels, mlp_back(): plain(down_back_kernel, (blocks,), [jax.ShapeDtypeStruct(shape, BF), jax....  48 us
    dot_general x3, matrix products, mm_rows(): lax.dot_general(left, right, (((0,), (0,)), ((), ())), preferred_element_...  47.5 us
    pallas_call x1, Pallas kernels, mlp(): plain(mlp_kernel, (blocks,), [jax.ShapeDtypeStruct(shape, F32), jax.Shape...  43.5 us
    pallas_call x1, Pallas kernels, adam_all(): plain(adam_kernel, (wrows // step,), [like(a) for a in gains] + [like(a)...  26.8 us
  transfers between devices with their start and end apart: 4, of which 0 were waited for; matrix products, arithmetic and copies ran while one was open for 4% of the time, Pallas kernels for 23%

profile of v3, /device:TPU:0, one launch (start us, length us, event | category | flops | bytes accessed | tf_op | source)
XLA Modules:
  0.0 869.5 jit_solution(10688785350829314588)
XLA Ops:
  0.7 1.4 fusion.15
  5.4 1.2 slice.50
  11.6 1.0 copy.34.marks_col
  14.6 1.2 reshape.358.own_gains.gw
  15.8 0.8 fusion.13
  16.7 1.3 fusion.8
  18.1 0.7 pad_maximum_fusion.1.low_kv
  18.8 2.6 multiply_sine_fusion
  21.4 1.3 fusion.7
  22.7 291.3 %shard_map.280 = (bf16[896,512]{1,0:T(8,128)(2,1)}, bf16[896,256]{1,0:T(8,128)(2,1)}, bf16[896,256]{1,0:T(8,128)(2,1)}, bf16[896,512]{1,0:T(8,128)(2,1)}, f32[22...) custom-call(bf16[288,512]{1,0:T(8,128)(2,1)} %get-tuple-element.139., ...), custom_call_target="tpu_custom_call" | custom-call | tf_op jit(solution)/shard_map/pallas_call | solution.py:529
  314.0 43.5 %shard_map.281 = (f32[8,224,1152]{2,1,0:T(8,128)}, f32[8,224,1152]{2,1,0:T(8,128)}, bf16[8,224,1152]{2,1,0:T(8,128)(2,1)}, bf16[8,224,2304]{2,1,0:T(8,128)(2,1)}) custom-call(bf16[8,224,2304]{2,1,0:T(8,128)(2,1)} %get-tuple-element.74.x, bf16[2304,1152]{1,0:T(8,128)(2,1)} %bitcast.78, bf16[2304,1152]{1,0:T(8,128)(2,1)} %bitcast.80, bf16[2304,1152]{1,0:T(8,128)(2,1)} %bitcast.82), custom_call_target="tpu_custom_call" | custom-call | flops 28538044416 | bytes 41943040 | tf_op jit(solution)/shard_map/pallas_call | solution.py:1022
  357.5 83.2 %shard_map.282 = (f32[224,2304]{1,0:T(8,128)S(1)}, f32[1,2304]{1,0:T(1,128)S(1)}, bf16[8,224,2304]{2,1,0:T(8,128)(2,1)}) custom-call(bf16[8,224,2304]{2,1,0:T(8,128)(2,1)} %get-tuple-element.78.part, f32[224,2304]{1,0:T(8,128)S(1)} %copy-done.2, f32[4,2304]{1,0:T(4,128)S(1)} %copy-done.16, f32[224,2304]{1,0:T(8,128)} %out_grad.3, f32[224,1]{1,0:T(8,128)S(1)} %copy.35.live), custom_call_target="tpu_custom_call" | custom-call | tf_op jit(solution)/shard_map/pallas_call | solution.py:637
  440.8 15.6 %fusion = bf16[2304,1152]{1,0:T(8,128)(2,1)} fusion(bf16[8,224,2304]{2,1,0:T(8,128)(2,1)} %get-tuple-element.84.grad, bf16[8,224,1152]{2,1,0:T(8,128)(2,1)S(1)} %copy-done.26), kind=kOutput, calls=%fused_computation.7 | convolution fusion | flops 9515335680 | bytes 17694720 | tf_op jit(solution)/shard_map/dot_general | solution.py:94
  456.4 2.0 dynamic-slice_bitcast_fusion
  458.3 1.9 collective-permute-start
  460.3 48.0 %shard_map.283 = (bf16[8,224,1152]{2,1,0:T(8,128)(2,1)}, bf16[8,224,1152]{2,1,0:T(8,128)(2,1)}, bf16[8,224,2304]{2,1,0:T(8,128)(2,1)}) custom-call(bf16[8,224,2304]{2,1,0:T(8,128)(2,1)} %get-tuple-element.84.grad, f32[8,224,1152]{2,1,0:T(8,128)} %get-tuple-element.85.gate, f32[8,224,1152]{2,1,0:T(8,128)} %get-tuple-element.86.up, ...), custom_call_target="tpu_custom_call" | custom-call | flops 28538044416 | bytes 41943040 | tf_op jit(solution)/shard_map/pallas_call | solution.py:1051
  508.3 16.7 %fusion.1 = bf16[2304,1152]{1,0:T(8,128)(2,1)} fusion(bf16[8,224,2304]{2,1,0:T(8,128)(2,1)} %get-tuple-element.74.x, bf16[8,224,1152]{2,1,0:T(8,128)(2,1)} %get-tuple-element.89), kind=kOutput, calls=%fused_computation.8 | convolution fusion | flops 9515335680 | bytes 17694720 | tf_op jit(solution)/shard_map/dot_general | solution.py:94
  525.0 2.6 fusion.3
  527.6 1.2 dynamic-slice_bitcast_fusion.1
  528.8 2.4 collective-permute-start.1
  531.2 2.4 collective-permute-start.3
  533.6 15.2 %fusion.2 = bf16[2304,1152]{1,0:T(8,128)(2,1)} fusion(bf16[8,224,2304]{2,1,0:T(8,128)(2,1)} %get-tuple-element.74.x, bf16[8,224,1152]{2,1,0:T(8,128)(2,1)S(1)} %copy-done.25), kind=kOutput, calls=%fused_computation.9 | convolution fusion | flops 9515335680 | bytes 17694720 | tf_op jit(solution)/shard_map/dot_general | solution.py:94
  548.8 152.7 %shard_map.284 = (f32[224,2304]{1,0:T(8,128)}, f32[1,2304]{1,0:T(1,128)}, f32[1,2304]{1,0:T(1,128)}, bf16[4,224,2304]{2,1,0:T(8,128)(2,1)}, f32[288,2304]{1,0:T(8,128)}, /*index=5*/f32[288,2304]{1,0:T(8,128)}) custom-call(bf16[8,224,2304]{2,1,0:T(8,128)(2,1)} %get-tuple-element.87.part, f32[224,2304]{1,0:T(8,128)} %get-tuple-element.79.hid, ...), custom_call_target="tpu_custom_call" | custom-call | tf_op jit(solution)/shard_map/pallas_call | solution.py:773
  701.5 115.7 %shard_map.285 = (f32[224,2304]{1,0:T(8,128)}, f32[1,2304]{1,0:T(1,128)}, f32[288,512]{1,0:T(8,128)}, f32[288,512]{1,0:T(8,128)}, f32[288,512]{1,0:T(8,128)}) custom-call(bf16[896,2304]{1,0:T(8,128)(2,1)} %bitcast.76, bf16[896,2304]{1,0:T(8,128)(2,1)} %get-tuple-element.97.seq_normed, bf16[896,512]{1,0:T(8,128)(2,1)} %get-tuple-element.98.q, ...), custom_call_target="tpu_custom_call" | custom-call | tf_op jit(solution)/shard_map/pallas_call | solution.py:962
  817.2 0.7 pad_maximum_fusion.2
  818.1 2.0 fusion.5
  820.4 0.8 copy-done.1
  821.7 14.5 %shard_map.286 = (f32[1,288]{1,0:T(1,128)S(1)}, f32[8,128]{1,0:T(8,128)S(1)}) custom-call(f32[32,1,288]{2,1,0:T(1,128)S(1)} %reshape.366.terms, f32[288,2304]{1,0:T(8,128)S(1)} %copy-done, f32[288,2304]{1,0:T(8,128)S(1)} %copy-done.1, f32[288,2304]{1,0:T(8,128)S(1)} %pad_maximum_fusion.g_down, f32[288,512]{1,0:T(8,128)S(1)} %copy-done.5, ...), custom_call_target="tpu_custom_call" | custom-call | tf_op jit(solution)/shard_map/pallas_call | solution.py:1103
  836.8 26.8 %shard_map.287 = (f32[1,288]{1,0:T(1,128)S(1)}, f32[1,288]{1,0:T(1,128)S(1)}, f32[1,288]{1,0:T(1,128)S(1)}, f32[3,288,2304]{2,1,0:T(8,128)}, f32[3,288,2304]{2,1...) custom-call(f32[8,128]{1,0:T(8,128)S(1)} %get-tuple-element.119.norm, ...), custom_call_target="tpu_custom_call" | custom-call | flops 100 | bytes 41943040 | tf_op jit(solution)/shard_map/pallas_call | solution.py:1143
  865.4 1.3 copy.43
  866.7 1.0 copy-done.19
  867.7 1.3 copy.44
  (93 shorter events, 9.2 us)
Async XLA Ops:
  0.6 20.8 %copy-start.3 = (f32[2,288,512]{2,1,0:T(8,128)S(1)}, f32[2,288,512]{2,1,0:T(8,128)}, u32[]{:S(2)}) copy-start(f32[2,288,512]{2,1,0:T(8,128)} %refs_3_.1) | copy-start | bytes 3538948
  11.6 11.1 %copy-start.20 = (s32[8,896]{1,0:T(8,128)}, s32[8,896]{1,0:T(8,128)S(1)}, u32[]{:S(2)}) copy-start(s32[8,896]{1,0:T(8,128)S(1)} %stack.23.marks_row) | copy-start | bytes 86020
  16.7 340.8 %copy-start.13 = (f32[224,1]{1,0:T(8,128)}, f32[224,1]{1,0:T(8,128)S(1)}, u32[]{:S(2)}) copy-start(f32[224,1]{1,0:T(8,128)S(1)} %copy.35.live) | copy-start | bytes 2692
  313.9 43.6 %copy-start.2 = (f32[224,2304]{1,0:T(8,128)S(1)}, f32[224,2304]{1,0:T(8,128)}, u32[]{:S(2)}) copy-start(f32[224,2304]{1,0:T(8,128)} %get-tuple-element.79.hid) | copy-start | bytes 6193156
  313.9 43.6 %copy-start.16 = (f32[4,2304]{1,0:T(4,128)S(1)}, f32[4,2304]{1,0:T(4,128)}, u32[]{:S(2)}) copy-start(f32[4,2304]{1,0:T(4,128)} %get-tuple-element.80.gains) | copy-start | bytes 110596
  357.5 83.2 %copy-start.26 = (bf16[8,224,1152]{2,1,0:T(8,128)(2,1)S(1)}, bf16[8,224,1152]{2,1,0:T(8,128)(2,1)}, u32[]{:S(2)}) copy-start(bf16[8,224,1152]{2,1,0:T(8,128)(2,1)} %get-tuple-element.83) | copy-start | bytes 12386308
  440.8 15.6 %copy-start.9 = (f32[224,2304]{1,0:T(8,128)}, f32[224,2304]{1,0:T(8,128)S(1)}, u32[]{:S(2)}) copy-start(f32[224,2304]{1,0:T(8,128)S(1)} %get-tuple-element.162) | copy-start | bytes 6193156
  458.3 66.7 %collective-permute-start = (bf16[4,288,1152]{2,1,0:T(8,128)(2,1)S(1)}, bf16[4,288,1152]{2,1,0:T(8,128)(2,1)}, u32[]{:S(2)}, u32[]{:S(2)}) collective-permute-start(bf16[4,288,1152]{2,1,0:T(8,128)(2,1)S(1)} %dynamic-slice_bitcast_fusion), channel_id=1, source_target_pairs={{0,4},{4,0},{8,12},{12,8},{16,20},{20,16},{24,28},{28,24},{1,5},{5... | collective-permute-start | bytes 7962632 | tf_op jit(solution)/shard_map/ppermute | solution.py:1155
  460.3 48.0 %copy-start.23 = (f32[288]{0:T(512)S(1)}, f32[288]{0:T(512)}, u32[]{:S(2)}) copy-start(f32[288]{0:T(512)} %param.29) | copy-start | bytes 3460
  460.3 48.0 %copy-start.24 = (f32[288]{0:T(512)S(1)}, f32[288]{0:T(512)}, u32[]{:S(2)}) copy-start(f32[288]{0:T(512)} %param.33) | copy-start | bytes 3460
  508.3 16.7 %copy-start.18 = (bf16[2304,1152]{1,0:T(8,128)(2,1)S(1)}, bf16[2304,1152]{1,0:T(8,128)(2,1)}, u32[]{:S(2)}) copy-start(bf16[2304,1152]{1,0:T(8,128)(2,1)} %fusion) | copy-start | bytes 15925252
  525.0 8.5 copy-start.25
  528.8 172.6 %collective-permute-start.1 = (bf16[288,1152]{1,0:T(8,128)(2,1)}, bf16[288,1152]{1,0:T(8,128)(2,1)}, u32[]{:S(2)}, u32[]{:S(2)}) collective-permute-start(bf16[288,1152]{1,0:T(8,128)(2,1)} %get-tuple-element.137), channel_id=1, source_target_pairs={{0,8},{4,12},{8,16},{12,20},{16,24},{20,28},{24,0},{28,4},{1,9},{5... | collective-permute-start | bytes 1990664 | tf_op jit(solution)/shard_map/ppermute | solution.py:1159
  531.2 170.3 %collective-permute-start.2 = (bf16[288,1152]{1,0:T(8,128)(2,1)}, bf16[288,1152]{1,0:T(8,128)(2,1)}, u32[]{:S(2)}, u32[]{:S(2)}) collective-permute-start(bf16[288,1152]{1,0:T(8,128)(2,1)} %get-tuple-element.136), channel_id=1, source_target_pairs={{0,16},{4,20},{8,24},{12,28},{16,0},{20,4},{24,8},{28,12},{1,17},{... | collective-permute-start | bytes 1990664 | tf_op jit(solution)/shard_map/ppermute | solution.py:1159
  531.2 170.3 %collective-permute-start.3 = (bf16[288,1152]{1,0:T(8,128)(2,1)S(1)}, bf16[288,1152]{1,0:T(8,128)(2,1)}, u32[]{:S(2)}, u32[]{:S(2)}) collective-permute-start(bf16[288,1152]{1,0:T(8,128)(2,1)S(1)} %get-tuple-element.135), channel_id=1, source_target_pairs={{0,24},{4,28},{8,0},{12,4},{16,8},{20,12},{24,16},{28,20},{1,25},{... | collective-permute-start | bytes 1990664 | tf_op jit(solution)/shard_map/ppermute | solution.py:1159
  701.5 115.7 %copy-start.21 = (f32[1,2304]{1,0:T(1,128)S(1)}, f32[1,2304]{1,0:T(1,128)}, u32[]{:S(2)}) copy-start(f32[1,2304]{1,0:T(1,128)} %get-tuple-element.108) | copy-start | bytes 27652
  701.5 115.7 %copy-start.22 = (f32[1,2304]{1,0:T(1,128)S(1)}, f32[1,2304]{1,0:T(1,128)}, u32[]{:S(2)}) copy-start(f32[1,2304]{1,0:T(1,128)} %get-tuple-element.109) | copy-start | bytes 27652
  818.1 2.3 copy-start
  818.1 3.1 copy-start.1
  818.1 3.2 copy-start.5
  818.1 3.4 copy-start.6
  818.1 3.5 copy-start.7
  821.7 15.0 %copy-start.4 = (f32[2,288,512]{2,1,0:T(8,128)S(1)}, f32[2,288,512]{2,1,0:T(8,128)}, u32[]{:S(2)}) copy-start(f32[2,288,512]{2,1,0:T(8,128)} %refs_3_.1) | copy-start | bytes 3538948
  821.7 15.1 %copy-start.8 = (f32[2,288,256]{2,1,0:T(8,128)S(1)}, f32[2,288,256]{2,1,0:T(8,128)}, u32[]{:S(2)}) copy-start(f32[2,288,256]{2,1,0:T(8,128)} %refs_6_.1) | copy-start | bytes 1769476
  821.7 15.1 %copy-start.11 = (f32[2,288,512]{2,1,0:T(8,128)S(1)}, f32[2,288,512]{2,1,0:T(8,128)}, u32[]{:S(2)}) copy-start(f32[2,288,512]{2,1,0:T(8,128)} %refs_4_.1) | copy-start | bytes 3538948
  821.7 15.1 %copy-start.12 = (f32[2,288,512]{2,1,0:T(8,128)S(1)}, f32[2,288,512]{2,1,0:T(8,128)}, u32[]{:S(2)}) copy-start(f32[2,288,512]{2,1,0:T(8,128)} %refs_5_.1) | copy-start | bytes 3538948
  821.7 15.1 %copy-start.14 = (f32[2,288,256]{2,1,0:T(8,128)S(1)}, f32[2,288,256]{2,1,0:T(8,128)}, u32[]{:S(2)}) copy-start(f32[2,288,256]{2,1,0:T(8,128)} %refs_7_.1) | copy-start | bytes 1769476
  821.7 15.0 %copy-start.15 = (f32[2,288,256]{2,1,0:T(8,128)S(1)}, f32[2,288,256]{2,1,0:T(8,128)}, u32[]{:S(2)}) copy-start(f32[2,288,256]{2,1,0:T(8,128)} %refs_8_.1) | copy-start | bytes 1769476
  821.7 15.0 %copy-start.17 = (f32[1,288]{1,0:T(1,128)S(1)}, f32[1,288]{1,0:T(1,128)}, u32[]{:S(2)}) copy-start(f32[1,288]{1,0:T(1,128)} %reshape.358.own_gains.gw) | copy-start | bytes 3460
  836.8 28.6 %copy-start.10 = (f32[224,2304]{1,0:T(8,128)S(1)}, f32[224,2304]{1,0:T(8,128)}, u32[]{:S(2)}) copy-start(f32[224,2304]{1,0:T(8,128)} %copy-done.9) | copy-start | bytes 6193156
  865.4 2.3 copy-start.19

commit v4 on v3

--- a/solution.py
+++ b/solution.py
@@ -157,6 +157,23 @@
         copy.start()
         self.open.append((copy, copy.wait_send))
         return copy
+
+    def family(self, count, make):
+        base = self.used
+        self.used += count
+
+        def copy_of(k):
+            return make(k, self.send_sems.at[base + k], self.recv_sems.at[base + k])
+
+        for k in range(count):
+            copy = copy_of(k)
+            self.open.append((copy, copy.wait_send))
+        return copy_of
+
+    def locals(self, count):
+        base = self.used_local
+        self.used_local += count
+        return base
 
     def sent(self, copy):
         copy.wait_send()
@@ -458,6 +475,7 @@
             weights.out(0)
     weights.out(1)
     weights.out(2)
+    weights.out(3)
     near.wait_recv()
     both.wait_recv()
     for copy in own_parts:
@@ -471,8 +489,8 @@
     def step(n):
         if n < len(pieces):
             weights.on(n)
-            if n + 3 < len(pieces):
-                weights.out(n + 3)
+            if n + 4 < len(pieces):
+                weights.out(n + 4)
 
     step(0)
     weights.done(0)
@@ -543,28 +561,28 @@
     )(low_q, low_kv, low_o, w_mlp, width_mlp, cosine, sine, marks_col, marks_row, inputs, gains)
 
 
-def reduce_pair_steps(net, near, far, r1, s2, r2, s3, r3, rows, loaded, split=False, hooks=()):
-    cores = {k: net.send(far.at[k], r1.at[k], net.core_n) for k in (3, 2, 1, 0)}
+def reduce_pair_steps(net, near, cores, r1, r2, r3, rows, split=False, compute=None, hooks=None):
     plan = [(pl.ds(0, D // 2 if split else D), (3, 2), net.x_n, 1, net.z_n)]
     if split:
         plan.append((pl.ds(D // 2, D // 2), (3, 1), net.z_n, 2, net.x_n))
     firsts = {}
-    loaded.wait()
     for k in (3, 2, 1) if split else (3, 2):
-        cores[k].wait_recv()
+        compute(k)
+        cores(k).wait_recv()
         for part, (cols, blocks, device, _, _) in enumerate(plan):
             if k not in blocks:
                 continue
             at_block = blocks.index(k)
 
-            def add(at, state, k=k, cols=cols, at_block=at_block):
-                s2[at_block, at, cols] = (near[k, at, cols].astype(F32) + r1[k, at, cols].astype(F32)).astype(BF)
+            def add(at, state, k=k, cols=cols):
+                near[k, at, cols] = (near[k, at, cols].astype(F32) + r1[k, at, cols].astype(F32)).astype(BF)
                 return state
 
             by_rows(rows, add)
-            firsts[part, at_block] = net.send(s2.at[at_block, :, cols], r2.at[at_block, :, cols], device)
+            firsts[part, at_block] = net.send(near.at[k, :, cols], r2.at[at_block, :, cols], device)
     for k in (0,) if split else (1, 0):
-        cores[k].wait_recv()
+        compute(k)
+        cores(k).wait_recv()
     last = []
     if hooks:
         hooks[0]()
@@ -572,13 +590,13 @@
         firsts[part, 0].wait_recv()
 
         def add(at, state, cols=cols, second=second):
-            s3[at, cols] = (
+            near[second, at, cols] = (
                 near[second, at, cols].astype(F32) + r1[second, at, cols].astype(F32) + r2[0, at, cols].astype(F32)
             ).astype(BF)
             return state
 
         by_rows(rows, add)
-        last.append(net.send(s3.at[:, cols], r3.at[:, cols], device))
+        last.append(net.send(near.at[second, :, cols], r3.at[:, cols], device))
     if hooks:
         hooks[1]()
     for part in range(len(plan)):
@@ -590,13 +608,48 @@
     return near[0, at].astype(F32) + r1[0, at].astype(F32) + r2[1, at].astype(F32) + r3[at].astype(F32)
 
 
-def pair_scratch(rows):
+def pair_scratch(rows, blocks=8):
     block = (rows, D)
     return [
-        pltpu.VMEM((4,) + block, BF),
-        pltpu.VMEM((4,) + block, BF), pltpu.VMEM((2,) + block, BF), pltpu.VMEM((2,) + block, BF),
-        pltpu.VMEM(block, BF), pltpu.VMEM(block, BF), pltpu.VMEM(block, BF),
+        pltpu.VMEM((blocks,) + block, BF), pltpu.VMEM((4,) + block, BF), pltpu.VMEM((2,) + block, BF),
+        pltpu.VMEM(block, BF), pltpu.VMEM(block, BF),
     ]
+
+
+def core_family(net, parts, r1):
+    return net.family(
+        4,
+        lambda k, send, recv: pltpu.make_async_remote_copy(
+            src_ref=parts.at[4 + k], dst_ref=r1.at[k], send_sem=send, recv_sem=recv,
+            device_id=net.core_n, device_id_type=MESH,
+        ),
+    )
+
+
+def block_at(t):
+    return 7 - t // 2 - 4 * (t % 2)
+
+
+class Stream:
+    def __init__(self, net, pairs, inward):
+        self.net, self.pairs, self.inward = net, pairs, inward
+        self.base = net.locals(2 * len(pairs))
+
+    def copies(self, t):
+        slot = t % 2
+        for n, (far, held) in enumerate(self.pairs):
+            ends = (far.at[block_at(t)], held.at[slot])
+            yield pltpu.make_async_copy(
+                *(ends if self.inward else ends[::-1]), self.net.local_sems.at[self.base + 2 * n + slot]
+            )
+
+    def start(self, t):
+        for copy in self.copies(t):
+            copy.start()
+
+    def wait(self, t):
+        for copy in self.copies(t):
+            copy.wait()
 
 
 def rms_back_rows(values, gain, grad):
@@ -607,20 +660,66 @@
 
 
 def turn_kernel(
-    n_dp, n_mp, part, hid, gains, out_grad, live, outputs, dgain, group,
-    near, r1, s2, r2, s3, r3, own, ss, rs, ls,
+    n_dp, n_mp, ffn, w_gate, w_up, w_down, hid, gains, out_grad, live,
+    outputs, dgain, gate, up, act, group,
+    parts, r1, r2, r3, own, wg, wu, wd, tokens, gate_b, up_b, act_b, ss, rs, ls,
 ):
     net = Net(n_dp, n_mp, ss, rs, ls)
+    loads = [net.move(src, dst) for src, dst in ((w_gate, wg), (w_up, wu), (w_down, wd))]
+    rows = hid.shape[0]
+    incoming = Stream(net, [(ffn, tokens)], True)
+    outgoing = Stream(net, [(gate, gate_b), (up, up_b), (act, act_b)], False)
+    cores = core_family(net, parts, r1)
+    incoming.start(0)
     net.meet(pair_partners(net, False))
-    rows = hid.shape[0]
-    far = part.at[pl.ds(4, 4)]
-    loaded = net.move(part.at[pl.ds(0, 4)], near)
-    for copy in reduce_pair_steps(net, near, far, r1, s2, r2, s3, r3, rows, loaded, True):
+    for load in loads:
+        load.wait()
+
+    def block(t, state):
+        slot, at = t % 2, block_at(t)
+        incoming.wait(t)
+
+        @pl.when(t < 7)
+        def _():
+            incoming.start(t + 1)
+
+        g = mm(tokens[slot], wg[...])
+        u = mm(tokens[slot], wu[...])
+        bend = jnp.tanh(GELU * (g + 0.044715 * (g * g * g)))
+        a = (0.5 * g * (1.0 + bend) * u).astype(BF)
+
+        @pl.when(t >= 2)
+        def _():
+            outgoing.wait(t - 2)
+
+        gate_b[slot] = g
+        up_b[slot] = u
+        act_b[slot] = a
+        outgoing.start(t)
+        parts[at] = mm_cols(a, wd[...]).astype(BF)
+        return state
+
+    def compute(k):
+        def both(t, state):
+            block(t, state)
+
+            @pl.when(t % 2 == 0)
+            def _():
+                cores(k).start()
+
+            return state
+
+        lax.fori_loop(6 - 2 * k, 8 - 2 * k, both, 0)
+
+    last_sums = reduce_pair_steps(net, parts, cores, r1, r2, r3, rows, True, compute)
+    outgoing.wait(6)
+    outgoing.wait(7)
+    for copy in last_sums:
         copy.wait_recv()
     g3 = 1.0 + gains[3:4]
 
     def last(at, state):
-        total = pair_sum(near, r1, r2, r3, at)
+        total = pair_sum(parts, r1, r2, r3, at)
         outputs[at] = hid[at] + total * inv_root(total) * g3
         grad, dg = rms_back_rows(total, g3, out_grad[at] * live[at])
         own[at] = grad.astype(BF)
@@ -631,15 +730,27 @@
     net.close()
 
 
-def turn(n_dp, n_mp, part, hid, gains, out_grad, live):
+def turn(n_dp, n_mp, ffn, w_gate, w_up, w_down, hid, gains, out_grad, live):
     rows = hid.shape[0]
     block = (rows, D)
+    width = w_gate.shape[1]
+    vm = lambda *shape: pltpu.VMEM(shape, BF)
     return call(
         functools.partial(turn_kernel, n_dp, n_mp),
-        [jax.ShapeDtypeStruct(block, F32), jax.ShapeDtypeStruct((1, D), F32), jax.ShapeDtypeStruct((8,) + block, BF)],
-        [VMEM, VMEM, ANY], [ANY, VMEM, VMEM, VMEM, VMEM],
-        pair_scratch(rows) + [dma(32), dma(32), dma(4)], 4, 48,
-    )(part, hid, gains, out_grad, live)
+        [
+            jax.ShapeDtypeStruct(block, F32), jax.ShapeDtypeStruct((1, D), F32),
+            jax.ShapeDtypeStruct((8, rows, width), F32), jax.ShapeDtypeStruct((8, rows, width), F32),
+            jax.ShapeDtypeStruct((8, rows, width), BF), jax.ShapeDtypeStruct((8,) + block, BF),
+        ],
+        [VMEM, VMEM] + [ANY] * 4, [ANY] * 4 + [VMEM] * 4,
+        pair_scratch(rows)
+        + [
+            vm(D, width), vm(D, width), vm(D, width), vm(2, *block),
+            pltpu.VMEM((2, rows, width), F32), pltpu.VMEM((2, rows, width), F32), vm(2, rows, width),
+            dma(32), dma(32), dma(16),
+        ],
+        4, 60,
+    )(ffn, w_gate, w_up, w_down, hid, gains, out_grad, live)
 
 
 def in_steps(count, body, carry=0, first=0):
@@ -693,9 +804,11 @@
             return state
 
         in_steps(self.wrows, collect)
+        copies = []
         for parity in range(2):
             half = (self.net.zl + parity) % 2
-            self.net.keep(total.at[parity], sums.at[:, pl.ds(pl.multiple_of(half * self.width, self.width), self.width)])
+            copies.append(self.net.move(total.at[parity], sums.at[:, pl.ds(pl.multiple_of(half * self.width, self.width), self.width)]))
+        return copies
 
     def whole(self, out):
         self.landed()
@@ -720,19 +833,21 @@
 def back_kernel(
     n_dp, n_mp, part, hid, att, gains, out_grad, live, grads, grads_up,
     ghid, dg1, dg2, seq, sums, sums_up,
-    near, r1, s2, r2, s3, r3, own, stay, came, last, ustay, ucame, ulast, total, ss, rs, ls,
+    near, r1, r2, r3, own, stay, came, last, ustay, ucame, ulast, total, ss, rs, ls,
 ):
     net = Net(n_dp, n_mp, ss, rs, ls)
-    nj = n_dp // 2
+    loaded = net.move(part.at[pl.ds(0, 4)], near)
+    cores = core_family(net, part, r1)
     net.meet(pair_partners(net, True))
     rows = hid.shape[0]
-    far = part.at[pl.ds(4, 4)]
-    loaded = net.move(part.at[pl.ds(0, 4)], near)
+    for k in (3, 2, 1, 0):
+        cores(k).start()
     weight = Scatter(net, grads, stay, came, last)
     weight_up = Scatter(net, grads_up, ustay, ucame, ulast)
     weight.along_y()
+    loaded.wait()
     last_sums = reduce_pair_steps(
-        net, near, far, r1, s2, r2, s3, r3, rows, loaded, False,
+        net, near, cores, r1, r2, r3, rows, False, lambda k: None,
         (lambda: weight.along_z(weight.turns[:1]), lambda: weight.along_z(weight.turns[1:2])),
     )
     weight_up.along_y()
@@ -758,9 +873,12 @@
     weight_up.along_z(weight_up.turns[:1])
     finish()
     weight_up.along_z(weight_up.turns[1:2])
-    weight.halves(total.at[0], sums)
+    first_out = weight.halves(total, sums)
     weight_up.along_z(weight_up.turns[2:])
-    weight_up.halves(total.at[1], sums_up)
+    for copy in first_out:
+        copy.wait()
+    for copy in weight_up.halves(total, sums_up):
+        copy.wait()
     net.close()
 
 
@@ -777,9 +895,9 @@
             jax.ShapeDtypeStruct((4,) + block, BF), jax.ShapeDtypeStruct((wrows, 2 * width), F32),
             jax.ShapeDtypeStruct((wrows, 2 * width), F32),
         ],
-        [VMEM, VMEM, VMEM, ANY, ANY, ANY], [ANY, VMEM, VMEM, VMEM, VMEM, VMEM, ANY, ANY],
-        pair_scratch(rows) + scatter_scratch(nj, wrows, width) * 2
-        + [pltpu.VMEM((2, 2, wrows, width), F32), dma(count), dma(count), dma(12 + 2 * nj)],
+        [VMEM, VMEM, VMEM, ANY, ANY, ANY], [ANY] + [VMEM] * 5 + [ANY, ANY],
+        pair_scratch(rows, 4) + scatter_scratch(nj, wrows, width) * 2
+        + [pltpu.VMEM((2, wrows, width), F32), dma(count), dma(count), dma(16 + 2 * nj)],
         5, 60,
     )(part, hid, att, gains, out_grad, live, grads, grads_up)
 
@@ -1004,32 +1122,6 @@
 GELU = math.sqrt(2.0 / math.pi)
 
 
-def mlp_kernel(x, wg, wu, wd, gate, up, act, part):
-    g = mm(x[...], wg[...])
-    u = mm(x[...], wu[...])
-    gate[...] = g
-    up[...] = u
-    bend = jnp.tanh(GELU * (g + 0.044715 * (g * g * g)))
-    a = (0.5 * g * (1.0 + bend) * u).astype(BF)
-    act[...] = a
-    part[...] = mm_cols(a, wd[...]).astype(BF)
-
-
-def mlp(x, wg, wu, wd):
-    blocks, rows, _ = x.shape
-    width = wg.shape[1]
-    shape = (blocks, rows, width)
-    return plain(
-        mlp_kernel, (blocks,),
-        [
-            jax.ShapeDtypeStruct(shape, F32), jax.ShapeDtypeStruct(shape, F32), jax.ShapeDtypeStruct(shape, BF),
-            jax.ShapeDtypeStruct((blocks, rows, D), BF),
-        ],
-        [tile(rows, width)] * 3 + [tile(rows, D)], [tile(rows, D)] + [whole(wg.shape)] * 3, 56,
-        6 * blocks * rows * D * width,
-    )(x, wg, wu, wd)
-
-
 def down_back_kernel(grad, gate, up, wg, wu, wd, dgate, dup, part):
     ga = mm(grad[...], wd[...])
     g = gate[...]
@@ -1135,7 +1227,7 @@
 
 def adam_all(norm, gain_grad, gains, grads, states):
     wrows = grads[0].shape[0]
-    step = 16 if wrows % 16 == 0 else 8
+    step = 48 if wrows % 48 == 0 else 8
     like = lambda a: jax.ShapeDtypeStruct(a.shape, F32)
     fixed = lambda a: pl.BlockSpec(a.shape, lambda t: (0, 0))
     flat = lambda a: pl.BlockSpec((step, a.shape[1]), lambda t: (t, 0))
@@ -1144,7 +1236,7 @@
         adam_kernel, (wrows // step,), [like(a) for a in gains] + [like(a) for a in states],
         [fixed(a) for a in gains] + [deep(a) for a in states],
         [fixed(a) for a in (norm, gain_grad) + tuple(gains)] + [flat(a) for a in grads] + [deep(a) for a in states],
-        32, 100,
+        56, 100,
     )(norm, gain_grad, *gains, *grads, *states)
 
 
@@ -1207,10 +1299,9 @@
             marks.T, marks, inputs, norm_gains.reshape(1, -1),
         )
         w_gate, w_up, w_down = w_gate.reshape(D, -1), w_up.reshape(D, -1), w_down.reshape(D, -1)
-        gate, up, activated, part = mlp(group_ffn, w_gate, w_up, w_down)
         live = lax.dynamic_slice_in_dim(pad_mask[0], m * rows, rows).astype(F32)[:, None]
-        outputs, grad_gain_three, group_grad = turn(
-            n_dp, n_mp, part, hidden_in, gain_rows, out_grad, live
+        outputs, grad_gain_three, gate, up, activated, group_grad = turn(
+            n_dp, n_mp, group_ffn, w_gate, w_up, w_down, hidden_in, gain_rows, out_grad, live
         )
         tokens = 8 * rows
         grad_down = mm_rows(group_grad.reshape(tokens, D), activated.reshape(tokens, -1))
@@ -1224,7 +1315,8 @@
         down_own, down_shifted = scatter_second(down_stay, down_came, j)
         grads_up = mm_rows(flat_ffn, grad_up.reshape(tokens, -1)).astype(BF).reshape(nj, 2, wrows, -1)
         grad_hidden, grad_gain_one, grad_gain_two, seq_grad, sum_gate, sum_up = back(
-            n_dp, n_mp, part, hidden_in, attended, gain_rows, out_grad, live, grads_gate, grads_up
+            n_dp, n_mp, part, hidden_in, attended, gain_rows, out_grad, live,
+            grads_gate, grads_up
         )
         seq_grad, down_shifted = lax.optimization_barrier((seq_grad, down_shifted))
         sums = [down_own.astype(F32), 0.0]

time: 880 us -> 856 us (0.973)
  Pallas kernels: 776 us -> 745 us
    pallas_call x1 -> x0, Pallas kernels: 43.5 us -> none  [mlp(): plain(mlp_kernel, (blocks,), [jax.ShapeDtypeStruct(shape, F32), jax.Shape...]
    pallas_call x1, Pallas kernels: 83.2 us -> 100 us  [turn(): call(functools.partial(turn_kernel, n_dp, n_mp), [jax.ShapeDtypeStruct(bl...]
where the time goes in v4:
time: 856 us; the launch traced here: 847 us
  Pallas kernels  745 us (87%)
  matrix products  48.2 us (6%)
  local copies, waits for them, and re-layouts  20.9 us (2%)
  other arithmetic  17.9 us (2%)
    pallas_call x1, Pallas kernels, open_layer(): call(functools.partial(open_kernel, n_dp, n_mp), [bf(total, cols), bf(tot...  286 us
    pallas_call x1, Pallas kernels, back(): call(functools.partial(back_kernel, n_dp, n_mp), [jax.ShapeDtypeStruct(bl...  150 us
    pallas_call x1, Pallas kernels, close(): call(functools.partial(close_kernel, n_dp, n_mp), [jax.ShapeDtypeStruct((...  122 us
    pallas_call x1, Pallas kernels, turn(): call(functools.partial(turn_kernel, n_dp, n_mp), [jax.ShapeDtypeStruct(bl...  100 us
    dot_general x3, matrix products, mm_rows(): lax.dot_general(left, right, (((0,), (0,)), ((), ())), preferred_element_...  48.2 us
    pallas_call x1, Pallas kernels, mlp_back(): plain(down_back_kernel, (blocks,), [jax.ShapeDtypeStruct(shape, BF), jax....  48 us
    pallas_call x1, Pallas kernels, adam_all(): plain(adam_kernel, (wrows // step,), [like(a) for a in gains] + [like(a)...  24.7 us
  transfers between devices with their start and end apart: 4, of which 0 were waited for; matrix products, arithmetic and copies ran while one was open for 4% of the time, Pallas kernels for 23%

profile of v4, /device:TPU:0, one launch (start us, length us, event | category | flops | bytes accessed | tf_op | source)
XLA Modules:
  0.0 846.6 jit_solution(8598025801719701562)
XLA Ops:
  0.7 1.4 fusion.15
  5.4 1.2 slice.50
  11.6 1.0 copy.34.marks_col
  14.6 1.2 reshape.358.own_gains.gw
  17.4 1.3 fusion.8
  19.4 2.6 multiply_sine_fusion
  22.0 1.3 fusion.7
  23.3 285.9 %shard_map.280 = (bf16[896,512]{1,0:T(8,128)(2,1)}, bf16[896,256]{1,0:T(8,128)(2,1)}, bf16[896,256]{1,0:T(8,128)(2,1)}, bf16[896,512]{1,0:T(8,128)(2,1)}, f32[22...) custom-call(bf16[288,512]{1,0:T(8,128)(2,1)} %get-tuple-element.137., ...), custom_call_target="tpu_custom_call" | custom-call | tf_op jit(solution)/shard_map/pallas_call | solution.py:547
  309.2 100.2 %shard_map.281 = (f32[224,2304]{1,0:T(8,128)}, f32[1,2304]{1,0:T(1,128)}, f32[8,224,1152]{2,1,0:T(8,128)}, f32[8,224,1152]{2,1,0:T(8,128)}, bf16[8,224,1152]{2,1...) custom-call(bf16[8,224,2304]{2,1,0:T(8,128)(2,1)} %get-tuple-element.73.ffn, bf16[2304,1152]{1,0:T(8,128)(2,1)} %bitcast.72, ...), custom_call_target="tpu_custom_call" | custom-call | tf_op jit(solution)/shard_map/pallas_call | solution.py:738
  409.4 16.5 %fusion = bf16[2304,1152]{1,0:T(8,128)(2,1)} fusion(bf16[8,224,2304]{2,1,0:T(8,128)(2,1)} %get-tuple-element.82.grad, bf16[8,224,1152]{2,1,0:T(8,128)(2,1)} %get-tuple-element.81), kind=kOutput, calls=%fused_computation.7 | convolution fusion | flops 9515335680 | bytes 17694720 | tf_op jit(solution)/shard_map/dot_general | solution.py:94
  426.0 2.0 dynamic-slice_bitcast_fusion
  427.9 0.9 collective-permute-start
  428.8 48.0 %shard_map.282 = (bf16[8,224,1152]{2,1,0:T(8,128)(2,1)}, bf16[8,224,1152]{2,1,0:T(8,128)(2,1)}, bf16[8,224,2304]{2,1,0:T(8,128)(2,1)}) custom-call(bf16[8,224,2304]{2,1,0:T(8,128)(2,1)} %get-tuple-element.82.grad, f32[8,224,1152]{2,1,0:T(8,128)} %get-tuple-element.83.gate, f32[8,224,1152]{2,1,0:T(8,128)} %get-tuple-element.84.up, ...), custom_call_target="tpu_custom_call" | custom-call | flops 28538044416 | bytes 41943040 | tf_op jit(solution)/shard_map/pallas_call | solution.py:1143
  477.9 16.4 %fusion.1 = bf16[2304,1152]{1,0:T(8,128)(2,1)} fusion(bf16[8,224,2304]{2,1,0:T(8,128)(2,1)} %get-tuple-element.73.ffn, bf16[8,224,1152]{2,1,0:T(8,128)(2,1)} %get-tuple-element.87), kind=kOutput, calls=%fused_computation.8 | convolution fusion | flops 9515335680 | bytes 17694720 | tf_op jit(solution)/shard_map/dot_general | solution.py:94
  494.3 2.6 fusion.3
  496.9 1.2 dynamic-slice_bitcast_fusion.1
  498.2 1.0 collective-permute-start.1
  499.1 4.9 collective-permute-start.2
  504.1 1.5 collective-permute-start.3
  505.6 15.2 %fusion.2 = bf16[2304,1152]{1,0:T(8,128)(2,1)} fusion(bf16[8,224,2304]{2,1,0:T(8,128)(2,1)} %get-tuple-element.73.ffn, bf16[8,224,1152]{2,1,0:T(8,128)(2,1)S(1)} %copy-done.18), kind=kOutput, calls=%fused_computation.9 | convolution fusion | flops 9515335680 | bytes 17694720 | tf_op jit(solution)/shard_map/dot_general | solution.py:94
  520.8 149.7 %shard_map.283 = (f32[224,2304]{1,0:T(8,128)}, f32[1,2304]{1,0:T(1,128)}, f32[1,2304]{1,0:T(1,128)}, bf16[4,224,2304]{2,1,0:T(8,128)(2,1)}, f32[288,2304]{1,0:T(8,128)}, /*index=5*/f32[288,2304]{1,0:T(8,128)}) custom-call(bf16[8,224,2304]{2,1,0:T(8,128)(2,1)} %get-tuple-element.85.part, f32[224,2304]{1,0:T(8,128)} %get-tuple-element.77.hid, ...), custom_call_target="tpu_custom_call" | custom-call | tf_op jit(solution)/shard_map/pallas_call | solution.py:891
  670.6 122.0 %shard_map.284 = (f32[224,2304]{1,0:T(8,128)}, f32[1,2304]{1,0:T(1,128)}, f32[288,512]{1,0:T(8,128)}, f32[288,512]{1,0:T(8,128)}, f32[288,512]{1,0:T(8,128)}) custom-call(bf16[896,2304]{1,0:T(8,128)(2,1)} %bitcast.82, bf16[896,2304]{1,0:T(8,128)(2,1)} %get-tuple-element.95.seq_normed, bf16[896,512]{1,0:T(8,128)(2,1)} %get-tuple-element.96.q, ...), custom_call_target="tpu_custom_call" | custom-call | tf_op jit(solution)/shard_map/pallas_call | solution.py:1080
  793.5 2.0 fusion.5
  795.8 0.8 copy-done.2
  798.0 14.7 %shard_map.285 = (f32[1,288]{1,0:T(1,128)S(1)}, f32[8,128]{1,0:T(8,128)S(1)}) custom-call(f32[32,1,288]{2,1,0:T(1,128)S(1)} %reshape.366.terms, f32[288,2304]{1,0:T(8,128)S(1)} %copy-done.1, f32[288,2304]{1,0:T(8,128)S(1)} %copy-done.2, f32[288,2304]{1,0:T(8,128)S(1)} %pad_maximum_fusion.g_down, f32[288,512]{1,0:T(8,128)S(1)} %copy-done.3, ...), custom_call_target="tpu_custom_call" | custom-call | tf_op jit(solution)/shard_map/pallas_call | solution.py:1195
  813.9 24.7 %shard_map.286 = (f32[1,288]{1,0:T(1,128)}, f32[1,288]{1,0:T(1,128)}, f32[1,288]{1,0:T(1,128)}, f32[3,288,2304]{2,1,0:T(8,128)}, f32[3,288,2304]{2,1,0:T(8,128)}...) custom-call(f32[8,128]{1,0:T(8,128)} %copy-done.6, ...), custom_call_target="tpu_custom_call" | custom-call | flops 100 | bytes 41943040 | tf_op jit(solution)/shard_map/pallas_call | solution.py:1235
  838.6 1.3 reduce.5
  839.9 1.3 reduce.6
  841.2 1.3 reduce.7
  842.4 1.3 copy.43
  843.7 1.0 copy-done.11
  844.8 1.3 copy.44
  (76 shorter events, 13.0 us)
Async XLA Ops:
  0.6 21.4 %copy-start.9 = (f32[2,288,512]{2,1,0:T(8,128)S(1)}, f32[2,288,512]{2,1,0:T(8,128)}, u32[]{:S(2)}) copy-start(f32[2,288,512]{2,1,0:T(8,128)} %refs_3_.1) | copy-start | bytes 3538948
  11.6 11.7 %copy-start.12 = (s32[8,896]{1,0:T(8,128)}, s32[8,896]{1,0:T(8,128)S(1)}, u32[]{:S(2)}) copy-start(s32[8,896]{1,0:T(8,128)S(1)} %stack.23.marks_row) | copy-start | bytes 86020
  427.9 66.4 %collective-permute-start = (bf16[4,288,1152]{2,1,0:T(8,128)(2,1)S(1)}, bf16[4,288,1152]{2,1,0:T(8,128)(2,1)}, u32[]{:S(2)}, u32[]{:S(2)}) collective-permute-start(bf16[4,288,1152]{2,1,0:T(8,128)(2,1)S(1)} %dynamic-slice_bitcast_fusion), channel_id=1, source_target_pairs={{0,4},{4,0},{8,12},{12,8},{16,20},{20,16},{24,28},{28,24},{1,5},{5... | collective-permute-start | bytes 7962632 | tf_op jit(solution)/shard_map/ppermute | solution.py:1247
  428.8 48.0 %copy-start.16 = (f32[288]{0:T(512)S(1)}, f32[288]{0:T(512)}, u32[]{:S(2)}) copy-start(f32[288]{0:T(512)} %param.29) | copy-start | bytes 3460
  428.8 48.6 %copy-start.17 = (f32[288]{0:T(512)S(1)}, f32[288]{0:T(512)}, u32[]{:S(2)}) copy-start(f32[288]{0:T(512)} %param.33) | copy-start | bytes 3460
  477.9 16.4 %copy-start.8 = (bf16[2304,1152]{1,0:T(8,128)(2,1)S(1)}, bf16[2304,1152]{1,0:T(8,128)(2,1)}, u32[]{:S(2)}) copy-start(bf16[2304,1152]{1,0:T(8,128)(2,1)} %fusion) | copy-start | bytes 15925252
  494.3 11.3 %copy-start.18 = (bf16[8,224,1152]{2,1,0:T(8,128)(2,1)S(1)}, bf16[8,224,1152]{2,1,0:T(8,128)(2,1)}, u32[]{:S(2)}) copy-start(bf16[8,224,1152]{2,1,0:T(8,128)(2,1)} %get-tuple-element.91) | copy-start | bytes 12386308
  498.2 172.4 %collective-permute-start.1 = (bf16[288,1152]{1,0:T(8,128)(2,1)}, bf16[288,1152]{1,0:T(8,128)(2,1)}, u32[]{:S(2)}, u32[]{:S(2)}) collective-permute-start(bf16[288,1152]{1,0:T(8,128)(2,1)} %get-tuple-element.135), channel_id=1, source_target_pairs={{0,8},{4,12},{8,16},{12,20},{16,24},{20,28},{24,0},{28,4},{1,9},{5... | collective-permute-start | bytes 1990664 | tf_op jit(solution)/shard_map/ppermute | solution.py:1251
  499.1 171.4 %collective-permute-start.2 = (bf16[288,1152]{1,0:T(8,128)(2,1)}, bf16[288,1152]{1,0:T(8,128)(2,1)}, u32[]{:S(2)}, u32[]{:S(2)}) collective-permute-start(bf16[288,1152]{1,0:T(8,128)(2,1)} %get-tuple-element.134), channel_id=1, source_target_pairs={{0,16},{4,20},{8,24},{12,28},{16,0},{20,4},{24,8},{28,12},{1,17},{... | collective-permute-start | bytes 1990664 | tf_op jit(solution)/shard_map/ppermute | solution.py:1251
  504.1 166.5 %collective-permute-start.3 = (bf16[288,1152]{1,0:T(8,128)(2,1)S(1)}, bf16[288,1152]{1,0:T(8,128)(2,1)}, u32[]{:S(2)}, u32[]{:S(2)}) collective-permute-start(bf16[288,1152]{1,0:T(8,128)(2,1)S(1)} %get-tuple-element.133), channel_id=1, source_target_pairs={{0,24},{4,28},{8,0},{12,4},{16,8},{20,12},{24,16},{28,20},{1,25},{... | collective-permute-start | bytes 1990664 | tf_op jit(solution)/shard_map/ppermute | solution.py:1251
  670.5 122.0 %copy-start.13 = (f32[1,2304]{1,0:T(1,128)S(1)}, f32[1,2304]{1,0:T(1,128)}, u32[]{:S(2)}) copy-start(f32[1,2304]{1,0:T(1,128)} %get-tuple-element.108) | copy-start | bytes 27652
  670.5 122.0 %copy-start.14 = (f32[1,2304]{1,0:T(1,128)S(1)}, f32[1,2304]{1,0:T(1,128)}, u32[]{:S(2)}) copy-start(f32[1,2304]{1,0:T(1,128)} %get-tuple-element.106) | copy-start | bytes 27652
  670.6 122.0 %copy-start.15 = (f32[1,2304]{1,0:T(1,128)S(1)}, f32[1,2304]{1,0:T(1,128)}, u32[]{:S(2)}) copy-start(f32[1,2304]{1,0:T(1,128)} %get-tuple-element.107) | copy-start | bytes 27652
  793.5 2.3 copy-start.1
  793.5 3.1 copy-start.2
  793.5 3.5 copy-start.3
  793.5 4.1 copy-start.4
  793.5 4.5 copy-start.5
  795.7 17.1 %copy-start = (f32[288,2304]{1,0:T(8,128)}, f32[288,2304]{1,0:T(8,128)S(1)}, u32[]{:S(2)}) copy-start(f32[288,2304]{1,0:T(8,128)S(1)} %pad_maximum_fusion.g_down) | copy-start | bytes 7962628
  812.8 0.6 copy-start.7
  813.3 0.6 copy-start.6
  813.9 28.5 %copy-start.10 = (f32[224,2304]{1,0:T(8,128)S(1)}, f32[224,2304]{1,0:T(8,128)}, u32[]{:S(2)}) copy-start(f32[224,2304]{1,0:T(8,128)} %get-tuple-element.160) | copy-start | bytes 6193156
  842.4 2.3 copy-start.11

commit v5 on v4

--- a/solution.py
+++ b/solution.py
@@ -63,27 +63,6 @@
     grad_values = root * scaled - values * (root * root * root * dot)
     grad_gain = jnp.sum(values * root * grad, axis=0)
     return grad_values, grad_gain
-
-
-def doc_positions(segments):
-    slot_index = jnp.arange(segments.shape[0], dtype=jnp.int32)
-    previous = jnp.concatenate([segments[:1] - 1, segments[:-1]])
-    starts = segments != previous
-    doc_begin = lax.cummax(jnp.where(starts, slot_index, 0), axis=0)
-    return slot_index - doc_begin
-
-
-def rotate(values, cosine, sine):
-    half_dim = HEAD_WIDTH // 2
-    turned = jnp.concatenate([-values[..., half_dim:], values[..., :half_dim]], -1)
-    return values * cosine + turned * sine
-
-
-def rotate_back(grads, cosine, sine):
-    half_dim = HEAD_WIDTH // 2
-    scaled = grads * sine
-    turned = jnp.concatenate([scaled[..., half_dim:], -scaled[..., :half_dim]], -1)
-    return grads * cosine + turned
 
 
 def mm(left, right):
@@ -761,6 +740,15 @@
     )
 
 
+def square_tile(value):
+    value = value * value
+    total = jnp.zeros((8, 128), F32)
+    for r in range(0, value.shape[0], 8):
+        for c in range(0, value.shape[1], 128):
+            total = total + value[r : r + 8, c : c + 128]
+    return total
+
+
 class Scatter:
     def __init__(self, net, grads, stay, came, last):
         self.net, self.grads, self.stay, self.came, self.last = net, grads, stay, came, last
@@ -801,14 +789,15 @@
                 both[d % 2] = both[d % 2] + self.last[d - 1, at].astype(F32)
             for parity in range(2):
                 total[parity, at] = both[parity]
+                state = state + square_tile(both[parity])
             return state
 
-        in_steps(self.wrows, collect)
+        square = in_steps(self.wrows, collect, jnp.zeros((8, 128), F32))
         copies = []
         for parity in range(2):
             half = (self.net.zl + parity) % 2
             copies.append(self.net.move(total.at[parity], sums.at[:, pl.ds(pl.multiple_of(half * self.width, self.width), self.width)]))
-        return copies
+        return copies, square
 
     def whole(self, out):
         self.landed()
@@ -832,7 +821,7 @@
 
 def back_kernel(
     n_dp, n_mp, part, hid, att, gains, out_grad, live, grads, grads_up,
-    ghid, dg1, dg2, seq, sums, sums_up,
+    ghid, dg1, dg2, seq, sums, sums_up, squares,
     near, r1, r2, r3, own, stay, came, last, ustay, ucame, ulast, total, ss, rs, ls,
 ):
     net = Net(n_dp, n_mp, ss, rs, ls)
@@ -873,11 +862,13 @@
     weight_up.along_z(weight_up.turns[:1])
     finish()
     weight_up.along_z(weight_up.turns[1:2])
-    first_out = weight.halves(total, sums)
+    first_out, square = weight.halves(total, sums)
     weight_up.along_z(weight_up.turns[2:])
     for copy in first_out:
         copy.wait()
-    for copy in weight_up.halves(total, sums_up):
+    last_out, square_up = weight_up.halves(total, sums_up)
+    squares[...] = square + square_up
+    for copy in last_out:
         copy.wait()
     net.close()
 
@@ -893,9 +884,9 @@
         [
             jax.ShapeDtypeStruct(block, F32), jax.ShapeDtypeStruct((1, D), F32), jax.ShapeDtypeStruct((1, D), F32),
             jax.ShapeDtypeStruct((4,) + block, BF), jax.ShapeDtypeStruct((wrows, 2 * width), F32),
-            jax.ShapeDtypeStruct((wrows, 2 * width), F32),
+            jax.ShapeDtypeStruct((wrows, 2 * width), F32), jax.ShapeDtypeStruct((8, 128), F32),
         ],
-        [VMEM, VMEM, VMEM, ANY, ANY, ANY], [ANY] + [VMEM] * 5 + [ANY, ANY],
+        [VMEM, VMEM, VMEM, ANY, ANY, ANY, VMEM], [ANY] + [VMEM] * 5 + [ANY, ANY],
         pair_scratch(rows, 4) + scatter_scratch(nj, wrows, width) * 2
         + [pltpu.VMEM((2, wrows, width), F32), dma(count), dma(count), dma(16 + 2 * nj)],
         5, 60,
@@ -942,9 +933,9 @@
 
 def close_kernel(
     n_dp, n_mp, seq_grad, seq_normed, q, k, v, mixed, wo, wq, wkv, cosine, sine, marks_col, marks_row,
-    inputs, gains, ghid,
-    gin, dg0, sum_q, sum_kv, sum_o,
-    tokens, normed, wa, gm, dq, dk, dv, dkv, go, gq, gkv, got_q, got_kv, r1, r2,
+    inputs, gains, ghid, terms_in, sum_down, squares,
+    gin, sum_q, sum_kv, sum_o, gain_sum, norm,
+    terms, got_terms, down, mine, got_squares, tokens, normed, wa, gm, dq, dk, dv, dkv, go, gq, gkv, got_q, got_kv, r1, r2,
     ostay, ocame, olast, ss, rs, ls,
 ):
     net = Net(n_dp, n_mp, ss, rs, ls)
@@ -954,7 +945,13 @@
     nj = n_dp // 2
     rows = inputs.shape[0]
     seq_len, wrows = tokens.shape[0], sum_q.shape[0]
-    net.meet(all_of_dp(net))
+    wide0 = terms.shape[2]
+    others = everyone(n_dp, n_mp, net.i, net.m)
+    flat = net.i * n_mp + net.m
+    per_norm = n_dp * n_mp // NORMS
+    terms_load = net.move(terms_in, terms.at[pl.ds(per_norm, (NORMS - 1) * per_norm)])
+    down_load = net.move(sum_down, down)
+    net.meet(others)
     token_load = net.move(seq_grad, tokens)
     wa_load = net.move(wo, wa)
     normed_load = net.move(seq_normed, normed)
@@ -999,8 +996,8 @@
     parts = two_parts(wrows)
     flight = {}
     for part in parts:
-        for lane, (terms, got, _, device, way) in enumerate(lanes):
-            flight[lane, part] = net.send(terms.at[block(way, part)], got.at[0, pl.ds(*part)], device)
+        for lane, (ref, got, _, device, way) in enumerate(lanes):
+            flight[lane, part] = net.send(ref.at[block(way, part)], got.at[0, pl.ds(*part)], device)
 
     def hop(n):
         end = n == n_dp - 1
@@ -1059,42 +1056,76 @@
         gin[at] = gin[at] + part
         return state + d0
 
-    dg0[...] = by_rows(rows, rows_in, jnp.zeros((1, D), F32))
+    dg0 = by_rows(rows, rows_in, jnp.zeros((1, D), F32))
+    terms_load.wait()
+    for n in range(per_norm):
+        terms[n] = dg0[:, n * wide0 : (n + 1) * wide0]
+    spread = [net.send(terms.at[dp * n_mp + mp], got_terms.at[flat], (dp, mp)) for dp, mp in others]
+    own_terms = net.move(terms.at[flat], got_terms.at[flat])
     for n in range(4, n_dp - 1):
         hop(n)
+    down_load.wait()
+
+    def square_of(ref, state):
+        return lax.fori_loop(
+            0, ref.shape[0] // 8,
+            lambda t, total: total + square_tile(ref[pl.ds(pl.multiple_of(t * 8, 8), 8)]), state,
+        )
+
+    square = square_of(down, squares[...])
     out.whole(sum_o)
+    square = square_of(sum_o, square)
+    own_terms.wait()
+    for copy in spread:
+        copy.wait_recv()
+    total_gain = lax.fori_loop(
+        0, n_dp * n_mp, lambda t, total: total + got_terms[t], jnp.zeros(got_terms.shape[1:], F32)
+    )
+    gain_sum[...] = total_gain
+    square = square + jnp.sum(total_gain * total_gain) * (1.0 / 1024.0)
     hop(n_dp - 1)
+    mine[...] = square_of(sum_kv, square_of(sum_q, square))
+    spread = [net.send(mine, got_squares.at[flat], device) for device in others]
+    net.move(mine, got_squares.at[flat]).wait()
+    for copy in spread:
+        copy.wait_recv()
+    total = lax.fori_loop(0, n_dp * n_mp, lambda t, value: value + got_squares[t], jnp.zeros((8, 128), F32))
+    norm[...] = jnp.broadcast_to(jnp.sqrt(jnp.sum(total, axis=(0, 1), keepdims=True)), (8, 128))
     net.close()
 
 
 def close(n_dp, n_mp, seq_grad, seq_normed, q, k, v, mixed, wo, wq, wkv, cosine, sine, marks_col, marks_row,
-          inputs, gains, ghid):
+          inputs, gains, ghid, terms, sum_down, squares):
     rows = inputs.shape[0]
     nj = n_dp // 2
     wrows = D // n_dp
     cols, kv_cols = q.shape[1], k.shape[1]
     seq_len = q.shape[0]
-    count = 16 + 6 * nj + 4 * n_dp
+    devices = n_dp * n_mp
+    count = 16 + 6 * nj + 4 * n_dp + 2 * devices
+    piece = (1, NORMS * D // devices)
     vm = lambda *shape: pltpu.VMEM(shape, BF)
     small = jax.ShapeDtypeStruct((wrows, cols), F32)
     return call(
         functools.partial(close_kernel, n_dp, n_mp),
         [
-            jax.ShapeDtypeStruct((rows, D), F32), jax.ShapeDtypeStruct((1, D), F32), small,
-            jax.ShapeDtypeStruct((wrows, 2 * kv_cols), F32), small,
+            jax.ShapeDtypeStruct((rows, D), F32), small, jax.ShapeDtypeStruct((wrows, 2 * kv_cols), F32), small,
+            jax.ShapeDtypeStruct(piece, F32), jax.ShapeDtypeStruct((8, 128), F32),
         ],
-        [VMEM] * 5,
-        [ANY, ANY] + [VMEM] * 4 + [ANY, ANY] + [VMEM] * 7 + [ANY],
+        [VMEM] * 6,
+        [ANY, ANY] + [VMEM] * 4 + [ANY, ANY] + [VMEM] * 7 + [ANY] * 3 + [VMEM],
         [
+            pltpu.VMEM((devices,) + piece, F32), pltpu.VMEM((devices,) + piece, F32),
+            pltpu.VMEM(sum_down.shape, F32), pltpu.VMEM((8, 128), F32), pltpu.VMEM((devices, 8, 128), F32),
             vm(seq_len, D), vm(seq_len, D), vm(D, cols), vm(seq_len, cols), vm(seq_len, cols),
             pltpu.VMEM((seq_len, kv_cols), F32), pltpu.VMEM((seq_len, kv_cols), F32), vm(seq_len, 2 * kv_cols),
             vm(nj, 2, wrows, cols), vm(D, cols), vm(D, 2 * kv_cols),
             vm(n_dp - 1, wrows, cols), vm(n_dp - 1, wrows, 2 * kv_cols), vm(2, rows, D), vm(rows, D),
         ]
-        + scatter_scratch(nj, wrows, cols) + [dma(count), dma(count), dma(10 + 2 * nj)],
+        + scatter_scratch(nj, wrows, cols) + [dma(count), dma(count), dma(14 + 2 * nj)],
         6, 60,
     )(seq_grad, seq_normed, q, k, v, mixed, wo, wq, wkv, cosine, sine, marks_col, marks_row,
-      inputs, gains, ghid)
+      inputs, gains, ghid, terms, sum_down, squares)
 
 
 def plain(kernel, grid, outs, out_specs, in_specs, mb, flops):
@@ -1149,66 +1180,10 @@
     )(grad, gate, up, wg, wu, wd)
 
 
-def norm_kernel(
-    n_dp, n_mp, terms, g_gate, g_up, g_down, g_q, g_o, g_kv, gain_sum, norm, *refs,
-):
-    grads, (got, sgot, mine, ss, rs, ls) = refs[:6], refs[6:]
-    net = Net(n_dp, n_mp, ss, rs, ls)
-    others = everyone(n_dp, n_mp, net.i, net.m)
-    loads = [net.move(src, dst) for src, dst in zip((g_gate, g_up, g_down, g_q, g_o, g_kv), grads)]
-    net.meet(others)
-    flat = net.i * n_mp + net.m
-    copies = [net.send(terms.at[dp * n_mp + mp], got.at[flat], (dp, mp)) for dp, mp in others]
-    own = net.move(terms.at[flat], got.at[flat])
-    square = jnp.zeros((8, 128), F32)
-    for load, grad in zip(loads, grads):
-        load.wait()
-        rows, cols = grad.shape
-
-        def add(t, state, grad=grad, cols=cols):
-            value = grad[pl.ds(pl.multiple_of(t * 8, 8), 8)]
-            value = value * value
-            for n in range(0, cols, 128):
-                state = state + value[:, n : n + 128]
-            return state
-
-        square = lax.fori_loop(0, rows // 8, add, square)
-    own.wait()
-    for copy in copies:
-        copy.wait_recv()
-    gain = lax.fori_loop(0, n_dp * n_mp, lambda t, s: s + got[t], jnp.zeros(got.shape[1:], F32))
-    gain_sum[...] = gain
-    mine[...] = square + jnp.sum(gain * gain) * (1.0 / 1024.0)
-    copies = [net.send(mine, sgot.at[flat], device) for device in others]
-    own = net.move(mine, sgot.at[flat])
-    own.wait()
-    for copy in copies:
-        copy.wait_recv()
-    total = lax.fori_loop(0, n_dp * n_mp, lambda t, s: s + sgot[t], jnp.zeros((8, 128), F32))
-    norm[...] = jnp.broadcast_to(jnp.sqrt(jnp.sum(total, axis=(0, 1), keepdims=True)), (8, 128))
-    net.close()
-
-
-def norm_all(n_dp, n_mp, terms, grads):
-    total = n_dp * n_mp
-    shape = terms.shape[1:]
-    return call(
-        functools.partial(norm_kernel, n_dp, n_mp),
-        [jax.ShapeDtypeStruct(shape, F32), jax.ShapeDtypeStruct((8, 128), F32)],
-        [VMEM] * 2, [VMEM] + [ANY] * 6,
-        [pltpu.VMEM(a.shape, F32) for a in grads]
-        + [
-            pltpu.VMEM((total,) + shape, F32), pltpu.VMEM((total, 8, 128), F32), pltpu.VMEM((8, 128), F32),
-            dma(2 * total), dma(2 * total), dma(8),
-        ],
-        7, 32,
-    )(terms, *grads)
-
-
 def adam_kernel(norm, gain_grad, gw, gm, gv, g_gate, g_up, g_down, g_q, g_o, g_kv, *refs):
     ins, gain_outs, outs = refs[:9], refs[9:12], refs[12:]
     factor = jnp.minimum(1.0, CLIP_SCALE * math.sqrt(PARAMS) / norm[0:1, 0:1])
-    news = adam_update(gw[...], gm[...], gv[...], gain_grad[...], factor)
+    news = adam_update(gw[...], gm[...], gv[...], gain_grad[0], factor[0])
     for out, new in zip(gain_outs, news):
         out[...] = new
     kv_cols = ins[6].shape[2]
@@ -1229,7 +1204,7 @@
     wrows = grads[0].shape[0]
     step = 48 if wrows % 48 == 0 else 8
     like = lambda a: jax.ShapeDtypeStruct(a.shape, F32)
-    fixed = lambda a: pl.BlockSpec(a.shape, lambda t: (0, 0))
+    fixed = lambda a: pl.BlockSpec(a.shape, lambda t: (0,) * a.ndim)
     flat = lambda a: pl.BlockSpec((step, a.shape[1]), lambda t: (t, 0))
     deep = lambda a: pl.BlockSpec((a.shape[0], step, a.shape[2]), lambda t: (0, t, 0))
     return plain(
@@ -1276,14 +1251,13 @@
         low_kv = jnp.concatenate([quantize(w_kv[0], D, bit_sel[1]), quantize(w_kv[1], D, bit_sel[1])], 1)
         order = jnp.stack([m, m ^ 2, m ^ 1, m ^ 3])
 
-        def in_order(vector):
-            return vector.reshape(n_mp, rows)[order].reshape(-1)
-
         segments = segment_ids[0]
-        positions = in_order(doc_positions(segments))
-        slots = in_order(jnp.arange(seq_len, dtype=jnp.int32))
-        segs = in_order(segments)
-        pads = in_order(pad_mask[0])
+        every = jnp.arange(seq_len, dtype=jnp.int32)
+        same = segments[:, None] == segments[None, :]
+        begins = jnp.min(jnp.where(same, every[None, :], seq_len), axis=1)
+        facts = jnp.stack([segments, pad_mask[0], every - begins]).reshape(3, n_mp, rows)
+        segs, pads, positions = facts[:, order].reshape(3, seq_len)
+        slots = (order[:, None] * rows + jnp.arange(rows, dtype=jnp.int32)[None, :]).reshape(-1)
         kv_cols = w_kv.shape[2]
         half_dim = HEAD_WIDTH // 2
         frequency = ROPE_BASE ** (-jnp.arange(half_dim, dtype=F32) * 2.0 / HEAD_WIDTH)
@@ -1310,11 +1284,12 @@
         down_stay, down_came = scatter_first(grad_down, y)
         grad_gate, grad_up, part = mlp_back(group_grad, gate, up, w_gate, w_up, w_down)
         flat_ffn = group_ffn.reshape(tokens, D)
+        grad_gate, grad_up, down_came = lax.optimization_barrier((grad_gate, grad_up, down_came))
+        down_own, down_shifted = scatter_second(down_stay, down_came, j)
         grads_gate = mm_rows(flat_ffn, grad_gate.reshape(tokens, -1)).astype(BF).reshape(nj, 2, wrows, -1)
-        grads_gate, grad_up, down_came = lax.optimization_barrier((grads_gate, grad_up, down_came))
-        down_own, down_shifted = scatter_second(down_stay, down_came, j)
+        grads_gate, grad_up = lax.optimization_barrier((grads_gate, grad_up))
         grads_up = mm_rows(flat_ffn, grad_up.reshape(tokens, -1)).astype(BF).reshape(nj, 2, wrows, -1)
-        grad_hidden, grad_gain_one, grad_gain_two, seq_grad, sum_gate, sum_up = back(
+        grad_hidden, grad_gain_one, grad_gain_two, seq_grad, sum_gate, sum_up, squares = back(
             n_dp, n_mp, part, hidden_in, attended, gain_rows, out_grad, live,
             grads_gate, grads_up
         )
@@ -1325,19 +1300,19 @@
         sum_down = jnp.concatenate(
             [jnp.where(zl == 0, sums[0], sums[1]), jnp.where(zl == 0, sums[1], sums[0])], 1
         )
-        grad_in, grad_gain_zero, sum_q, sum_kv, sum_o = close(
+        terms = jnp.concatenate([grad_gain_one, grad_gain_two, grad_gain_three])
+        terms = terms.reshape((NORMS - 1) * n_dp * n_mp // NORMS, 1, -1)
+        grad_in, sum_q, sum_kv, sum_o, sum_gains, norm = close(
             n_dp, n_mp, seq_grad.reshape(seq_len, D), seq_normed, query_bf, key_bf, value_bf, mixed_bf,
             wo, wq, wkv, cosine, sine, marks.T, marks, inputs, gain_rows, grad_hidden,
+            terms, sum_down, squares,
         )
-        terms = jnp.concatenate([grad_gain_zero, grad_gain_one, grad_gain_two, grad_gain_three])
-        flat_gains = [a.reshape(1, -1) for a in (norm_gains, m_gains, v_gains)]
         sums = [sum_gate, sum_up, sum_down, sum_q, sum_o, sum_kv]
-        sum_gains, norm = norm_all(n_dp, n_mp, terms.reshape(n_dp * n_mp, 1, -1), sums)
         news = adam_all(
-            norm, sum_gains, flat_gains, sums, [w_mlp, m_mlp, v_mlp, w_qo, m_qo, v_qo, w_kv, m_kv, v_kv]
+            norm, sum_gains, [norm_gains, m_gains, v_gains], sums, [w_mlp, m_mlp, v_mlp, w_qo, m_qo, v_qo, w_kv, m_kv, v_kv]
         )
         grad_norm = norm[0, :1]
-        new_gains, new_m_gains, new_v_gains = [a.reshape(-1) for a in news[:3]]
+        new_gains, new_m_gains, new_v_gains = news[:3]
         new_w_mlp, new_m_mlp, new_v_mlp, new_w_qo, new_m_qo, new_v_qo, new_w_kv, new_m_kv, new_v_kv = news[3:]
         return (
             outputs, grad_in, grad_norm, new_w_qo, new_w_kv, new_w_mlp, new_gains,

time: 856 us -> 844 us (0.986)
  Pallas kernels: 745 us -> 728 us
  waiting for transfers between devices: 0.01 us -> 11.3 us
    pallas_call x1 -> x0, Pallas kernels: 14.7 us -> none  [norm_all(): call(functools.partial(norm_kernel, n_dp, n_mp), [jax.ShapeDtypeStruct(sh...]
    ppermute x1, waiting for transfers between devices: 0.01 us -> 11.3 us  [y_swap(): return lax.ppermute(value, 'dp', [(k, k ^ 1) for k in range(n_dp)])]
  transfers between devices with their start and end apart: 4 -> 4, of which waited for: 0 -> 1; matrix products, arithmetic and copies ran while one was open for 4% -> 4% of each run, Pallas kernels for 23% -> 23%
where the time goes in v5:
time: 844 us; the launch traced here: 830 us
  Pallas kernels  728 us (86%)
  matrix products  45.5 us (5%)
  other arithmetic  16.8 us (2%)
  local copies, waits for them, and re-layouts  14.4 us (2%)
  waiting for transfers between devices  11.3 us (1%)
  starting transfers between devices  8.69 us (1%)
    pallas_call x1, Pallas kernels, open_layer(): call(functools.partial(open_kernel, n_dp, n_mp), [bf(total, cols), bf(tot...  286 us
    pallas_call x1, Pallas kernels, back(): call(functools.partial(back_kernel, n_dp, n_mp), [jax.ShapeDtypeStruct(bl...  145 us
    pallas_call x1, Pallas kernels, close(): call(functools.partial(close_kernel, n_dp, n_mp), [jax.ShapeDtypeStruct((...  125 us
    pallas_call x1, Pallas kernels, turn(): call(functools.partial(turn_kernel, n_dp, n_mp), [jax.ShapeDtypeStruct(bl...  100 us
    pallas_call x1, Pallas kernels, mlp_back(): plain(down_back_kernel, (blocks,), [jax.ShapeDtypeStruct(shape, BF), jax....  48 us
    dot_general x3, matrix products, mm_rows(): lax.dot_general(left, right, (((0,), (0,)), ((), ())), preferred_element_...  45.5 us
    pallas_call x1, Pallas kernels, adam_all(): plain(adam_kernel, (wrows // step,), [like(a) for a in gains] + [like(a)...  24.7 us
  transfers between devices with their start and end apart: 4, of which 1 were waited for; matrix products, arithmetic and copies ran while one was open for 4% of the time, Pallas kernels for 23%

profile of v5, /device:TPU:0, one launch (start us, length us, event | category | flops | bytes accessed | tf_op | source)
XLA Modules:
  0.0 829.6 jit_solution(6707711795508661122)
XLA Ops:
  0.7 0.8 reduce
  2.2 1.4 fusion.14
  9.6 1.0 copy.39.marks_col
  10.7 1.2 reshape.406.own_gains
  11.9 0.8 fusion.12
  12.7 0.8 copy.40.live
  13.5 1.3 fusion.8
  15.5 2.6 multiply_sine_fusion
  18.1 1.3 fusion.7
  19.4 285.8 %shard_map.280 = (bf16[896,512]{1,0:T(8,128)(2,1)}, bf16[896,256]{1,0:T(8,128)(2,1)}, bf16[896,256]{1,0:T(8,128)(2,1)}, bf16[896,512]{1,0:T(8,128)(2,1)}, f32[22...) custom-call(bf16[288,512]{1,0:T(8,128)(2,1)} %get-tuple-element.143., ...), custom_call_target="tpu_custom_call" | custom-call | tf_op jit(solution)/shard_map/pallas_call | solution.py:526
  305.1 100.2 %shard_map.281 = (f32[224,2304]{1,0:T(8,128)}, f32[1,2304]{1,0:T(1,128)}, f32[8,224,1152]{2,1,0:T(8,128)}, f32[8,224,1152]{2,1,0:T(8,128)}, bf16[8,224,1152]{2,1...) custom-call(bf16[8,224,2304]{2,1,0:T(8,128)(2,1)} %get-tuple-element.75.ffn, bf16[2304,1152]{1,0:T(8,128)(2,1)} %bitcast.68, ...), custom_call_target="tpu_custom_call" | custom-call | tf_op jit(solution)/shard_map/pallas_call | solution.py:717
  405.3 16.3 %fusion = bf16[2304,1152]{1,0:T(8,128)(2,1)} fusion(bf16[8,224,2304]{2,1,0:T(8,128)(2,1)} %get-tuple-element.84.grad, bf16[8,224,1152]{2,1,0:T(8,128)(2,1)} %get-tuple-element.83), kind=kOutput, calls=%fused_computation.4 | convolution fusion | flops 9515335680 | bytes 17694720 | tf_op jit(solution)/shard_map/dot_general | solution.py:73
  421.7 2.0 dynamic-slice_bitcast_fusion
  423.6 0.9 collective-permute-start
  424.5 48.0 %shard_map.282 = (bf16[8,224,1152]{2,1,0:T(8,128)(2,1)}, bf16[8,224,1152]{2,1,0:T(8,128)(2,1)}, bf16[8,224,2304]{2,1,0:T(8,128)(2,1)}) custom-call(bf16[8,224,2304]{2,1,0:T(8,128)(2,1)} %get-tuple-element.84.grad, f32[8,224,1152]{2,1,0:T(8,128)} %get-tuple-element.85.gate, f32[8,224,1152]{2,1,0:T(8,128)} %get-tuple-element.86.up, ...), custom_call_target="tpu_custom_call" | custom-call | flops 28538044416 | bytes 41943040 | tf_op jit(solution)/shard_map/pallas_call | solution.py:1174
  472.4 11.3 %collective-permute-done = bf16[4,288,1152]{2,1,0:T(8,128)(2,1)} collective-permute-done((bf16[4,288,1152]{2,1,0:T(8,128)(2,1)S(1)}, bf16[4,288,1152]{2,1,0:T(8,128)(2,1)}, u32[]{:S(2)}, u32[]{:S(2)}) %collective-permute-start) | collective-permute-done | bytes 2654240 | tf_op jit(solution)/shard_map/ppermute | solution.py:1222
  483.7 3.4 fusion.3
  487.0 1.2 dynamic-slice_bitcast_fusion.1
  488.3 1.1 collective-permute-start.1
  489.3 5.4 collective-permute-start.2
  494.7 1.4 collective-permute-start.3
  496.1 16.2 %fusion.1 = bf16[2304,1152]{1,0:T(8,128)(2,1)} fusion(bf16[8,224,2304]{2,1,0:T(8,128)(2,1)} %get-tuple-element.75.ffn, bf16[8,224,1152]{2,1,0:T(8,128)(2,1)S(1)} %copy-done.6), kind=kOutput, calls=%fused_computation.5 | convolution fusion | flops 9515335680 | bytes 17694720 | tf_op jit(solution)/shard_map/dot_general | solution.py:73
  512.3 13.0 %fusion.2 = bf16[2304,1152]{1,0:T(8,128)(2,1)} fusion(bf16[8,224,2304]{2,1,0:T(8,128)(2,1)S(1)} %bitcast.67, bf16[8,224,1152]{2,1,0:T(8,128)(2,1)S(1)} %copy-done.5), kind=kOutput, calls=%fused_computation.6 | convolution fusion | flops 9515335680 | bytes 17694720 | tf_op jit(solution)/shard_map/dot_general | solution.py:73
  525.3 144.6 %shard_map.283 = (f32[224,2304]{1,0:T(8,128)}, f32[1,2304]{1,0:T(1,128)}, f32[1,2304]{1,0:T(1,128)}, bf16[4,224,2304]{2,1,0:T(8,128)(2,1)}, f32[288,2304]{1,0:T(...) custom-call(bf16[8,224,2304]{2,1,0:T(8,128)(2,1)} %get-tuple-element.87.part, f32[224,2304]{1,0:T(8,128)} %get-tuple-element.79.hid, ...), custom_call_target="tpu_custom_call" | custom-call | tf_op jit(solution)/shard_map/pallas_call | solution.py:882
  671.4 1.8 fusion.5
  673.3 1.8 pad_maximum_fusion.sum_down.g_down
  675.0 124.8 %shard_map.284 = (f32[224,2304]{1,0:T(8,128)}, f32[288,512]{1,0:T(8,128)}, f32[288,512]{1,0:T(8,128)}, f32[288,512]{1,0:T(8,128)}, f32[1,288]{1,0:T(1,128)}, /*index=5*/f32[8,128]{1,0:T(8,128)}) custom-call(bf16[896,2304]{1,0:T(8,128)(2,1)} %bitcast.78, bf16[896,2304]{1,0:T(8,128)(2,1)} %get-tuple-element.99.seq_normed, ...), custom_call_target="tpu_custom_call" | custom-call | tf_op jit(solution)/shard_map/pallas_call | solution.py:1109
  799.9 1.2 slice.36
  801.0 24.7 %shard_map.285 = (f32[288]{0:T(512)}, f32[288]{0:T(512)}, f32[288]{0:T(512)}, f32[3,288,2304]{2,1,0:T(8,128)}, f32[3,288,2304]{2,1,0:T(8,128)}, /*index=5*/f32[3...) custom-call(f32[8,128]{1,0:T(8,128)} %get-tuple-element.116.norm, ...), custom_call_target="tpu_custom_call" | custom-call | flops 100 | bytes 41943040 | tf_op jit(solution)/shard_map/pallas_call | solution.py:1210
  825.8 1.3 copy.48
  827.1 1.0 copy-done.2
  828.1 1.3 copy.49
  (44 shorter events, 5.2 us)
Async XLA Ops:
  0.6 17.5 %copy-start = (f32[2,288,512]{2,1,0:T(8,128)S(1)}, f32[2,288,512]{2,1,0:T(8,128)}, u32[]{:S(2)}) copy-start(f32[2,288,512]{2,1,0:T(8,128)} %refs_3_.1) | copy-start | bytes 3538948
  9.6 9.7 %copy-start.3 = (s32[8,896]{1,0:T(8,128)}, s32[8,896]{1,0:T(8,128)S(1)}, u32[]{:S(2)}) copy-start(s32[8,896]{1,0:T(8,128)S(1)} %stack.49.marks_row) | copy-start | bytes 86020
  423.6 60.1 %collective-permute-start = (bf16[4,288,1152]{2,1,0:T(8,128)(2,1)S(1)}, bf16[4,288,1152]{2,1,0:T(8,128)(2,1)}, u32[]{:S(2)}, u32[]{:S(2)}) collective-permute-start(bf16[4,288,1152]{2,1,0:T(8,128)(2,1)S(1)} %dynamic-slice_bitcast_fusion), channel_id=1, source_target_pairs={{0,4},{4,0},{8,12},{12,8},{16,20},{20,16},{24,28},{28,24},{1,5},{5... | collective-permute-start | bytes 7962632 | tf_op jit(solution)/shard_map/ppermute | solution.py:1222
  483.7 12.4 %copy-start.6 = (bf16[8,224,1152]{2,1,0:T(8,128)(2,1)S(1)}, bf16[8,224,1152]{2,1,0:T(8,128)(2,1)}, u32[]{:S(2)}) copy-start(bf16[8,224,1152]{2,1,0:T(8,128)(2,1)} %get-tuple-element.92) | copy-start | bytes 12386308
  488.3 183.2 %collective-permute-start.1 = (bf16[288,1152]{1,0:T(8,128)(2,1)}, bf16[288,1152]{1,0:T(8,128)(2,1)}, u32[]{:S(2)}, u32[]{:S(2)}) collective-permute-start(bf16[288,1152]{1,0:T(8,128)(2,1)} %get-tuple-element.141), channel_id=1, source_target_pairs={{0,8},{4,12},{8,16},{12,20},{16,24},{20,28},{24,0},{28,4},{1,9},{5... | collective-permute-start | bytes 1990664 | tf_op jit(solution)/shard_map/ppermute | solution.py:1226
  489.3 182.1 %collective-permute-start.2 = (bf16[288,1152]{1,0:T(8,128)(2,1)}, bf16[288,1152]{1,0:T(8,128)(2,1)}, u32[]{:S(2)}, u32[]{:S(2)}) collective-permute-start(bf16[288,1152]{1,0:T(8,128)(2,1)} %get-tuple-element.140), channel_id=1, source_target_pairs={{0,16},{4,20},{8,24},{12,28},{16,0},{20,4},{24,8},{28,12},{1,17},{... | collective-permute-start | bytes 1990664 | tf_op jit(solution)/shard_map/ppermute | solution.py:1226
  494.7 17.6 %slice-start = ((s8[8257536]{0:T(1024)(128)(4,1)}), s8[4194304]{0:T(1024)(128)(4,1)S(1)}, s32[]{:S(2)}) async-start(s8[8257536]{0:T(1024)(128)(4,1)} %bitcast.66), calls=%async_computation | async-start | bytes 8388608
  494.7 17.6 %slice-start.1 = ((s8[8257536]{0:T(1024)(128)(4,1)}), s8[4063232]{0:T(1024)(128)(4,1)S(1)}, s32[]{:S(2)}) async-start(s8[8257536]{0:T(1024)(128)(4,1)} %bitcast.66), calls=%async_computation.1 | async-start | bytes 8126464
  494.7 17.6 %copy-start.5 = (bf16[8,224,1152]{2,1,0:T(8,128)(2,1)S(1)}, bf16[8,224,1152]{2,1,0:T(8,128)(2,1)}, u32[]{:S(2)}) copy-start(bf16[8,224,1152]{2,1,0:T(8,128)(2,1)} %get-tuple-element.95) | copy-start | bytes 12386308
  494.7 176.7 %collective-permute-start.3 = (bf16[288,1152]{1,0:T(8,128)(2,1)S(1)}, bf16[288,1152]{1,0:T(8,128)(2,1)}, u32[]{:S(2)}, u32[]{:S(2)}) collective-permute-start(bf16[288,1152]{1,0:T(8,128)(2,1)S(1)} %get-tuple-element.139), channel_id=1, source_target_pairs={{0,24},{4,28},{8,0},{12,4},{16,8},{20,12},{24,16},{28,20},{1,25},{... | collective-permute-start | bytes 1990664 | tf_op jit(solution)/shard_map/ppermute | solution.py:1226
  525.3 144.6 %copy-start.4 = (f32[1,2304]{1,0:T(1,128)S(1)}, f32[1,2304]{1,0:T(1,128)}, u32[]{:S(2)}) copy-start(f32[1,2304]{1,0:T(1,128)} %get-tuple-element.110) | copy-start | bytes 27652
  801.0 24.7 %copy-start.1 = (f32[224,2304]{1,0:T(8,128)S(1)}, f32[224,2304]{1,0:T(8,128)}, u32[]{:S(2)}) copy-start(f32[224,2304]{1,0:T(8,128)} %get-tuple-element.166) | copy-start | bytes 6193156
  825.7 2.3 copy-start.2

commit v6 on v5

--- a/solution.py
+++ b/solution.py
@@ -326,9 +326,9 @@
             part[pair * 2 + 1, :, n : n + wide] = got[rows:]
 
 
-def chunks(wrows):
-    if wrows % 48 == 0:
-        return tuple((n * wrows // 3, wrows // 3) for n in range(3))
+def chunks(wrows, parts=3):
+    if wrows % (16 * parts) == 0:
+        return tuple((n * wrows // parts, wrows // parts) for n in range(parts))
     return ((0, upper(wrows)), (upper(wrows), wrows - upper(wrows)))
 
 
@@ -434,8 +434,8 @@
         rows_at = pl.ds(first, count)
         pieces.append((lambda which: ref.at[rows_at, half(which)], lambda at: full.at[at, rows_at], 2))
 
-    for ref, full in ((lows.at[0], full0), (lows.at[1], full1), (lows.at[2], full2)):
-        for first, count in chunks(wrows):
+    for ref, full, cuts in ((lows.at[0], full0, 3), (lows.at[1], full1, 3), (lows.at[2], full2, 6)):
+        for first, count in chunks(wrows, cuts):
             add_piece(ref, full, first, count)
     weights = Gather(net, pieces)
     for hop in range(1, n_dp):
@@ -514,7 +514,7 @@
     rows = inputs.shape[0]
     nj = n_dp // 2
     total_devices = n_dp * n_mp
-    count = 24 + 4 * n_dp + 20 * nj + total_devices
+    count = 24 + 4 * n_dp + 28 * nj + total_devices
     block = (rows, D)
     wrows, width = w_mlp.shape[1], w_mlp.shape[2] // 2
     cols, kv_cols = low_q.shape[1], low_kv.shape[1] // 2
@@ -1168,16 +1168,19 @@
 
 
 def mlp_back(grad, gate, up, wg, wu, wd):
-    blocks, rows, _ = grad.shape
+    real_blocks, real_rows, _ = grad.shape
     width = wg.shape[1]
+    blocks, rows = real_blocks // 2, real_rows * 2
+    grad, gate, up = (a.reshape(blocks, rows, a.shape[2]) for a in (grad, gate, up))
     shape = (blocks, rows, width)
-    return plain(
+    dgate, dup, part = plain(
         down_back_kernel, (blocks,),
         [jax.ShapeDtypeStruct(shape, BF), jax.ShapeDtypeStruct(shape, BF), jax.ShapeDtypeStruct((blocks, rows, D), BF)],
         [tile(rows, width), tile(rows, width), tile(rows, D)],
         [tile(rows, D), tile(rows, width), tile(rows, width)] + [whole(wg.shape)] * 3, 56,
         6 * blocks * rows * D * width,
     )(grad, gate, up, wg, wu, wd)
+    return dgate, dup, part.reshape(real_blocks, real_rows, D)
 
 
 def adam_kernel(norm, gain_grad, gw, gm, gv, g_gate, g_up, g_down, g_q, g_o, g_kv, *refs):

time: 844 us -> 836 us (level)
  no operation moved by 1% of the time
where the time goes in v6:
time: 836 us; the launch traced here: 828 us
  Pallas kernels  728 us (87%)
  matrix products  44.5 us (5%)
  other arithmetic  16.8 us (2%)
  local copies, waits for them, and re-layouts  14.4 us (2%)
  waiting for transfers between devices  12.8 us (2%)
    pallas_call x1, Pallas kernels, open_layer(): call(functools.partial(open_kernel, n_dp, n_mp), [bf(total, cols), bf(tot...  289 us
    pallas_call x1, Pallas kernels, back(): call(functools.partial(back_kernel, n_dp, n_mp), [jax.ShapeDtypeStruct(bl...  144 us
    pallas_call x1, Pallas kernels, close(): call(functools.partial(close_kernel, n_dp, n_mp), [jax.ShapeDtypeStruct((...  125 us
    pallas_call x1, Pallas kernels, turn(): call(functools.partial(turn_kernel, n_dp, n_mp), [jax.ShapeDtypeStruct(bl...  99.7 us
    pallas_call x1, Pallas kernels, mlp_back(): plain(down_back_kernel, (blocks,), [jax.ShapeDtypeStruct(shape, BF), jax....  46.4 us
    dot_general x3, matrix products, mm_rows(): lax.dot_general(left, right, (((0,), (0,)), ((), ())), preferred_element_...  44.5 us
    pallas_call x1, Pallas kernels, adam_all(): plain(adam_kernel, (wrows // step,), [like(a) for a in gains] + [like(a)...  24.7 us
  transfers between devices with their start and end apart: 4, of which 1 were waited for; matrix products, arithmetic and copies ran while one was open for 4% of the time, Pallas kernels for 23%

profile of v6, /device:TPU:0, one launch (start us, length us, event | category | flops | bytes accessed | tf_op | source)
XLA Modules:
  0.0 827.9 jit_solution(1595892782130638375)
XLA Ops:
  0.7 0.8 reduce
  2.2 1.4 fusion.12
  9.6 1.0 copy.39.marks_col
  10.7 1.2 reshape.424.own_gains
  11.9 0.8 fusion.10
  12.7 0.8 copy.40.live
  13.5 1.3 fusion.6
  15.5 2.6 multiply_sine_fusion
  18.1 1.3 fusion.5
  19.4 288.8 %shard_map.280 = (bf16[896,512]{1,0:T(8,128)(2,1)}, bf16[896,256]{1,0:T(8,128)(2,1)}, bf16[896,256]{1,0:T(8,128)(2,1)}, bf16[896,512]{1,0:T(8,128)(2,1)}, f32[22...) custom-call(bf16[288,512]{1,0:T(8,128)(2,1)} %get-tuple-element.143., ...), custom_call_target="tpu_custom_call" | custom-call | tf_op jit(solution)/shard_map/pallas_call | solution.py:526
  308.1 99.7 %shard_map.281 = (f32[224,2304]{1,0:T(8,128)}, f32[1,2304]{1,0:T(1,128)}, f32[8,224,1152]{2,1,0:T(8,128)}, f32[8,224,1152]{2,1,0:T(8,128)}, bf16[8,224,1152]{2,1...) custom-call(bf16[8,224,2304]{2,1,0:T(8,128)(2,1)} %get-tuple-element.75.ffn, bf16[2304,1152]{1,0:T(8,128)(2,1)} %bitcast.70, ...), custom_call_target="tpu_custom_call" | custom-call | tf_op jit(solution)/shard_map/pallas_call | solution.py:717
  407.8 16.1 %fusion = bf16[2304,1152]{1,0:T(8,128)(2,1)} fusion(bf16[8,224,2304]{2,1,0:T(8,128)(2,1)} %get-tuple-element.84, bf16[8,224,1152]{2,1,0:T(8,128)(2,1)} %get-tuple-element.83), kind=kOutput, calls=%fused_computation.2 | convolution fusion | flops 9515335680 | bytes 17694720 | tf_op jit(solution)/shard_map/dot_general | solution.py:73
  423.9 2.0 dynamic-slice_bitcast_fusion
  425.9 0.9 collective-permute-start
  426.8 46.4 %shard_map.282 = (bf16[4,448,1152]{2,1,0:T(8,128)(2,1)}, bf16[4,448,1152]{2,1,0:T(8,128)(2,1)}, bf16[4,448,2304]{2,1,0:T(8,128)(2,1)}) custom-call(bf16[4,448,2304]{2,1,0:T(8,128)(2,1)} %bitcast.86, f32[4,448,1152]{2,1,0:T(8,128)} %bitcast.84, f32[4,448,1152]{2,1,0:T(8,128)} %bitcast.85, bf16[2304,1152]{1,0:T(8,128)(2,1)} %bitcast.71, ...), custom_call_target="tpu_custom_call" | custom-call | flops 28538044416 | bytes 41943040 | tf_op jit(solution)/shard_map/pallas_call | solution.py:1176
  473.2 12.8 %collective-permute-done = bf16[4,288,1152]{2,1,0:T(8,128)(2,1)} collective-permute-done((bf16[4,288,1152]{2,1,0:T(8,128)(2,1)S(1)}, bf16[4,288,1152]{2,1,0:T(8,128)(2,1)}, u32[]{:S(2)}, u32[]{:S(2)}) %collective-permute-start) | collective-permute-done | bytes 2654240 | tf_op jit(solution)/shard_map/ppermute | solution.py:1225
  486.0 3.4 fusion.1
  489.3 1.2 dynamic-slice_bitcast_fusion.1
  490.6 1.1 collective-permute-start.1
  491.7 2.7 collective-permute-start.2
  494.4 1.7 collective-permute-start.3
  496.1 15.4 %convolution_convert_fusion.1 = bf16[2304,1152]{1,0:T(8,128)(2,1)} fusion(bf16[1792,2304]{1,0:T(8,128)(2,1)} %bitcast.65, bf16[1792,1152]{1,0:T(8,128)(2,1)S(1)} %bitcast.88), kind=kOutput, calls=%fused_computation.4 | convolution fusion | flops 9515335680 | bytes 17694720 | tf_op jit(solution)/shard_map/dot_general | solution.py:73
  511.5 13.0 %convolution_convert_fusion = bf16[2304,1152]{1,0:T(8,128)(2,1)} fusion(bf16[1792,2304]{1,0:T(8,128)(2,1)S(1)} %bitcast.68, bf16[1792,1152]{1,0:T(8,128)(2,1)S(1)} %bitcast.87), kind=kOutput, calls=%fused_computation.3 | convolution fusion | flops 9515335680 | bytes 17694720 | tf_op jit(solution)/shard_map/dot_general | solution.py:73
  524.4 143.8 %shard_map.283 = (f32[224,2304]{1,0:T(8,128)}, f32[1,2304]{1,0:T(1,128)}, f32[1,2304]{1,0:T(1,128)}, bf16[4,224,2304]{2,1,0:T(8,128)(2,1)}, f32[288,2304]{1,0:T(...) custom-call(bf16[8,224,2304]{2,1,0:T(8,128)(2,1)} %bitcast.69, f32[224,2304]{1,0:T(8,128)} %get-tuple-element.79.hid, ...), custom_call_target="tpu_custom_call" | custom-call | tf_op jit(solution)/shard_map/pallas_call | solution.py:882
  669.7 1.8 fusion.3
  671.6 1.8 pad_maximum_fusion.sum_down.g_down
  673.3 124.6 %shard_map.284 = (f32[224,2304]{1,0:T(8,128)}, f32[288,512]{1,0:T(8,128)}, f32[288,512]{1,0:T(8,128)}, f32[288,512]{1,0:T(8,128)}, f32[1,288]{1,0:T(1,128)}, /*index=5*/f32[8,128]{1,0:T(8,128)}) custom-call(bf16[896,2304]{1,0:T(8,128)(2,1)} %bitcast.80, bf16[896,2304]{1,0:T(8,128)(2,1)} %get-tuple-element.99.seq_normed, ...), custom_call_target="tpu_custom_call" | custom-call | tf_op jit(solution)/shard_map/pallas_call | solution.py:1109
  798.0 1.2 slice.36
  799.1 24.7 %shard_map.285 = (f32[288]{0:T(512)}, f32[288]{0:T(512)}, f32[288]{0:T(512)}, f32[3,288,2304]{2,1,0:T(8,128)}, f32[3,288,2304]{2,1,0:T(8,128)}, /*index=5*/f32[3...) custom-call(f32[8,128]{1,0:T(8,128)} %get-tuple-element.116.norm, ...), custom_call_target="tpu_custom_call" | custom-call | flops 100 | bytes 41943040 | tf_op jit(solution)/shard_map/pallas_call | solution.py:1213
  823.9 1.3 copy.48
  825.2 1.0 copy-done.2
  826.2 1.3 copy.49
  (44 shorter events, 5.2 us)
Async XLA Ops:
  0.6 17.5 %copy-start = (f32[2,288,512]{2,1,0:T(8,128)S(1)}, f32[2,288,512]{2,1,0:T(8,128)}, u32[]{:S(2)}) copy-start(f32[2,288,512]{2,1,0:T(8,128)} %refs_3_.1) | copy-start | bytes 3538948
  9.6 9.7 %copy-start.3 = (s32[8,896]{1,0:T(8,128)}, s32[8,896]{1,0:T(8,128)S(1)}, u32[]{:S(2)}) copy-start(s32[8,896]{1,0:T(8,128)S(1)} %stack.49.marks_row) | copy-start | bytes 86020
  425.9 60.1 %collective-permute-start = (bf16[4,288,1152]{2,1,0:T(8,128)(2,1)S(1)}, bf16[4,288,1152]{2,1,0:T(8,128)(2,1)}, u32[]{:S(2)}, u32[]{:S(2)}) collective-permute-start(bf16[4,288,1152]{2,1,0:T(8,128)(2,1)S(1)} %dynamic-slice_bitcast_fusion), channel_id=1, source_target_pairs={{0,4},{4,0},{8,12},{12,8},{16,20},{20,16},{24,28},{28,24},{1,5},{5... | collective-permute-start | bytes 7962632 | tf_op jit(solution)/shard_map/ppermute | solution.py:1225
  486.0 10.1 %copy-start.6 = (bf16[4,448,1152]{2,1,0:T(8,128)(2,1)S(1)}, bf16[4,448,1152]{2,1,0:T(8,128)(2,1)}, u32[]{:S(2)}) copy-start(bf16[4,448,1152]{2,1,0:T(8,128)(2,1)} %get-tuple-element.92) | copy-start | bytes 12386308
  489.3 22.1 %slice-start = ((s8[8257536]{0:T(1024)(128)(4,1)}), s8[4194304]{0:T(1024)(128)(4,1)S(1)}, s32[]{:S(2)}) async-start(s8[8257536]{0:T(1024)(128)(4,1)} %bitcast.66), calls=%async_computation | async-start | bytes 8388608
  490.6 179.2 %collective-permute-start.1 = (bf16[288,1152]{1,0:T(8,128)(2,1)}, bf16[288,1152]{1,0:T(8,128)(2,1)}, u32[]{:S(2)}, u32[]{:S(2)}) collective-permute-start(bf16[288,1152]{1,0:T(8,128)(2,1)} %get-tuple-element.141), channel_id=1, source_target_pairs={{0,8},{4,12},{8,16},{12,20},{16,24},{20,28},{24,0},{28,4},{1,9},{5... | collective-permute-start | bytes 1990664 | tf_op jit(solution)/shard_map/ppermute | solution.py:1229
  491.7 178.0 %collective-permute-start.2 = (bf16[288,1152]{1,0:T(8,128)(2,1)}, bf16[288,1152]{1,0:T(8,128)(2,1)}, u32[]{:S(2)}, u32[]{:S(2)}) collective-permute-start(bf16[288,1152]{1,0:T(8,128)(2,1)} %get-tuple-element.140), channel_id=1, source_target_pairs={{0,16},{4,20},{8,24},{12,28},{16,0},{20,4},{24,8},{28,12},{1,17},{... | collective-permute-start | bytes 1990664 | tf_op jit(solution)/shard_map/ppermute | solution.py:1229
  494.4 175.4 %collective-permute-start.3 = (bf16[288,1152]{1,0:T(8,128)(2,1)S(1)}, bf16[288,1152]{1,0:T(8,128)(2,1)}, u32[]{:S(2)}, u32[]{:S(2)}) collective-permute-start(bf16[288,1152]{1,0:T(8,128)(2,1)S(1)} %get-tuple-element.139), channel_id=1, source_target_pairs={{0,24},{4,28},{8,0},{12,4},{16,8},{20,12},{24,16},{28,20},{1,25},{... | collective-permute-start | bytes 1990664 | tf_op jit(solution)/shard_map/ppermute | solution.py:1229
  496.1 15.4 %slice-start.1 = ((s8[8257536]{0:T(1024)(128)(4,1)}), s8[4063232]{0:T(1024)(128)(4,1)S(1)}, s32[]{:S(2)}) async-start(s8[8257536]{0:T(1024)(128)(4,1)} %bitcast.66), calls=%async_computation.1 | async-start | bytes 8126464
  496.1 15.4 %copy-start.5 = (bf16[4,448,1152]{2,1,0:T(8,128)(2,1)S(1)}, bf16[4,448,1152]{2,1,0:T(8,128)(2,1)}, u32[]{:S(2)}) copy-start(bf16[4,448,1152]{2,1,0:T(8,128)(2,1)} %get-tuple-element.95) | copy-start | bytes 12386308
  524.4 143.8 %copy-start.4 = (f32[1,2304]{1,0:T(1,128)S(1)}, f32[1,2304]{1,0:T(1,128)}, u32[]{:S(2)}) copy-start(f32[1,2304]{1,0:T(1,128)} %get-tuple-element.110) | copy-start | bytes 27652
  799.1 24.7 %copy-start.1 = (f32[224,2304]{1,0:T(8,128)S(1)}, f32[224,2304]{1,0:T(8,128)}, u32[]{:S(2)}) copy-start(f32[224,2304]{1,0:T(8,128)} %get-tuple-element.166) | copy-start | bytes 6193156
  823.8 2.3 copy-start.2

commit v7 on v6

--- a/solution.py
+++ b/solution.py
@@ -318,12 +318,14 @@
 
 def out_project(mixed, wo, part):
     blocks, rows, _ = part.shape
-    wide = D // 3
     for pair in range(blocks // 2 - 1, -1, -1):
-        for n in range(0, D, wide):
-            got = mm_cols(mixed[pair * 2 * rows : (pair + 1) * 2 * rows], wo[n : n + wide]).astype(BF)
-            part[pair * 2, :, n : n + wide] = got[:rows]
-            part[pair * 2 + 1, :, n : n + wide] = got[rows:]
+
+        def body(at, pair=pair):
+            got = mm_cols(mixed[pair * 2 * rows : (pair + 1) * 2 * rows], wo[at]).astype(BF)
+            part[pair * 2, :, at] = got[:rows]
+            part[pair * 2 + 1, :, at] = got[rows:]
+
+        row_tiles(D, D // 3, body)
 
 
 def chunks(wrows, parts=3):
@@ -926,9 +928,10 @@
 
 
 def weight_grad(tokens, grads, out):
-    wide = D // 3
-    for n in range(0, D, wide):
-        out[n : n + wide] = mm_rows(tokens[:, n : n + wide], grads[...]).astype(BF)
+    def body(at):
+        out[at] = mm_rows(tokens[:, at], grads[...]).astype(BF)
+
+    row_tiles(D, D // 3, body)
 
 
 def close_kernel(
@@ -1022,14 +1025,13 @@
                     )
 
     wa_load.wait()
-    wide = D // 3
-    copies = []
     for pair in (1, 0):
         at = pl.ds(pair * 2 * rows, 2 * rows)
-        for n in range(0, D, wide):
-            tokens[at, n : n + wide] = (
-                mm_cols(dq[at], wa[n : n + wide]) + mm_cols(dkv[at], wkv[n : n + wide])
-            ).astype(BF)
+
+        def body(n, at=at):
+            tokens[at, n] = (mm_cols(dq[at], wa[n]) + mm_cols(dkv[at], wkv[n])).astype(BF)
+
+        row_tiles(D, D // 3, body)
         if pair:
             c1 = net.send(tokens.at[pl.ds(3 * rows, rows)], r1.at[1], net.core_n)
             c0 = net.send(tokens.at[pl.ds(2 * rows, rows)], r1.at[0], net.core_n)

time: 836 us -> 840 us (level)
  no operation moved by 1% of the time
where the time goes in v7:
time: 840 us; the launch traced here: 831 us
  Pallas kernels  731 us (87%)
  matrix products  44.9 us (5%)
  other arithmetic  16.8 us (2%)
  local copies, waits for them, and re-layouts  14.4 us (2%)
  waiting for transfers between devices  12.1 us (1%)
    pallas_call x1, Pallas kernels, open_layer(): call(functools.partial(open_kernel, n_dp, n_mp), [bf(total, cols), bf(tot...  289 us
    pallas_call x1, Pallas kernels, back(): call(functools.partial(back_kernel, n_dp, n_mp), [jax.ShapeDtypeStruct(bl...  145 us
    pallas_call x1, Pallas kernels, close(): call(functools.partial(close_kernel, n_dp, n_mp), [jax.ShapeDtypeStruct((...  126 us
    pallas_call x1, Pallas kernels, turn(): call(functools.partial(turn_kernel, n_dp, n_mp), [jax.ShapeDtypeStruct(bl...  99.8 us
    pallas_call x1, Pallas kernels, mlp_back(): plain(down_back_kernel, (blocks,), [jax.ShapeDtypeStruct(shape, BF), jax....  46.1 us
    dot_general x3, matrix products, mm_rows(): lax.dot_general(left, right, (((0,), (0,)), ((), ())), preferred_element_...  44.9 us
    pallas_call x1, Pallas kernels, adam_all(): plain(adam_kernel, (wrows // step,), [like(a) for a in gains] + [like(a)...  24.7 us
  transfers between devices with their start and end apart: 4, of which 1 were waited for; matrix products, arithmetic and copies ran while one was open for 4% of the time, Pallas kernels for 23%

profile of v7, /device:TPU:0, one launch (start us, length us, event | category | flops | bytes accessed | tf_op | source)
XLA Modules:
  0.0 831.1 jit_solution(5165208155228215728)
XLA Ops:
  0.7 0.8 reduce
  2.2 1.4 fusion.12
  9.6 1.0 copy.39.marks_col
  10.7 1.2 reshape.424.own_gains
  11.9 0.8 fusion.10
  12.7 0.8 copy.40.live
  13.5 1.3 fusion.6
  15.5 2.6 multiply_sine_fusion
  18.1 1.3 fusion.5
  19.4 289.4 %shard_map.280 = (bf16[896,512]{1,0:T(8,128)(2,1)}, bf16[896,256]{1,0:T(8,128)(2,1)}, bf16[896,256]{1,0:T(8,128)(2,1)}, bf16[896,512]{1,0:T(8,128)(2,1)}, f32[22...) custom-call(bf16[288,512]{1,0:T(8,128)(2,1)} %get-tuple-element.143., ...), custom_call_target="tpu_custom_call" | custom-call | tf_op jit(solution)/shard_map/pallas_call | solution.py:528
  308.8 99.8 %shard_map.281 = (f32[224,2304]{1,0:T(8,128)}, f32[1,2304]{1,0:T(1,128)}, f32[8,224,1152]{2,1,0:T(8,128)}, f32[8,224,1152]{2,1,0:T(8,128)}, bf16[8,224,1152]{2,1...) custom-call(bf16[8,224,2304]{2,1,0:T(8,128)(2,1)} %get-tuple-element.75.ffn, bf16[2304,1152]{1,0:T(8,128)(2,1)} %bitcast.70, ...), custom_call_target="tpu_custom_call" | custom-call | tf_op jit(solution)/shard_map/pallas_call | solution.py:719
  408.6 16.5 %fusion = bf16[2304,1152]{1,0:T(8,128)(2,1)} fusion(bf16[8,224,2304]{2,1,0:T(8,128)(2,1)} %get-tuple-element.84, bf16[8,224,1152]{2,1,0:T(8,128)(2,1)} %get-tuple-element.83), kind=kOutput, calls=%fused_computation.2 | convolution fusion | flops 9515335680 | bytes 17694720 | tf_op jit(solution)/shard_map/dot_general | solution.py:73
  425.1 2.0 dynamic-slice_bitcast_fusion
  427.1 2.1 collective-permute-start
  429.1 46.1 %shard_map.282 = (bf16[4,448,1152]{2,1,0:T(8,128)(2,1)}, bf16[4,448,1152]{2,1,0:T(8,128)(2,1)}, bf16[4,448,2304]{2,1,0:T(8,128)(2,1)}) custom-call(bf16[4,448,2304]{2,1,0:T(8,128)(2,1)} %bitcast.86, f32[4,448,1152]{2,1,0:T(8,128)} %bitcast.84, f32[4,448,1152]{2,1,0:T(8,128)} %bitcast.85, bf16[2304,1152]{1,0:T(8,128)(2,1)} %bitcast.71, ...), custom_call_target="tpu_custom_call" | custom-call | flops 28538044416 | bytes 41943040 | tf_op jit(solution)/shard_map/pallas_call | solution.py:1178
  475.3 12.1 %collective-permute-done = bf16[4,288,1152]{2,1,0:T(8,128)(2,1)} collective-permute-done((bf16[4,288,1152]{2,1,0:T(8,128)(2,1)S(1)}, bf16[4,288,1152]{2,1,0:T(8,128)(2,1)}, u32[]{:S(2)}, u32[]{:S(2)}) %collective-permute-start) | collective-permute-done | bytes 2654240 | tf_op jit(solution)/shard_map/ppermute | solution.py:1227
  487.4 3.4 fusion.1
  490.8 1.2 dynamic-slice_bitcast_fusion.1
  492.7 2.7 collective-permute-start.2
  495.4 1.5 collective-permute-start.3
  496.9 15.4 %convolution_convert_fusion.1 = bf16[2304,1152]{1,0:T(8,128)(2,1)} fusion(bf16[1792,2304]{1,0:T(8,128)(2,1)} %bitcast.65, bf16[1792,1152]{1,0:T(8,128)(2,1)S(1)} %bitcast.88), kind=kOutput, calls=%fused_computation.4 | convolution fusion | flops 9515335680 | bytes 17694720 | tf_op jit(solution)/shard_map/dot_general | solution.py:73
  512.3 13.0 %convolution_convert_fusion = bf16[2304,1152]{1,0:T(8,128)(2,1)} fusion(bf16[1792,2304]{1,0:T(8,128)(2,1)S(1)} %bitcast.68, bf16[1792,1152]{1,0:T(8,128)(2,1)S(1)} %bitcast.87), kind=kOutput, calls=%fused_computation.3 | convolution fusion | flops 9515335680 | bytes 17694720 | tf_op jit(solution)/shard_map/dot_general | solution.py:73
  525.3 144.5 %shard_map.283 = (f32[224,2304]{1,0:T(8,128)}, f32[1,2304]{1,0:T(1,128)}, f32[1,2304]{1,0:T(1,128)}, bf16[4,224,2304]{2,1,0:T(8,128)(2,1)}, f32[288,2304]{1,0:T(...) custom-call(bf16[8,224,2304]{2,1,0:T(8,128)(2,1)} %bitcast.69, f32[224,2304]{1,0:T(8,128)} %get-tuple-element.79.hid, ...), custom_call_target="tpu_custom_call" | custom-call | tf_op jit(solution)/shard_map/pallas_call | solution.py:884
  669.8 0.7 pad_maximum_fusion.2
  671.3 1.8 fusion.3
  673.1 1.8 pad_maximum_fusion.sum_down.g_down
  674.9 126.1 %shard_map.284 = (f32[224,2304]{1,0:T(8,128)}, f32[288,512]{1,0:T(8,128)}, f32[288,512]{1,0:T(8,128)}, f32[288,512]{1,0:T(8,128)}, f32[1,288]{1,0:T(1,128)}, /*index=5*/f32[8,128]{1,0:T(8,128)}) custom-call(bf16[896,2304]{1,0:T(8,128)(2,1)} %bitcast.80, bf16[896,2304]{1,0:T(8,128)(2,1)} %get-tuple-element.99.seq_normed, ...), custom_call_target="tpu_custom_call" | custom-call | tf_op jit(solution)/shard_map/pallas_call | solution.py:1111
  801.1 1.2 slice.36
  802.2 24.7 %shard_map.285 = (f32[288]{0:T(512)}, f32[288]{0:T(512)}, f32[288]{0:T(512)}, f32[3,288,2304]{2,1,0:T(8,128)}, f32[3,288,2304]{2,1,0:T(8,128)}, /*index=5*/f32[3...) custom-call(f32[8,128]{1,0:T(8,128)} %get-tuple-element.116.norm, ...), custom_call_target="tpu_custom_call" | custom-call | flops 100 | bytes 41943040 | tf_op jit(solution)/shard_map/pallas_call | solution.py:1215
  827.0 1.3 copy.48
  828.3 1.0 copy-done.2
  829.3 1.3 copy.49
  (44 shorter events, 5.2 us)
Async XLA Ops:
  0.6 17.5 %copy-start = (f32[2,288,512]{2,1,0:T(8,128)S(1)}, f32[2,288,512]{2,1,0:T(8,128)}, u32[]{:S(2)}) copy-start(f32[2,288,512]{2,1,0:T(8,128)} %refs_3_.1) | copy-start | bytes 3538948
  9.6 9.7 %copy-start.3 = (s32[8,896]{1,0:T(8,128)}, s32[8,896]{1,0:T(8,128)S(1)}, u32[]{:S(2)}) copy-start(s32[8,896]{1,0:T(8,128)S(1)} %stack.49.marks_row) | copy-start | bytes 86020
  427.1 60.3 %collective-permute-start = (bf16[4,288,1152]{2,1,0:T(8,128)(2,1)S(1)}, bf16[4,288,1152]{2,1,0:T(8,128)(2,1)}, u32[]{:S(2)}, u32[]{:S(2)}) collective-permute-start(bf16[4,288,1152]{2,1,0:T(8,128)(2,1)S(1)} %dynamic-slice_bitcast_fusion), channel_id=1, source_target_pairs={{0,4},{4,0},{8,12},{12,8},{16,20},{20,16},{24,28},{28,24},{1,5},{5... | collective-permute-start | bytes 7962632 | tf_op jit(solution)/shard_map/ppermute | solution.py:1227
  487.4 9.5 %copy-start.6 = (bf16[4,448,1152]{2,1,0:T(8,128)(2,1)S(1)}, bf16[4,448,1152]{2,1,0:T(8,128)(2,1)}, u32[]{:S(2)}) copy-start(bf16[4,448,1152]{2,1,0:T(8,128)(2,1)} %get-tuple-element.92) | copy-start | bytes 12386308
  490.7 21.6 %slice-start = ((s8[8257536]{0:T(1024)(128)(4,1)}), s8[4194304]{0:T(1024)(128)(4,1)S(1)}, s32[]{:S(2)}) async-start(s8[8257536]{0:T(1024)(128)(4,1)} %bitcast.66), calls=%async_computation | async-start | bytes 8388608
  492.0 179.3 %collective-permute-start.1 = (bf16[288,1152]{1,0:T(8,128)(2,1)}, bf16[288,1152]{1,0:T(8,128)(2,1)}, u32[]{:S(2)}, u32[]{:S(2)}) collective-permute-start(bf16[288,1152]{1,0:T(8,128)(2,1)} %get-tuple-element.141), channel_id=1, source_target_pairs={{0,8},{4,12},{8,16},{12,20},{16,24},{20,28},{24,0},{28,4},{1,9},{5... | collective-permute-start | bytes 1990664 | tf_op jit(solution)/shard_map/ppermute | solution.py:1231
  492.7 178.6 %collective-permute-start.2 = (bf16[288,1152]{1,0:T(8,128)(2,1)}, bf16[288,1152]{1,0:T(8,128)(2,1)}, u32[]{:S(2)}, u32[]{:S(2)}) collective-permute-start(bf16[288,1152]{1,0:T(8,128)(2,1)} %get-tuple-element.140), channel_id=1, source_target_pairs={{0,16},{4,20},{8,24},{12,28},{16,0},{20,4},{24,8},{28,12},{1,17},{... | collective-permute-start | bytes 1990664 | tf_op jit(solution)/shard_map/ppermute | solution.py:1231
  495.4 175.9 %collective-permute-start.3 = (bf16[288,1152]{1,0:T(8,128)(2,1)S(1)}, bf16[288,1152]{1,0:T(8,128)(2,1)}, u32[]{:S(2)}, u32[]{:S(2)}) collective-permute-start(bf16[288,1152]{1,0:T(8,128)(2,1)S(1)} %get-tuple-element.139), channel_id=1, source_target_pairs={{0,24},{4,28},{8,0},{12,4},{16,8},{20,12},{24,16},{28,20},{1,25},{... | collective-permute-start | bytes 1990664 | tf_op jit(solution)/shard_map/ppermute | solution.py:1231
  496.9 15.4 %slice-start.1 = ((s8[8257536]{0:T(1024)(128)(4,1)}), s8[4063232]{0:T(1024)(128)(4,1)S(1)}, s32[]{:S(2)}) async-start(s8[8257536]{0:T(1024)(128)(4,1)} %bitcast.66), calls=%async_computation.1 | async-start | bytes 8126464
  496.9 15.4 %copy-start.5 = (bf16[4,448,1152]{2,1,0:T(8,128)(2,1)S(1)}, bf16[4,448,1152]{2,1,0:T(8,128)(2,1)}, u32[]{:S(2)}) copy-start(bf16[4,448,1152]{2,1,0:T(8,128)(2,1)} %get-tuple-element.95) | copy-start | bytes 12386308
  525.3 144.5 %copy-start.4 = (f32[1,2304]{1,0:T(1,128)S(1)}, f32[1,2304]{1,0:T(1,128)}, u32[]{:S(2)}) copy-start(f32[1,2304]{1,0:T(1,128)} %get-tuple-element.110) | copy-start | bytes 27652
  802.2 24.7 %copy-start.1 = (f32[224,2304]{1,0:T(8,128)S(1)}, f32[224,2304]{1,0:T(8,128)}, u32[]{:S(2)}) copy-start(f32[224,2304]{1,0:T(8,128)} %get-tuple-element.166) | copy-start | bytes 6193156
  827.0 2.3 copy-start.2
